TPU v7x, 32 devices: a whole 2x2x4 slice. The times are simulated.
32 devices in a mesh: narrow: 2 (over x), wide: 16 (over z, y, core).
Axes of the slice: x: 2, y: 2, z: 4, core: 2. Of those that a mesh axis runs over, the one named last changes fastest.
Arguments:
- inputs: bfloat16 [24576, 768], P('wide', 'narrow'), may hold values from -6 to 6
- block_segment: int32 [48], P('wide'), may hold values from 0 to 2, as said below
- query_weight: bfloat16 [768, 768], P('wide', 'narrow'), may hold values from -0.21875 to 0.21875
- key_weight: bfloat16 [768, 768], P('wide', 'narrow'), may hold values from -0.21875 to 0.21875
- value_weight: bfloat16 [768, 768], P('wide', 'narrow'), may hold values from -0.21875 to 0.21875
- output_weight: bfloat16 [768, 768], P('narrow', 'wide'), may hold values from -1.25 to 1.25
- inner_weight: bfloat16 [768, 3072], P('wide', 'narrow'), may hold values from -0.21875 to 0.21875
- outer_weight: bfloat16 [3072, 768], P('narrow', 'wide'), may hold values from -0.109375 to 0.109375
- first_gain: float32 [768], P('narrow'), may hold values from 0.5 to 1.5
- first_bias: float32 [768], P('narrow'), may hold values from -3 to 3
- second_gain: float32 [768], P('narrow'), may hold values from 0.5 to 1.5
- second_bias: float32 [768], P('narrow'), may hold values from -3 to 3
- output_cotangent: bfloat16 [24576, 768], P('wide', 'narrow'), may hold values from -6 to 6
Outputs:
- layer_output: bfloat16 [24576, 768], P('wide', 'narrow')
- input_gradient: bfloat16 [24576, 768], P('wide', 'narrow')
- query_gradient: float32 [768, 768], P('wide', 'narrow')
- key_gradient: float32 [768, 768], P('wide', 'narrow')
- value_gradient: float32 [768, 768], P('wide', 'narrow')
- output_gradient: float32 [768, 768], P('narrow', 'wide')
- inner_gradient: float32 [768, 3072], P('wide', 'narrow')
- outer_gradient: float32 [3072, 768], P('narrow', 'wide')
- first_gain_gradient: float32 [768], P(('narrow', 'wide'))
- first_bias_gradient: float32 [768], P(('narrow', 'wide'))
- second_gain_gradient: float32 [768], P(('narrow', 'wide'))
- second_bias_gradient: float32 [768], P(('narrow', 'wide'))
Inputs may be any that keep to these rules, and one draw needn't show every extreme that they name: `block_segment`: entry b belongs to block b; every 3 consecutive entries form a group that lies on one index of wide; within a group the entries start at 0 and rise by 0 or 1 from block to block, so sequences hold 1 to 3 whole blocks.
All inputs are finite; a program needn't handle non-finite values.
Results may differ from a plain program's by a relative error of at most 0.017.
Values may be sent and summed in bfloat16 or wider, within the bound.
A program may use at most 256 MiB of HBM per device.

v0:
```python
import jax
import jax.numpy as jnp
from jax import lax
from jax.sharding import PartitionSpec as P

HEAD_DIM = 64
BLOCK = 512
SPAN = 3


EPSILON = 1e-06
NEGATIVE = -1e30
THETA = 10000.0
ROOT_HALF = 0.7071067811865476
INVERSE_ROOT = 0.3989422804014327


def product(left, right):
    return jnp.dot(left, right, preferred_element_type=jnp.float32)


def left_transposed(left, right):
    return lax.dot_general(
        left, right, (((0,), (0,)), ((), ())), preferred_element_type=jnp.float32
    )


def right_transposed(left, right):
    return lax.dot_general(
        left, right, (((1,), (1,)), ((), ())), preferred_element_type=jnp.float32
    )


def whole_features(values):
    return lax.all_gather(values, "narrow", axis=1, tiled=True)


def feature_sums(values):
    return lax.psum_scatter(
        values.astype(jnp.bfloat16), "narrow", scatter_dimension=1, tiled=True
    ).astype(jnp.float32)


def moments(first_sum, second_sum):
    return lax.psum((first_sum, second_sum), "narrow")


def gelu_value(values):
    return 0.5 * values * (1.0 + lax.erf(values * ROOT_HALF))


def gelu_slope(values):
    return (
        0.5 * (1.0 + lax.erf(values * ROOT_HALF))
        + values * jnp.exp(-0.5 * values * values) * INVERSE_ROOT
    )


def rotate(values, cosine, sine):
    half = values.shape[-1] // 2
    first = values[..., :half]
    second = values[..., half:]
    return jnp.concatenate(
        [first * cosine - second * sine, second * cosine + first * sine], axis=-1
    )


def rotate_back(values, cosine, sine):
    half = values.shape[-1] // 2
    first = values[..., :half]
    second = values[..., half:]
    return jnp.concatenate(
        [first * cosine + second * sine, second * cosine - first * sine], axis=-1
    )


def tables(block_segment):
    segment = block_segment.reshape(-1, SPAN)
    earlier = jnp.sum((segment[:, None, :] < segment[:, :, None]).astype(jnp.int32), axis=2)
    offsets = (jnp.arange(SPAN, dtype=jnp.int32)[None, :] - earlier) * BLOCK
    positions = (
        (offsets[:, :, None] + jnp.arange(BLOCK, dtype=jnp.int32)[None, None, :])
        .reshape(-1)
        .astype(jnp.float32)
    )
    half = HEAD_DIM // 2
    rates = THETA ** (-jnp.arange(half, dtype=jnp.float32) / half)
    angle = positions[:, None] * rates[None, :]
    labels = jnp.repeat(segment, BLOCK, axis=1)
    return (jnp.cos(angle)[:, None, :], jnp.sin(angle)[:, None, :], labels)


def normalize(summed, gain, bias, width):
    total, squares = moments(jnp.sum(summed, axis=1), jnp.sum(summed * summed, axis=1))
    mean = total / width
    reciprocal = lax.rsqrt(squares / width - mean * mean + EPSILON)
    normed = (summed - mean[:, None]) * reciprocal[:, None]
    return (normed * gain + bias, normed, reciprocal)


def normalize_back(grad, normed, reciprocal, gain, width):
    scaled = grad * gain
    total, cross = moments(jnp.sum(scaled, axis=1), jnp.sum(scaled * normed, axis=1))
    return reciprocal[:, None] * (scaled - total[:, None] / width - normed * cross[:, None] / width)


def block_scores(block_queries, group_keys, block_labels, group_labels, factor):
    scores = (
        jnp.einsum("qhd,khd->hqk", block_queries, group_keys, preferred_element_type=jnp.float32)
        * factor
    )
    same = block_labels[:, None] == group_labels[None, :]
    return jnp.where(same[None], scores, NEGATIVE)


def attention_forward(queries, keys, values, labels, factor):
    groups, length = labels.shape
    shape = (groups, length) + queries.shape[1:]

    def one_group(items):
        group_queries, group_keys, group_values, group_labels = items
        contexts = []
        totals = []
        for index in range(length // BLOCK):
            low_end = index * BLOCK
            high_end = low_end + BLOCK
            scores = block_scores(
                group_queries[low_end:high_end],
                group_keys,
                group_labels[low_end:high_end],
                group_labels,
                factor,
            )
            top = jnp.max(scores, axis=2, keepdims=True)
            raised = jnp.exp(scores - top)
            summed = jnp.sum(raised, axis=2, keepdims=True)
            soft = (raised / summed).astype(jnp.bfloat16)
            contexts.append(
                jnp.einsum("hqk,khd->qhd", soft, group_values, preferred_element_type=jnp.float32)
            )
            totals.append((top + jnp.log(summed))[..., 0])
        return (jnp.concatenate(contexts, axis=0), jnp.concatenate(totals, axis=1))

    contexts, totals = lax.map(
        one_group, (queries.reshape(shape), keys.reshape(shape), values.reshape(shape), labels)
    )
    return (contexts.reshape(queries.shape), totals)


def attention_backward(queries, keys, values, totals, grad_context, labels, factor):
    groups, length = labels.shape
    shape = (groups, length) + queries.shape[1:]

    def one_group(items):
        group_queries, group_keys, group_values, group_totals, group_grads, group_labels = items
        keys_grad = jnp.zeros(group_keys.shape, jnp.float32)
        values_grad = jnp.zeros(group_values.shape, jnp.float32)
        pieces = []
        for index in range(length // BLOCK):
            low_end = index * BLOCK
            high_end = low_end + BLOCK
            block_queries = group_queries[low_end:high_end]
            block_grads = group_grads[low_end:high_end]
            scores = block_scores(
                block_queries, group_keys, group_labels[low_end:high_end], group_labels, factor
            )
            soft = jnp.exp(scores - group_totals[:, low_end:high_end, None])
            inner = jnp.einsum(
                "qhd,khd->hqk", block_grads, group_values, preferred_element_type=jnp.float32
            )
            centre = jnp.sum(soft * inner, axis=2, keepdims=True)
            scores_grad = (soft * (inner - centre)).astype(jnp.bfloat16)
            pieces.append(
                jnp.einsum(
                    "hqk,khd->qhd", scores_grad, group_keys, preferred_element_type=jnp.float32
                )
                * factor
            )
            keys_grad = (
                keys_grad
                + jnp.einsum(
                    "hqk,qhd->khd", scores_grad, block_queries, preferred_element_type=jnp.float32
                )
                * factor
            )
            values_grad = values_grad + jnp.einsum(
                "hqk,qhd->khd",
                soft.astype(jnp.bfloat16),
                block_grads,
                preferred_element_type=jnp.float32,
            )
        return (jnp.concatenate(pieces, axis=0), keys_grad, values_grad)

    queries_grad, keys_grad, values_grad = lax.map(
        one_group,
        (
            queries.reshape(shape),
            keys.reshape(shape),
            values.reshape(shape),
            totals,
            grad_context.reshape(shape),
            labels,
        ),
    )
    return (
        queries_grad.reshape(queries.shape),
        keys_grad.reshape(queries.shape),
        values_grad.reshape(queries.shape),
    )


def shards(
    inputs,
    block_segment,
    query_weight,
    key_weight,
    value_weight,
    output_weight,
    inner_weight,
    outer_weight,
    first_gain,
    first_bias,
    second_gain,
    second_bias,
    output_cotangent,
):
    width = first_gain.shape[0] * lax.axis_size("narrow")
    tokens = inputs.shape[0]
    factor = HEAD_DIM ** (-0.5)
    cosine, sine, labels = tables(block_segment)
    full_inputs = whole_features(inputs)
    query_full, key_full, value_full, inner_full = (
        lax.all_gather(query_weight, "wide", axis=0, tiled=True),
        lax.all_gather(key_weight, "wide", axis=0, tiled=True),
        lax.all_gather(value_weight, "wide", axis=0, tiled=True),
        lax.all_gather(inner_weight, "wide", axis=0, tiled=True),
    )
    output_full, outer_full = (
        lax.all_gather(output_weight, "wide", axis=1, tiled=True),
        lax.all_gather(outer_weight, "wide", axis=1, tiled=True),
    )
    head_shape = (tokens, query_weight.shape[1] // HEAD_DIM, HEAD_DIM)
    queries = rotate(product(full_inputs, query_full).reshape(head_shape), cosine, sine).astype(
        jnp.bfloat16
    )
    keys = rotate(product(full_inputs, key_full).reshape(head_shape), cosine, sine).astype(
        jnp.bfloat16
    )
    values = product(full_inputs, value_full).astype(jnp.bfloat16).reshape(head_shape)
    context, totals = attention_forward(queries, keys, values, labels, factor)
    context_low = context.reshape(tokens, -1).astype(jnp.bfloat16)
    attended = feature_sums(product(context_low, output_full))
    first, first_normed, first_scale = normalize(
        inputs.astype(jnp.float32) + attended, first_gain, first_bias, width
    )
    first_low = first.astype(jnp.bfloat16)
    feed_rows = whole_features(first_low)
    inner = product(feed_rows, inner_full)
    activated = gelu_value(inner).astype(jnp.bfloat16)
    mixed = feature_sums(product(activated, outer_full))
    second, second_normed, second_scale = normalize(first + mixed, second_gain, second_bias, width)
    layer_output = second.astype(jnp.bfloat16)
    cotangent = output_cotangent.astype(jnp.float32)
    second_gain_grad = jnp.sum(cotangent * second_normed, axis=0)
    second_bias_grad = jnp.sum(cotangent, axis=0)
    grad_second = normalize_back(cotangent, second_normed, second_scale, second_gain, width)
    grad_mixed = grad_second.astype(jnp.bfloat16)
    grad_rows = whole_features(grad_mixed)
    grad_activated = right_transposed(grad_rows, outer_full)
    outer_grad = left_transposed(activated, grad_rows)
    grad_inner = (grad_activated * gelu_slope(inner)).astype(jnp.bfloat16)
    inner_grad = left_transposed(feed_rows, grad_inner)
    grad_first = grad_second + feature_sums(right_transposed(grad_inner, inner_full))
    first_gain_grad = jnp.sum(grad_first * first_normed, axis=0)
    first_bias_grad = jnp.sum(grad_first, axis=0)
    grad_first_sum = normalize_back(grad_first, first_normed, first_scale, first_gain, width)
    attended_rows = whole_features(grad_first_sum.astype(jnp.bfloat16))
    output_grad = left_transposed(context_low, attended_rows)
    grad_context = right_transposed(attended_rows, output_full).astype(jnp.bfloat16)
    queries_grad, keys_grad, values_grad = attention_backward(
        queries, keys, values, totals, grad_context.reshape(head_shape), labels, factor
    )
    queries_grad = rotate_back(queries_grad, cosine, sine).reshape(tokens, -1).astype(jnp.bfloat16)
    keys_grad = rotate_back(keys_grad, cosine, sine).reshape(tokens, -1).astype(jnp.bfloat16)
    values_grad = values_grad.reshape(tokens, -1).astype(jnp.bfloat16)
    query_grad = left_transposed(full_inputs, queries_grad)
    key_grad = left_transposed(full_inputs, keys_grad)
    value_grad = left_transposed(full_inputs, values_grad)
    spread = (
        right_transposed(queries_grad, query_full)
        + right_transposed(keys_grad, key_full)
        + right_transposed(values_grad, value_full)
    )
    input_gradient = (grad_first_sum + feature_sums(spread)).astype(jnp.bfloat16)
    (
        query_total,
        key_total,
        value_total,
        inner_total,
        first_gain_total,
        first_bias_total,
        second_gain_total,
        second_bias_total,
    ) = (
        lax.psum_scatter(query_grad, "wide", scatter_dimension=0, tiled=True),
        lax.psum_scatter(key_grad, "wide", scatter_dimension=0, tiled=True),
        lax.psum_scatter(value_grad, "wide", scatter_dimension=0, tiled=True),
        lax.psum_scatter(inner_grad, "wide", scatter_dimension=0, tiled=True),
        lax.psum_scatter(first_gain_grad, "wide", scatter_dimension=0, tiled=True),
        lax.psum_scatter(first_bias_grad, "wide", scatter_dimension=0, tiled=True),
        lax.psum_scatter(second_gain_grad, "wide", scatter_dimension=0, tiled=True),
        lax.psum_scatter(second_bias_grad, "wide", scatter_dimension=0, tiled=True),
    )
    output_total, outer_total = (
        lax.psum_scatter(output_grad, "wide", scatter_dimension=1, tiled=True),
        lax.psum_scatter(outer_grad, "wide", scatter_dimension=1, tiled=True),
    )
    return (
        layer_output,
        input_gradient,
        query_total,
        key_total,
        value_total,
        output_total,
        inner_total,
        outer_total,
        first_gain_total,
        first_bias_total,
        second_gain_total,
        second_bias_total,
    )


def solution(mesh):
    placed = (
        P("wide", "narrow"),
        P("wide"),
        P("wide", "narrow"),
        P("wide", "narrow"),
        P("wide", "narrow"),
        P("narrow", "wide"),
        P("wide", "narrow"),
        P("narrow", "wide"),
        P("narrow"),
        P("narrow"),
        P("narrow"),
        P("narrow"),
        P("wide", "narrow"),
    )
    return jax.shard_map(
        shards,
        mesh=mesh,
        in_specs=placed,
        out_specs=(
            P("wide", "narrow"),
            P("wide", "narrow"),
            P("wide", "narrow"),
            P("wide", "narrow"),
            P("wide", "narrow"),
            P("narrow", "wide"),
            P("wide", "narrow"),
            P("narrow", "wide"),
            P(("narrow", "wide")),
            P(("narrow", "wide")),
            P(("narrow", "wide")),
            P(("narrow", "wide")),
        ),
        check_vma=False,
    )
```

profile of v0, /device:TPU:1, one launch (start us, length us, event | category | flops | bytes accessed | tf_op | source)
XLA Modules:
  0.0 1154.8 jit_solution(4590739033261593181)
XLA Ops:
  14.7 25.0 %all_gather.32 = bf16[768,384]{1,0:T(8,128)(2,1)S(1)} all-gather(bf16[48,384]{1,0:T(8,128)(2,1)} %param.15), channel_id=1, replica_groups=mesh['narrow'=2,'wide'=16] {'wide'}, dimensions={0}, use_global_device_ids=true | all-gather | bytes 626688 | tf_op jit(solution)/shard_map/all_gather | solution.py:233
  39.7 19.3 %all_gather.33 = bf16[768,384]{1,0:T(8,128)(2,1)S(1)} all-gather(bf16[48,384]{1,0:T(8,128)(2,1)} %param.16), channel_id=1, replica_groups=mesh['narrow'=2,'wide'=16] {'wide'}, dimensions={0}, use_global_device_ids=true | all-gather | bytes 626688 | tf_op jit(solution)/shard_map/all_gather | solution.py:234
  59.0 21.8 %all_gather.31 = bf16[768,384]{1,0:T(8,128)(2,1)} all-gather(bf16[48,384]{1,0:T(8,128)(2,1)S(1)} %copy-done.42), channel_id=1, replica_groups=mesh['narrow'=2,'wide'=16] {'wide'}, dimensions={0}, use_global_device_ids=true | all-gather | bytes 626688 | tf_op jit(solution)/shard_map/all_gather | solution.py:235
  80.8 20.4 %all_gather.34 = bf16[384,768]{0,1:T(8,128)(2,1)} all-gather(bf16[384,48]{0,1:T(8,128)(2,1)S(1)} %copy-done.43), channel_id=1, replica_groups=mesh['narrow'=2,'wide'=16] {'wide'}, dimensions={1}, use_global_device_ids=true | all-gather | bytes 626688 | tf_op jit(solution)/shard_map/all_gather | solution.py:239
  106.9 8.3 fusion.68
  115.2 8.0 fusion.67
  123.2 9.6 fusion.1
  135.7 9.3 fusion.50
  145.1 9.6 fusion.2
  154.7 9.4 fusion.51
  164.1 7.9 fusion.69
  172.0 9.0 fusion
  181.1 8.3 fusion.49
  195.2 32.3 %reduce-scatter.31.cloned.1.call-done = bf16[384,1536]{1,0:T(8,128)(2,1)} async-done(((bf16[768,1536]{1,0:T(8,128)(2,1)}), bf16[384,1536]{1,0:T(8,128)(2,1)}) %reduce-scatter.31.cloned.1.call-update) | async-done | bytes 1179664
  229.7 6.3 all-reduce.8
  239.8 37.6 %all-gather.9.cloned.1.call-done = bf16[1536,768]{1,0:T(8,128)(2,1)} async-done(((bf16[1536,384]{1,0:T(8,128)(2,1)}), bf16[1536,768]{1,0:T(8,128)(2,1)}) %all-gather.9.cloned.1.call-update) | async-done | bytes 2359312 | tf_op jit(solution)/shard_map/all_gather | solution.py:35
  277.4 9.8 multiply_convert_fusion.3
  287.2 35.9 %all-gather.13.cloned.1.call-done = bf16[1536,768]{0,1:T(8,128)(2,1)} async-done(((bf16[1536,48]{0,1:T(8,128)(2,1)}), bf16[1536,768]{0,1:T(8,128)(2,1)}) %all-gather.13.cloned.1.call-update) | async-done | bytes 2359312 | tf_op jit(solution)/shard_map/all_gather | solution.py:240
  323.1 8.4 convolution_convert_fusion.1
  335.9 32.9 %reduce-scatter.33.cloned.1.call-done = bf16[384,1536]{1,0:T(8,128)(2,1)} async-done(((bf16[768,1536]{1,0:T(8,128)(2,1)}), bf16[384,1536]{1,0:T(8,128)(2,1)}) %reduce-scatter.33.cloned.1.call-update) | async-done | bytes 1179664
  375.1 6.5 all-reduce.7
  386.5 7.2 all-reduce.6
  398.9 39.9 %all-gather.15.cloned.1.call-done = bf16[1536,768]{1,0:T(8,128)(2,1)} async-done(((bf16[1536,384]{1,0:T(8,128)(2,1)}), bf16[1536,768]{1,0:T(8,128)(2,1)}) %all-gather.15.cloned.1.call-update) | async-done | bytes 2359312 | tf_op jit(solution)/shard_map/all_gather | solution.py:35
  438.8 9.9 fusion.22
  460.3 34.9 %reduce-scatter.35.cloned.1.call-done = bf16[384,1536]{1,0:T(8,128)(2,1)} async-done(((bf16[768,1536]{1,0:T(8,128)(2,1)}), bf16[384,1536]{1,0:T(8,128)(2,1)}) %reduce-scatter.35.cloned.1.call-update) | async-done | bytes 1179664
  501.5 6.6 all-reduce.5
  515.3 36.4 %all-gather.17.cloned.1.call-done = bf16[1536,768]{1,0:T(8,128)(2,1)} async-done(((bf16[1536,384]{1,0:T(8,128)(2,1)}), bf16[1536,768]{1,0:T(8,128)(2,1)}) %all-gather.17.cloned.1.call-update) | async-done | bytes 2359312 | tf_op jit(solution)/shard_map/all_gather | solution.py:35
  556.2 12.1 %multiply_reduce_fusion.2 = (f32[6,512]{1,0:T(8,128)S(1)}, f32[6,512,1536]{2,1,0:T(8,128)}) fusion(f32[6,512,1536]{2,1,0:T(8,128)} %get-tuple-element.161, f32[6,512]{1,0:T(8,128)S(1)} %log_add_fusion.2, bf16[512,6,64]{0,2,1:T(8,128)(2,1)S(1)} %bitcast.125, bf16[1536,6,64]{0,2,1:T(8,128)(2,1)S(1)} %bitcast.110), kind=kOutput, calls=%fused_computation.7 | convolution fusion | flops 618132480 | bytes 39346176 | tf_op jit(solution)/shard_map/while/body/eval_jaxpr/qhd,khd->hqk/dot_general | solution.py:168
  568.4 18.0 %multiply_convert_fusion.2 = bf16[6,512,1536]{2,1,0:T(8,128)(2,1)} fusion(f32[6,512,1536]{2,1,0:T(8,128)} %get-tuple-element.165, f32[6,512,1536]{2,1,0:T(8,128)} %get-tuple-element.161, f32[6,512]{1,0:T(8,128)S(1)} %get-tuple-element.164, f32[6,512]{1,0:T(8,128)S(1)} %log_add_fusion.2), kind=kLoop, calls=%fused_computation.6 | loop fusion | flops 18874368 | bytes 47210496 | tf_op jit(solution)/shard_map/while/body/eval_jaxpr/convert_element_type | solution.py:172
  586.4 8.6 fusion.45
  595.0 7.0 fusion.55
  606.4 13.0 %multiply_reduce_fusion.1 = (f32[6,512]{1,0:T(8,128)S(1)}, f32[6,512,1536]{2,1,0:T(8,128)}) fusion(f32[6,512,1536]{2,1,0:T(8,128)} %get-tuple-element.159, f32[6,512]{1,0:T(8,128)S(1)} %log_add_fusion.1, bf16[512,6,64]{0,2,1:T(8,128)(2,1)} %bitcast.127, bf16[1536,6,64]{0,2,1:T(8,128)(2,1)S(1)} %bitcast.111), kind=kOutput, calls=%fused_computation.4 | convolution fusion | flops 618132480 | bytes 39346176 | tf_op jit(solution)/shard_map/while/body/eval_jaxpr/qhd,khd->hqk/dot_general | solution.py:168
  619.5 8.1 fusion.28
  627.6 12.5 %multiply_reduce_fusion = (f32[6,512]{1,0:T(8,128)S(1)}, f32[6,512,1536]{2,1,0:T(8,128)}) fusion(f32[6,512,1536]{2,1,0:T(8,128)} %get-tuple-element.157, f32[6,512]{1,0:T(8,128)S(1)} %log_add_fusion, bf16[512,6,64]{0,2,1:T(8,128)(2,1)S(1)} %bitcast.123, bf16[1536,6,64]{0,2,1:T(8,128)(2,1)S(1)} %bitcast.112), kind=kOutput, calls=%fused_computation.1 | convolution fusion | flops 618132480 | bytes 39346176 | tf_op jit(solution)/shard_map/while/body/eval_jaxpr/qhd,khd->hqk/dot_general | solution.py:168
  640.1 9.4 fusion.34
  649.5 17.9 %multiply_convert_fusion = bf16[6,512,1536]{2,1,0:T(8,128)(2,1)} fusion(f32[6,512,1536]{2,1,0:T(8,128)} %get-tuple-element.169, f32[6,512,1536]{2,1,0:T(8,128)} %get-tuple-element.157, f32[6,512]{1,0:T(8,128)S(1)} %get-tuple-element.168, f32[6,512]{1,0:T(8,128)S(1)} %log_add_fusion), kind=kLoop, calls=%fused_computation | loop fusion | flops 18874368 | bytes 47210496 | tf_op jit(solution)/shard_map/while/body/eval_jaxpr/convert_element_type | solution.py:172
  667.5 6.6 fusion.43
  674.1 13.0 %multiply_convert_fusion.1 = bf16[6,512,1536]{2,1,0:T(8,128)(2,1)} fusion(f32[6,512,1536]{2,1,0:T(8,128)} %get-tuple-element.167, f32[6,512,1536]{2,1,0:T(8,128)S(1)} %bitcast.104, f32[6,512]{1,0:T(8,128)S(1)} %get-tuple-element.166, f32[6,512]{1,0:T(8,128)S(1)} %log_add_fusion.1), kind=kLoop, calls=%fused_computation.3 | loop fusion | flops 18874368 | bytes 47210496 | tf_op jit(solution)/shard_map/while/body/eval_jaxpr/convert_element_type | solution.py:172
  687.2 6.8 fusion.44
  712.8 7.8 fusion.75
  722.3 8.1 fusion.76
  750.0 30.1 %all-reduce.4 = (f32[384]{0:T(512)S(1)}, f32[384]{0:T(512)S(1)}, f32[384]{0:T(512)S(1)}, f32[384]{0:T(512)S(1)}) all-reduce(f32[384]{0:T(512)S(1)} %copy-done.46, f32[384]{0:T(512)S(1)} %copy-done.47, f32[384]{0:T(512)S(1)} %copy-done.44, f32[384]{0:T(512)S(1)} %copy-done.45), channel_id=12, replica_groups=mesh['narrow'=2,'wide'=16] {'wide'}, use_global_device_ids=true, to_apply=%region_37.38.clone | all-reduce | flops 1536 | bytes 12288
  785.3 39.0 %reduce-scatter.27.cloned.1.call-done = f32[48,1536]{1,0:T(8,128)} async-done(((f32[768,1536]{1,0:T(8,128)}), f32[48,1536]{1,0:T(8,128)}) %reduce-scatter.27.cloned.1.call-update) | async-done | bytes 294928 | tf_op jit(solution)/shard_map/reduce_scatter | solution.py:308
  824.3 78.9 %reduce-scatter.29.cloned.1.call-done = f32[1536,48]{0,1:T(8,128)} async-done(((f32[1536,768]{0,1:T(8,128)}), f32[1536,48]{0,1:T(8,128)}) %reduce-scatter.29.cloned.1.call-update) | async-done | bytes 294928 | tf_op jit(solution)/shard_map/reduce_scatter | solution.py:316
  903.2 60.8 %reduce-scatter.25.cloned.1.call-done = f32[384,48]{0,1:T(8,128)} async-done(((f32[384,768]{0,1:T(8,128)}), f32[384,48]{0,1:T(8,128)}) %reduce-scatter.25.cloned.1.call-update) | async-done | bytes 73744 | tf_op jit(solution)/shard_map/reduce_scatter | solution.py:315
  964.1 61.2 %reduce-scatter.43.cloned.1.call-done = f32[48,384]{1,0:T(8,128)} async-done(((f32[768,384]{1,0:T(8,128)}), f32[48,384]{1,0:T(8,128)}) %reduce-scatter.43.cloned.1.call-update) | async-done | bytes 73744
  1025.2 61.0 %reduce-scatter.41.cloned.1.call-done = f32[48,384]{1,0:T(8,128)} async-done(((f32[768,384]{1,0:T(8,128)}), f32[48,384]{1,0:T(8,128)}) %reduce-scatter.41.cloned.1.call-update) | async-done | bytes 73744
  1086.3 61.2 %reduce-scatter.39.cloned.1.call-done = f32[48,384]{1,0:T(8,128)} async-done(((f32[768,384]{1,0:T(8,128)}), f32[48,384]{1,0:T(8,128)}) %reduce-scatter.39.cloned.1.call-update) | async-done | bytes 73744
  (244 shorter events, 125.8 us)
Async XLA Ops:
  8.0 51.0 %copy-start.42 = (bf16[48,384]{1,0:T(8,128)(2,1)S(1)}, bf16[48,384]{1,0:T(8,128)(2,1)}, u32[]{:S(2)}) copy-start(bf16[48,384]{1,0:T(8,128)(2,1)} %param.17) | copy-start | bytes 110596
  8.0 72.8 %copy-start.43 = (bf16[384,48]{0,1:T(8,128)(2,1)S(1)}, bf16[384,48]{0,1:T(8,128)(2,1)}, u32[]{:S(2)}) copy-start(bf16[384,48]{0,1:T(8,128)(2,1)} %param.18) | copy-start | bytes 110596
  8.0 94.0 %all-gather.7.cloned.1.call-start = ((), (), s32[]{:S(2)}) async-start(), calls=%async_computation.10 | async-start | bytes 3538944 | tf_op jit(solution)/shard_map/all_gather | solution.py:35
  8.8 218.6 %reduce-scatter.31.cloned.1.call-start = ((), (), s32[]{:S(2)}) async-start(), calls=%async_computation.19 | async-start | bytes 3538944
  39.7 65.3 %copy-start.23 = (bf16[768,384]{1,0:T(8,128)(2,1)}, bf16[768,384]{1,0:T(8,128)(2,1)S(1)}, u32[]{:S(2)}) copy-start(bf16[768,384]{1,0:T(8,128)(2,1)S(1)} %all_gather.32) | copy-start | bytes 1769476
  59.0 46.0 %copy-start.21 = (bf16[768,384]{1,0:T(8,128)(2,1)}, bf16[768,384]{1,0:T(8,128)(2,1)S(1)}, u32[]{:S(2)}) copy-start(bf16[768,384]{1,0:T(8,128)(2,1)S(1)} %all_gather.33) | copy-start | bytes 1769476
  106.9 57.2 %copy-start.1 = (bf16[1536,6,32]{0,2,1:T(8,128)(2,1)}, bf16[1536,6,32]{0,2,1:T(8,128)(2,1)S(1)}, u32[]{:S(2)}) copy-start(bf16[1536,6,32]{0,2,1:T(8,128)(2,1)S(1)} %get-tuple-element.142) | copy-start | bytes 1769476
  106.9 57.2 %copy-start.3 = (bf16[1536,6,32]{0,2,1:T(8,128)(2,1)}, bf16[1536,6,32]{0,2,1:T(8,128)(2,1)S(1)}, u32[]{:S(2)}) copy-start(bf16[1536,6,32]{0,2,1:T(8,128)(2,1)S(1)} %get-tuple-element.143) | copy-start | bytes 1769476
  123.2 31.5 %copy-start.34 = (f32[6,512]{1,0:T(8,128)}, f32[6,512]{1,0:T(8,128)S(1)}, u32[]{:S(2)}) copy-start(f32[6,512]{1,0:T(8,128)S(1)} %get-tuple-element.156) | copy-start | bytes 36868
  135.7 45.3 %copy-start.5 = (bf16[1536,384]{0,1:T(8,128)(2,1)}, bf16[1536,384]{0,1:T(8,128)(2,1)S(1)}, u32[]{:S(2)}) copy-start(bf16[1536,384]{0,1:T(8,128)(2,1)S(1)} %convolution_convert_fusion.4) | copy-start | bytes 3538948
  154.7 9.4 copy-start.48
  172.0 9.0 copy-start.40
  181.0 8.4 copy-start.41
  194.5 34.6 %copy-start = (bf16[1536,384]{1,0:T(8,128)(2,1)S(1)}, bf16[1536,384]{1,0:T(8,128)(2,1)}, u32[]{:S(2)}) copy-start(bf16[1536,384]{1,0:T(8,128)(2,1)} %param.13) | copy-start | bytes 3538948
  194.5 45.3 %all-gather.11.cloned.1.call-start = ((), (), s32[]{:S(2)}) async-start(), calls=%async_computation.12 | async-start | bytes 2506752 | tf_op jit(solution)/shard_map/all_gather | solution.py:236
  195.1 82.3 %all-gather.9.cloned.1.call-start = ((), (), s32[]{:S(2)}) async-start(), calls=%async_computation.11 | async-start | bytes 3538944 | tf_op jit(solution)/shard_map/all_gather | solution.py:35
  239.2 83.9 %all-gather.13.cloned.1.call-start = ((), (), s32[]{:S(2)}) async-start(), calls=%async_computation.13 | async-start | bytes 2506752 | tf_op jit(solution)/shard_map/all_gather | solution.py:240
  239.7 129.1 %reduce-scatter.33.cloned.1.call-start = ((), (), s32[]{:S(2)}) async-start(), calls=%async_computation.20 | async-start | bytes 3538944
  335.8 103.0 %all-gather.15.cloned.1.call-start = ((), (), s32[]{:S(2)}) async-start(), calls=%async_computation.14 | async-start | bytes 3538944 | tf_op jit(solution)/shard_map/all_gather | solution.py:35
  398.9 96.3 %reduce-scatter.35.cloned.1.call-start = ((), (), s32[]{:S(2)}) async-start(), calls=%async_computation.21 | async-start | bytes 3538944
  438.8 12.0 %copy-start.52 = (bf16[768,1536]{1,0:T(8,128)(2,1)S(1)}, bf16[768,1536]{1,0:T(8,128)(2,1)}, u32[]{:S(2)}) copy-start(bf16[768,1536]{1,0:T(8,128)(2,1)} %all-gather.11.cloned.1.call-done) | copy-start | bytes 7077892
  460.3 91.5 %all-gather.17.cloned.1.call-start = ((), (), s32[]{:S(2)}) async-start(), calls=%async_computation.15 | async-start | bytes 3538944 | tf_op jit(solution)/shard_map/all_gather | solution.py:35
  513.1 269.3 %reduce-scatter.37.cloned.1.call-start = ((), (), s32[]{:S(2)}) async-start(), calls=%async_computation.22 | async-start | bytes 3538944
  555.7 12.7 %copy-start.16 = (bf16[512,384]{0,1:T(8,128)(2,1)}, bf16[512,384]{0,1:T(8,128)(2,1)S(1)}, u32[]{:S(2)}) copy-start(bf16[512,384]{0,1:T(8,128)(2,1)S(1)} %get-tuple-element.137) | copy-start | bytes 1179652
  568.4 33.6 %slice-start = ((s8[18874368]{0:T(1024)(128)(4,1)}), s8[4194304]{0:T(1024)(128)(4,1)S(1)}, s32[]{:S(2)}) async-start(s8[18874368]{0:T(1024)(128)(4,1)} %bitcast.101), calls=%async_computation.26 | async-start | bytes 8388608
  568.4 33.6 %slice-start.1 = ((s8[18874368]{0:T(1024)(128)(4,1)}), s8[4194304]{0:T(1024)(128)(4,1)S(1)}, s32[]{:S(2)}) async-start(s8[18874368]{0:T(1024)(128)(4,1)} %bitcast.101), calls=%async_computation.27 | async-start | bytes 8388608
  568.4 33.6 %slice-start.2 = ((s8[18874368]{0:T(1024)(128)(4,1)}), s8[4194304]{0:T(1024)(128)(4,1)S(1)}, s32[]{:S(2)}) async-start(s8[18874368]{0:T(1024)(128)(4,1)} %bitcast.101), calls=%async_computation.28 | async-start | bytes 8388608
  568.4 33.6 %slice-start.3 = ((s8[18874368]{0:T(1024)(128)(4,1)}), s8[4194304]{0:T(1024)(128)(4,1)S(1)}, s32[]{:S(2)}) async-start(s8[18874368]{0:T(1024)(128)(4,1)} %bitcast.101), calls=%async_computation.29 | async-start | bytes 8388608
  586.4 8.6 copy-start.2
  586.4 8.6 copy-start.4
  586.4 15.6 %slice-start.4 = ((s8[18874368]{0:T(1024)(128)(4,1)}), s8[2097152]{0:T(1024)(128)(4,1)S(1)}, s32[]{:S(2)}) async-start(s8[18874368]{0:T(1024)(128)(4,1)} %bitcast.101), calls=%async_computation.30 | async-start | bytes 4194304
  606.4 13.1 %copy-start.7 = (f32[6,64,1536]{2,1,0:T(8,128)S(1)}, f32[6,64,1536]{2,1,0:T(8,128)}, u32[]{:S(2)}) copy-start(f32[6,64,1536]{2,1,0:T(8,128)} %fusion.12) | copy-start | bytes 7077892
  606.4 13.1 %copy-start.17 = (bf16[512,384]{0,1:T(8,128)(2,1)S(1)}, bf16[512,384]{0,1:T(8,128)(2,1)}, u32[]{:S(2)}) copy-start(bf16[512,384]{0,1:T(8,128)(2,1)} %copy-done.16) | copy-start | bytes 1179652
  627.6 12.5 %copy-start.15 = (bf16[512,384]{0,1:T(8,128)(2,1)S(1)}, bf16[512,384]{0,1:T(8,128)(2,1)}, u32[]{:S(2)}) copy-start(bf16[512,384]{0,1:T(8,128)(2,1)} %get-tuple-element.138) | copy-start | bytes 1179652
  640.1 34.0 %slice-start.5 = ((s8[18874368]{0:T(1024)(128)(4,1)}), s8[4194304]{0:T(1024)(128)(4,1)S(1)}, s32[]{:S(2)}) async-start(s8[18874368]{0:T(1024)(128)(4,1)} %bitcast.103), calls=%async_computation.31 | async-start | bytes 8388608
  640.1 34.0 %slice-start.6 = ((s8[18874368]{0:T(1024)(128)(4,1)}), s8[2097152]{0:T(1024)(128)(4,1)S(1)}, s32[]{:S(2)}) async-start(s8[18874368]{0:T(1024)(128)(4,1)} %bitcast.103), calls=%async_computation.32 | async-start | bytes 4194304
  649.5 24.6 %slice-start.7 = ((s8[18874368]{0:T(1024)(128)(4,1)}), s8[4194304]{0:T(1024)(128)(4,1)S(1)}, s32[]{:S(2)}) async-start(s8[18874368]{0:T(1024)(128)(4,1)} %bitcast.103), calls=%async_computation.33 | async-start | bytes 8388608
  649.5 24.6 %slice-start.8 = ((s8[18874368]{0:T(1024)(128)(4,1)}), s8[4194304]{0:T(1024)(128)(4,1)S(1)}, s32[]{:S(2)}) async-start(s8[18874368]{0:T(1024)(128)(4,1)} %bitcast.103), calls=%async_computation.34 | async-start | bytes 8388608
  649.5 24.6 %slice-start.9 = ((s8[18874368]{0:T(1024)(128)(4,1)}), s8[4194304]{0:T(1024)(128)(4,1)S(1)}, s32[]{:S(2)}) async-start(s8[18874368]{0:T(1024)(128)(4,1)} %bitcast.103), calls=%async_computation.35 | async-start | bytes 8388608
  687.2 12.4 %slice-start.10 = ((s8[9437184]{0:T(1024)(128)(4,1)}), s8[1048576]{0:T(1024)(128)(4,1)S(1)}, s32[]{:S(2)}) async-start(s8[9437184]{0:T(1024)(128)(4,1)} %bitcast.105), calls=%async_computation.36 | async-start | bytes 2097152
  687.2 12.4 %slice-start.11 = ((s8[9437184]{0:T(1024)(128)(4,1)}), s8[4194304]{0:T(1024)(128)(4,1)S(1)}, s32[]{:S(2)}) async-start(s8[9437184]{0:T(1024)(128)(4,1)} %bitcast.105), calls=%async_computation.37 | async-start | bytes 8388608
  711.2 113.2 %reduce-scatter.27.cloned.1.call-start = ((), (), s32[]{:S(2)}) async-start(), calls=%async_computation.17 | async-start | bytes 5013504 | tf_op jit(solution)/shard_map/reduce_scatter | solution.py:308
  720.7 182.5 %reduce-scatter.29.cloned.1.call-start = ((), (), s32[]{:S(2)}) async-start(), calls=%async_computation.18 | async-start | bytes 5013504 | tf_op jit(solution)/shard_map/reduce_scatter | solution.py:316
  730.5 233.6 %reduce-scatter.25.cloned.1.call-start = ((), (), s32[]{:S(2)}) async-start(), calls=%async_computation.16 | async-start | bytes 1253376 | tf_op jit(solution)/shard_map/reduce_scatter | solution.py:315
  735.8 289.4 %reduce-scatter.43.cloned.1.call-start = ((), (), s32[]{:S(2)}) async-start(), calls=%async_computation.25 | async-start | bytes 1253376
  740.1 346.2 %reduce-scatter.41.cloned.1.call-start = ((), (), s32[]{:S(2)}) async-start(), calls=%async_computation.24 | async-start | bytes 1253376
  744.3 403.1 %reduce-scatter.39.cloned.1.call-start = ((), (), s32[]{:S(2)}) async-start(), calls=%async_computation.23 | async-start | bytes 1253376
  748.6 35.5 %copy-start.8 = (f32[1536,384]{1,0:T(8,128)S(1)}, f32[1536,384]{1,0:T(8,128)}, u32[]{:S(2)}) copy-start(f32[1536,384]{1,0:T(8,128)} %get-tuple-element.124) | copy-start | bytes 7077892
  (36 other events, 115.8 us)
Sparse Core Ops, SparseCore 0:
  10.4 38.1 all-gather.6
  194.7 32.7 reduce-scatter.30
  335.9 32.7 reduce-scatter.32
  460.4 34.7 reduce-scatter.34
Sparse Core Ops, SparseCore 1:
  197.6 40.9 all-gather.10
  240.6 36.7 all-gather.8
  279.8 43.2 all-gather.12
  399.0 39.8 all-gather.14
  513.1 38.6 all-gather.16
  711.3 34.6 reduce-scatter.36
  750.2 74.1 reduce-scatter.26
  829.1 74.0 reduce-scatter.28
  907.3 56.7 reduce-scatter.24
  968.3 56.9 reduce-scatter.42
  1029.3 56.9 reduce-scatter.40
  1090.5 56.9 reduce-scatter.38
where the time goes:
time: 1160 us; the launch traced here: 1150 us
  waiting for transfers between devices  614 us (53%)
  matrix products  224 us (19%)
  blocking collectives  143 us (12%)
  other arithmetic  113 us (10%)
  local copies, waits for them, and re-layouts  42.9 us (4%)
  between operations  17.3 us (1%)
    unnamed x23, waiting for transfers between devices  285 us
    all_gather x4, waiting for transfers between devices, whole_features(): return lax.all_gather(values, 'narrow', axis=1, tiled=True)  114 us
    reduce_scatter x1, waiting for transfers between devices, shards(): lax.psum_scatter(outer_grad, 'wide', scatter_dimension=1, tiled=True)  78.9 us
    reduce_scatter x1, waiting for transfers between devices, shards(): lax.psum_scatter(output_grad, 'wide', scatter_dimension=1, tiled=True)  60.8 us
    convert_element_type x3, other arithmetic, one_group(): scores_grad = (soft * (inner - centre)).astype(jnp.bfloat16)  48.9 us
    unnamed x152, local copies, waits for them, and re-layouts  39.5 us
    reduce_scatter x1, waiting for transfers between devices, shards(): lax.psum_scatter(inner_grad, 'wide', scatter_dimension=0, tiled=True)  39 us
    dot_general x3, matrix products, one_group(): jnp.einsum('qhd,khd->hqk', block_grads, group_values, preferred_element_t...  37.7 us
  transfers between devices with their start and end apart: 16, of which 13 were waited for; matrix products, arithmetic and copies ran while one was open for 5% of the time, Pallas kernels for 0%

commit v1 on v0

--- a/solution.py
+++ b/solution.py
@@ -1,6 +1,11 @@
+import functools
+
 import jax
 import jax.numpy as jnp
+import numpy as np
 from jax import lax
+from jax.experimental import pallas as pl
+from jax.experimental.pallas import tpu as pltpu
 from jax.sharding import PartitionSpec as P
 
 HEAD_DIM = 64
@@ -331,6 +336,965 @@
     )
 
 
+LOW = jnp.bfloat16
+WIDE = jnp.float32
+MESH = pl.DeviceIdType.MESH
+MEGA = 1 << 20
+ANY = pl.BlockSpec(memory_space=pl.ANY)
+
+
+def contract(left, right, left_dim, right_dim):
+    return lax.dot_general(
+        left, right, (((left_dim,), (right_dim,)), ((), ())), preferred_element_type=WIDE
+    )
+
+
+def place():
+    x = lax.axis_index("narrow")
+    w = lax.axis_index("wide")
+    c = lax.rem(w, 2)
+    y = lax.rem(lax.div(w, 2), 2)
+    q = lax.div(w, 4)
+    return x, w, c, y, q
+
+
+class Links:
+    def __init__(self, depth):
+        self.depth = depth
+        self.x, self.w, self.c, self.y, self.q = place()
+        self.across = (1 - self.x, self.w)
+        self.beside = (self.x, self.w + 2 - 4 * self.y)
+        self.sibling = (self.x, self.w + 1 - 2 * self.c)
+        self.corner = (1 - self.x, self.w + 1 - 2 * self.c)
+
+    def far(self, step):
+        return (self.x, lax.rem(self.w + 4 * step, 4 * self.depth))
+
+    def row(self, step):
+        return lax.rem(self.q + self.depth - step, self.depth)
+
+    def meet(self):
+        barrier = pltpu.get_barrier_semaphore()
+        others = [self.across, self.beside, self.sibling, self.corner]
+        others += [self.far(step) for step in range(1, self.depth)]
+        for other in others:
+            pl.semaphore_signal(barrier, 1, device_id=other, device_id_type=MESH)
+        pl.semaphore_wait(barrier, len(others))
+
+
+def remote(source, target, send, recv, device):
+    return pltpu.make_async_remote_copy(
+        src_ref=source,
+        dst_ref=target,
+        send_sem=send,
+        recv_sem=recv,
+        device_id=device,
+        device_id_type=MESH,
+    )
+
+
+def gather_marks(depth):
+    return 5 * depth + 2
+
+
+class Gather:
+    def __init__(self, links, own, full, cut, whole, send, recv, index, local):
+        self.links, self.own, self.full, self.cut = links, own, full, cut
+        self.whole, self.local = whole, local
+        self.send = lambda k: send.at[index, k]
+        self.recv = lambda k: recv.at[index, k]
+        self.sent = []
+        self.width = own.shape[-1]
+
+    def slot(self, h, q, y):
+        return self.full.at[h, q, y, self.links.c]
+
+    def go(self, source, mark, device):
+        copy = remote(source, source, self.send(mark), self.recv(mark), device)
+        copy.start()
+        self.sent.append(copy)
+
+    def arrived(self, target, mark):
+        remote(target, target, self.send(mark), self.recv(mark), self.links.sibling).wait_recv()
+
+    def begin(self):
+        n, d = self.links, self.links.depth
+        mine = self.slot(n.x, n.q, n.y)
+        for step in range(1, d):
+            copy = remote(self.own, mine, self.send(step - 1), self.recv(step - 1), n.far(step))
+            copy.start()
+            self.sent.append(copy)
+        for mark, device in ((d, n.across), (2 * d, n.beside)):
+            copy = remote(self.own, mine, self.send(mark), self.recv(mark), device)
+            copy.start()
+            self.sent.append(copy)
+        self.keep = pltpu.make_async_copy(self.own, mine, self.local)
+        self.keep.start()
+
+    def second(self, step):
+        n, d = self.links, self.links.depth
+        got = self.slot(n.x, n.row(step), n.y)
+        self.arrived(got, step - 1)
+        self.go(got, d + step, n.across)
+        self.go(got, 2 * d + step, n.beside)
+
+    def third(self, step):
+        n, d = self.links, self.links.depth
+        got = self.slot(1 - n.x, n.row(step), n.y)
+        self.arrived(got, d + step)
+        part = got.at[:, pl.ds(self.cut, self.width - self.cut)]
+        self.go(part, 3 * d + step, n.beside)
+        got = self.slot(n.x, n.row(step), 1 - n.y)
+        self.arrived(got, 2 * d + step)
+        part = got.at[:, pl.ds(0, self.cut)]
+        self.go(part, 4 * d + step, n.across)
+
+    def fourth(self):
+        n, d = self.links, self.links.depth
+        for step in range(d):
+            got = self.slot(1 - n.x, n.row(step), 1 - n.y)
+            self.arrived(got.at[:, pl.ds(self.cut, self.width - self.cut)], 3 * d + step)
+            self.arrived(got.at[:, pl.ds(0, self.cut)], 4 * d + step)
+        self.keep.wait()
+        if self.whole:
+            for h in range(2):
+                self.go(self.full.at[h, :, :, n.c], 5 * d + h, n.sibling)
+        else:
+            self.go(self.full.at[1 - n.c, :, :, n.c], 5 * d, n.sibling)
+
+    def finish(self):
+        n, d = self.links, self.links.depth
+        if self.whole:
+            for h in range(2):
+                self.arrived(self.full.at[h, :, :, 1 - n.c], 5 * d + h)
+        else:
+            self.arrived(self.full.at[n.c, :, :, 1 - n.c], 5 * d)
+
+    def close(self):
+        for copy in self.sent:
+            copy.wait_send()
+
+
+def gather_kernel(depth, cuts, meta_in, cot_in, in_ref, q_own, m_own, o_own,
+                  meta, cot, rows, q_full, m_full, o_full, send, recv, local, extra_send, extra_recv):
+    n = Links(depth)
+    n.meet()
+    half = in_ref.shape[0] // 2
+    home = n.x == n.c
+    gathers = [
+        Gather(n, own, full, cut, whole, send, recv, k, local.at[k])
+        for k, (own, full, cut, whole) in enumerate(
+            zip((q_own, m_own, o_own), (q_full, m_full, o_full), cuts, (False, True, True))
+        )
+    ]
+    es = lambda k: extra_send.at[k]
+    er = lambda k: extra_recv.at[k]
+
+    @pl.when(jnp.logical_not(home))
+    def _():
+        remote(in_ref, rows.at[n.x], es(0), er(0), n.across).start()
+
+    gathers[0].begin()
+
+    @pl.when(home)
+    def _():
+        keep = pltpu.make_async_copy(in_ref, rows.at[n.x], local.at[3])
+        keep.start()
+        first = remote(in_ref, rows.at[n.x], es(1), er(1), n.sibling)
+        first.start()
+        note = remote(meta_in, meta, es(3), er(3), n.sibling)
+        note.start()
+        own = pltpu.make_async_copy(meta_in, meta, local.at[4])
+        own.start()
+        mine = pltpu.make_async_copy(cot_in.at[pl.ds(n.c * half, half)], cot.at[n.x], local.at[5])
+        mine.start()
+        theirs = remote(
+            cot_in.at[pl.ds((1 - n.c) * half, half)], cot.at[n.x], es(4), er(4), n.sibling
+        )
+        theirs.start()
+        remote(in_ref, rows.at[1 - n.x], es(0), er(0), n.across).wait_recv()
+        second = remote(rows.at[1 - n.x], rows.at[1 - n.x], es(2), er(2), n.sibling)
+        second.start()
+        keep.wait()
+        own.wait()
+        mine.wait()
+        first.wait_send()
+        note.wait_send()
+        theirs.wait_send()
+        second.wait_send()
+
+    @pl.when(jnp.logical_not(home))
+    def _():
+        remote(in_ref, rows.at[n.x], es(0), er(0), n.across).wait_send()
+        one = remote(
+            cot_in.at[pl.ds((1 - n.c) * half, half)], cot.at[n.x], es(6), er(6), n.corner
+        )
+        two = remote(cot_in.at[pl.ds(n.c * half, half)], cot.at[n.x], es(5), er(5), n.across)
+        one.start()
+        two.start()
+        remote(in_ref, rows.at[n.x], es(1), er(1), n.sibling).wait_recv()
+        remote(in_ref, rows.at[1 - n.x], es(2), er(2), n.sibling).wait_recv()
+        remote(meta_in, meta, es(3), er(3), n.sibling).wait_recv()
+        remote(cot_in.at[pl.ds(0, half)], cot.at[n.x], es(4), er(4), n.sibling).wait_recv()
+        one.wait_send()
+        two.wait_send()
+
+    for k in (0, 1, 2):
+        if k:
+            gathers[k].begin()
+        for step in range(1, depth):
+            gathers[k].second(step)
+        for step in range(depth):
+            gathers[k].third(step)
+        gathers[k].fourth()
+
+    @pl.when(home)
+    def _():
+        remote(cot_in.at[pl.ds(0, half)], cot.at[1 - n.x], es(5), er(5), n.across).wait_recv()
+
+    @pl.when(jnp.logical_not(home))
+    def _():
+        remote(cot_in.at[pl.ds(0, half)], cot.at[1 - n.x], es(6), er(6), n.corner).wait_recv()
+
+    for k in (0, 1, 2):
+        gathers[k].finish()
+        gathers[k].close()
+
+
+def gather_call(depth, cuts, meta, cot, rows, q_own, m_own, o_own):
+    r = q_own.shape[0]
+    shapes = [jax.ShapeDtypeStruct((2, depth, 2, 2) + own.shape, LOW) for own in (q_own, m_own, o_own)]
+    return pl.pallas_call(
+        functools.partial(gather_kernel, depth, cuts),
+        out_shape=[
+            jax.ShapeDtypeStruct(meta.shape, meta.dtype),
+            jax.ShapeDtypeStruct((2, cot.shape[0] // 2, cot.shape[1]), LOW),
+            jax.ShapeDtypeStruct((2,) + rows.shape, LOW),
+        ]
+        + shapes,
+        in_specs=[ANY] * 6,
+        out_specs=[ANY] * 6,
+        scratch_shapes=[
+            pltpu.SemaphoreType.DMA((3, gather_marks(depth))),
+            pltpu.SemaphoreType.DMA((3, gather_marks(depth))),
+            pltpu.SemaphoreType.DMA((6,)),
+            pltpu.SemaphoreType.DMA((7,)),
+            pltpu.SemaphoreType.DMA((7,)),
+        ],
+        compiler_params=pltpu.CompilerParams(collective_id=0, has_side_effects=True),
+        name="gather",
+    )(meta, cot, rows, q_own, m_own, o_own)
+
+
+def plus(left, right):
+    return (left.astype(WIDE) + right.astype(WIDE)).astype(LOW)
+
+
+def scatter_marks(depth):
+    return depth + 5
+
+
+class Scatter:
+    def __init__(self, links, part, cut, whole, bufs, out, send, recv, index, local):
+        self.links, self.part, self.cut, self.whole, self.out = links, part, cut, whole, out
+        self.held, self.other, self.x1, self.y1, self.x2, self.y2, self.z = bufs
+        self.send = lambda k: send.at[index, k]
+        self.recv = lambda k: recv.at[index, k]
+        self.local = local
+        self.sent = []
+        self.rest = part.shape[-1] - cut
+
+    def go(self, source, target, mark, device):
+        copy = remote(source, target, self.send(mark), self.recv(mark), device)
+        copy.start()
+        self.sent.append(copy)
+
+    def arrived(self, target, mark):
+        remote(target, target, self.send(mark), self.recv(mark), self.links.sibling).wait_recv()
+
+    def begin(self):
+        n = self.links
+        if self.whole:
+            self.go(self.part.at[:, :, :, 1 - n.c], self.other, 0, n.sibling)
+            self.keep = pltpu.make_async_copy(self.part.at[:, :, :, n.c], self.held, self.local)
+        else:
+            self.go(self.part.at[:, :, 1 - n.c], self.held.at[n.c], 0, n.sibling)
+            self.keep = pltpu.make_async_copy(
+                self.part.at[:, :, n.c], self.held.at[n.c], self.local
+            )
+        self.keep.start()
+
+    def join(self, h, y):
+        for q in range(self.links.depth):
+            self.held[h, q, y] = plus(self.held[h, q, y], self.other[h, q, y])
+
+    def first(self):
+        n = self.links
+        self.keep.wait()
+        if self.whole:
+            self.arrived(self.other, 0)
+            self.join(1 - n.x, 1 - n.y)
+        else:
+            self.arrived(self.held.at[1 - n.c], 0)
+        corner = self.held.at[1 - n.x, :, 1 - n.y]
+        self.go(corner.at[:, :, pl.ds(0, self.cut)], self.x1, 1, n.across)
+        self.go(corner.at[:, :, pl.ds(self.cut, self.rest)], self.y1, 2, n.beside)
+        if self.whole:
+            self.join(n.x, 1 - n.y)
+            self.join(1 - n.x, n.y)
+            self.join(n.x, n.y)
+
+    def second(self):
+        n = self.links
+        low, high = pl.ds(0, self.cut), pl.ds(self.cut, self.rest)
+        self.arrived(self.x1, 1)
+        for q in range(n.depth):
+            self.held[n.x, q, 1 - n.y, :, low] = plus(
+                self.held[n.x, q, 1 - n.y, :, low], self.x1[q]
+            )
+        self.go(self.held.at[n.x, :, 1 - n.y], self.y2, 3, n.beside)
+        self.arrived(self.y1, 2)
+        for q in range(n.depth):
+            self.held[1 - n.x, q, n.y, :, high] = plus(
+                self.held[1 - n.x, q, n.y, :, high], self.y1[q]
+            )
+        self.go(self.held.at[1 - n.x, :, n.y], self.x2, 4, n.across)
+
+    def third(self):
+        n = self.links
+        self.arrived(self.y2, 3)
+        self.arrived(self.x2, 4)
+        for step in range(1, n.depth):
+            q = lax.rem(n.q + step, n.depth)
+            self.held[n.x, q, n.y] = plus(
+                plus(self.held[n.x, q, n.y], self.x2[q]), self.y2[q]
+            )
+            self.go(self.held.at[n.x, q, n.y], self.z.at[step - 1], 4 + step, n.far(step))
+
+    def fourth(self):
+        n = self.links
+        total = (
+            self.held[n.x, n.q, n.y].astype(WIDE)
+            + self.x2[n.q].astype(WIDE)
+            + self.y2[n.q].astype(WIDE)
+        )
+        for step in range(1, n.depth):
+            self.arrived(self.z.at[step - 1], 4 + step)
+            total = total + self.z[step - 1].astype(WIDE)
+        self.out[...] = total
+
+    def close(self):
+        for copy in self.sent:
+            copy.wait_send()
+
+
+def scatter_scratch(depth, r, columns, cut):
+    return [
+        pltpu.VMEM((2, depth, 2, r, columns), LOW),
+        pltpu.VMEM((2, depth, 2, r, columns), LOW),
+        pltpu.VMEM((depth, r, cut), LOW),
+        pltpu.VMEM((depth, r, columns - cut), LOW),
+        pltpu.VMEM((depth, r, columns), LOW),
+        pltpu.VMEM((depth, r, columns), LOW),
+        pltpu.VMEM((depth - 1, r, columns), LOW),
+    ]
+
+
+class HandOver:
+    def __init__(self, links, source, target, send, recv, base, local):
+        self.links, self.source, self.target, self.local = links, source, target, local
+        self.send = lambda k: send.at[base + k]
+        self.recv = lambda k: recv.at[base + k]
+        self.half = source.shape[1]
+
+    def rows(self, c):
+        return self.target.at[pl.ds(c * self.half, self.half)]
+
+    def copies(self):
+        n = self.links
+        near, far = self.source.at[n.x], self.source.at[1 - n.x]
+        mine = self.rows(n.c)
+        return (
+            pltpu.make_async_copy(near, mine, self.local),
+            remote(far, mine, self.send(0), self.recv(0), n.across),
+            remote(near, mine, self.send(1), self.recv(1), n.sibling),
+            remote(far, mine, self.send(2), self.recv(2), n.corner),
+        )
+
+    def begin(self):
+        n = self.links
+        keep, across, sibling, corner = self.copies()
+
+        @pl.when(n.x == n.c)
+        def _():
+            keep.start()
+            across.start()
+
+        @pl.when(n.x != n.c)
+        def _():
+            sibling.start()
+            corner.start()
+
+    def finish(self):
+        n = self.links
+        keep, across, sibling, corner = self.copies()
+        mine, theirs = self.rows(n.c), self.rows(1 - n.c)
+
+        @pl.when(n.x == n.c)
+        def _():
+            keep.wait()
+            across.wait_send()
+            remote(theirs, theirs, self.send(1), self.recv(1), n.sibling).wait_recv()
+
+        @pl.when(n.x != n.c)
+        def _():
+            sibling.wait_send()
+            corner.wait_send()
+            remote(mine, mine, self.send(0), self.recv(0), n.across).wait_recv()
+            remote(theirs, theirs, self.send(2), self.recv(2), n.corner).wait_recv()
+
+
+def scatter_kernel(depth, cuts, lo_in, dx_in, o_part, m_part, q_part,
+                   lo_out, dx_out, o_out, m_out, q_out, *scratch):
+    bufs = [scratch[7 * k : 7 * k + 7] for k in range(3)]
+    dx_own, dx_other, send, recv, local, extra_send, extra_recv = scratch[21:]
+    n = Links(depth)
+    n.meet()
+    spread_out = remote(
+        dx_in.at[1 - n.c], dx_other, extra_send.at[6], extra_recv.at[6], n.sibling
+    )
+    spread_out.start()
+    spread_own = pltpu.make_async_copy(dx_in.at[n.c], dx_own, local.at[3])
+    spread_own.start()
+    scatters = [
+        Scatter(n, part, cut, whole, buf, out, send, recv, k, local.at[k])
+        for k, (part, out, cut, whole, buf) in enumerate(
+            zip(
+                (o_part, m_part, q_part), (o_out, m_out, q_out), cuts, (True, True, False), bufs
+            )
+        )
+    ]
+    for item in scatters:
+        item.begin()
+    spread_own.wait()
+    spread_out.wait_recv()
+    for h in range(2):
+        dx_own[h] = plus(dx_own[h], dx_other[h])
+    lo_over = HandOver(n, lo_in, lo_out, extra_send, extra_recv, 0, local.at[4])
+    dx_over = HandOver(n, dx_own, dx_out, extra_send, extra_recv, 3, local.at[5])
+    dx_over.begin()
+    lo_over.begin()
+    for item in scatters:
+        item.first()
+    for item in scatters:
+        item.second()
+    for item in scatters:
+        item.third()
+    for item in scatters:
+        item.fourth()
+    for item in scatters:
+        item.close()
+    spread_out.wait_send()
+    lo_over.finish()
+    dx_over.finish()
+
+
+def scatter_call(depth, cuts, lo, dx, o_part, m_part, q_part):
+    r = o_part.shape[-2]
+    half, part = lo.shape[1:]
+    widths = [item.shape[-1] for item in (o_part, m_part, q_part)]
+    scratch = []
+    for columns, cut in zip(widths, cuts):
+        scratch += scatter_scratch(depth, r, columns, cut)
+    vmem = pl.BlockSpec(memory_space=pltpu.VMEM)
+    return pl.pallas_call(
+        functools.partial(scatter_kernel, depth, cuts),
+        out_shape=[jax.ShapeDtypeStruct((2 * half, part), LOW)] * 2
+        + [jax.ShapeDtypeStruct((r, columns), WIDE) for columns in widths],
+        in_specs=[ANY] * 5,
+        out_specs=[ANY] * 2 + [vmem] * 3,
+        scratch_shapes=scratch
+        + [
+            pltpu.VMEM((2, half, part), LOW),
+            pltpu.VMEM((2, half, part), LOW),
+            pltpu.SemaphoreType.DMA((3, scatter_marks(depth))),
+            pltpu.SemaphoreType.DMA((3, scatter_marks(depth))),
+            pltpu.SemaphoreType.DMA((6,)),
+            pltpu.SemaphoreType.DMA((7,)),
+            pltpu.SemaphoreType.DMA((7,)),
+        ],
+        compiler_params=pltpu.CompilerParams(
+            collective_id=1, has_side_effects=True, vmem_limit_bytes=56 * MEGA
+        ),
+        name="scatter",
+    )(lo, dx, o_part, m_part, q_part)
+
+
+def angle_tables():
+    rates = THETA ** (-np.arange(HEAD_DIM // 2) / (HEAD_DIM // 2))
+    rates = np.tile(rates, 4)[None]
+    base = np.arange(BLOCK)[:, None] * rates
+    jump = np.arange(SPAN)[:, None] * BLOCK * rates
+    base = np.concatenate([np.cos(base), np.sin(base)], axis=0)
+    jump = np.concatenate([np.cos(jump), np.sin(jump), np.zeros((2, 128))], axis=0)
+    return jnp.asarray(base, WIDE), jnp.asarray(jump, WIDE)
+
+
+def lanes(rows):
+    return lax.broadcasted_iota(jnp.int32, (rows, 128), 1)
+
+
+def turn_parts(meta, base, jump, block):
+    offset = meta[0, SPAN + block]
+    far_cos = jump[pl.ds(offset, 1), :]
+    far_sin = jump[pl.ds(SPAN + offset, 1), :]
+    near_cos, near_sin = base[0:BLOCK], base[BLOCK : 2 * BLOCK]
+    cosine = near_cos * far_cos - near_sin * far_sin
+    sine = near_sin * far_cos + near_cos * far_sin
+    low = (lanes(BLOCK) % HEAD_DIM) < HEAD_DIM // 2
+    return cosine, jnp.where(low, -sine, sine), low
+
+
+def turn(values, cosine, sine, low):
+    swapped = jnp.where(low, pltpu.roll(values, 96, 1), pltpu.roll(values, 32, 1))
+    return values * cosine + swapped * sine
+
+
+def forward_kernel(meta, rows, weight, base, jump, q_ref, k_ref, v_ref, p_ref, r_ref, c_ref, marks):
+    step = pl.program_id(0)
+    scale = HEAD_DIM ** (-0.5)
+
+    @pl.when(step < SPAN)
+    def _():
+        here = pl.ds(step * BLOCK, BLOCK)
+        cosine, sine, low = turn_parts(meta, base, jump, step)
+        values = jnp.concatenate([rows[0, here], rows[1, here]], axis=1)
+        for p in range(3):
+            made = contract(values, weight[:, p * 384 : p * 384 + 384], 1, 0)
+            q_ref[p, here] = (turn(made[:, 0:128], cosine, sine, low) * scale).astype(LOW)
+            k_ref[p, here] = turn(made[:, 128:256], cosine, sine, low).astype(LOW)
+            v_ref[p, here] = made[:, 256:384].astype(LOW)
+        marks[here] = (lanes(BLOCK) == meta[0, step]).astype(WIDE).astype(LOW)
+
+    @pl.when(step >= SPAN)
+    def _():
+        turn_number = step - SPAN
+        p = turn_number // SPAN
+        i = turn_number % SPAN
+        here = pl.ds(i * BLOCK, BLOCK)
+        lane = lanes(BLOCK)
+        queries = q_ref[p, here]
+        values = v_ref[p]
+        keys = jnp.concatenate([k_ref[p], marks[...]], axis=1)
+        barred = jnp.where((lane < SPAN) & (lane != meta[0, i]), NEGATIVE, 0.0).astype(LOW)
+        outs = []
+        scales = []
+        for head in range(2):
+            chosen = (lane // HEAD_DIM) == head
+            ours = jnp.concatenate([jnp.where(chosen, queries, 0).astype(LOW), barred], axis=1)
+            scores = contract(ours, keys, 1, 1)
+            top = jnp.max(scores, axis=1, keepdims=True)
+            raised = jnp.exp(scores - top)
+            inverse = 1.0 / jnp.sum(raised, axis=1, keepdims=True)
+            soft = raised.astype(LOW)
+            p_ref[0, head] = soft
+            outs.append(contract(soft, values, 1, 0))
+            scales.append(inverse)
+        inverse = jnp.where(lane < HEAD_DIM, scales[0], scales[1])
+        r_ref[p, here] = inverse
+        c_ref[p, here] = (jnp.where(lane < HEAD_DIM, outs[0], outs[1]) * inverse).astype(LOW)
+
+
+def forward_call(meta, rows, weight, base, jump):
+    length = rows.shape[1]
+    trio = jax.ShapeDtypeStruct((3, length, 128), LOW)
+    vmem = pl.BlockSpec(memory_space=pltpu.VMEM)
+    soft_shape = (SPAN * 3, 2, BLOCK, length)
+    return pl.pallas_call(
+        forward_kernel,
+        grid=(SPAN + 3 * SPAN,),
+        out_shape=[
+            trio,
+            trio,
+            trio,
+            jax.ShapeDtypeStruct(soft_shape, LOW),
+            jax.ShapeDtypeStruct((3, length, 128), WIDE),
+            trio,
+        ],
+        in_specs=[pl.BlockSpec(memory_space=pltpu.SMEM)] + [vmem] * 4,
+        out_specs=[
+            vmem,
+            vmem,
+            vmem,
+            pl.BlockSpec((1, 2, BLOCK, length), lambda s: (jnp.maximum(s - SPAN, 0), 0, 0, 0)),
+            vmem,
+            vmem,
+        ],
+        scratch_shapes=[pltpu.VMEM((length, 128), LOW)],
+        compiler_params=pltpu.CompilerParams(vmem_limit_bytes=60 * MEGA),
+        name="attend",
+    )(meta, rows, weight, base, jump)
+
+
+def norm_of(summed):
+    mean = jnp.mean(summed, axis=1, keepdims=True)
+    centred = summed - mean
+    variance = jnp.mean(centred * centred, axis=1, keepdims=True)
+    scale = lax.rsqrt(variance + EPSILON)
+    return centred * scale, scale
+
+
+def norm_back(scaled, normed, scale):
+    total = jnp.mean(scaled, axis=1, keepdims=True)
+    cross = jnp.mean(scaled * normed, axis=1, keepdims=True)
+    return scale * (scaled - total - normed * cross)
+
+
+HIDDEN = 512
+
+
+def middle_kernel(context, rows, cot, m_full, o_full, gains, lo_ref, gc_ref, act_ref, gi_ref, fl_ref,
+                  gm_ref, ga_ref, gfs_ref, sums, slopes):
+    tile = rows.shape[1]
+    part = rows.shape[2]
+    pieces = o_full.shape[2] // HIDDEN
+    gain1, bias1, gain2, bias2 = (gains[k : k + 1, :] for k in range(4))
+    summed = jnp.concatenate([rows[0], rows[1]], axis=1).astype(WIDE)
+    for h in range(2):
+        summed = summed + contract(context[h], m_full[h, :, 0:part], 1, 1)
+    normed1, scale1 = norm_of(summed)
+    first = normed1 * gain1 + bias1
+    first_low = first.astype(LOW)
+    fl_ref[...] = first_low
+    mixed = jnp.zeros(first.shape, WIDE)
+    for h in range(2):
+        for j in range(pieces):
+            k = h * pieces + j
+            lo_end = part + j * HIDDEN
+            inner = contract(first_low, m_full[h, :, lo_end : lo_end + HIDDEN], 1, 0)
+            share = 0.5 * (1.0 + lax.erf(inner * ROOT_HALF))
+            slopes[:, k * HIDDEN : (k + 1) * HIDDEN] = (
+                share + inner * jnp.exp(-0.5 * inner * inner) * INVERSE_ROOT
+            )
+            act_ref[:, k * HIDDEN : (k + 1) * HIDDEN] = (inner * share).astype(LOW)
+    for h in range(2):
+        width = pieces * HIDDEN
+        mixed = mixed + contract(act_ref[:, h * width : (h + 1) * width], o_full[h], 1, 1)
+    normed2, scale2 = norm_of(first + mixed)
+    result = (normed2 * gain2 + bias2).astype(LOW)
+    for h in range(2):
+        lo_ref[h] = result[:, h * part : (h + 1) * part]
+    cotangent = jnp.concatenate([cot[0], cot[1]], axis=1).astype(WIDE)
+    second_gain = jnp.sum(cotangent * normed2, axis=0, keepdims=True)
+    second_bias = jnp.sum(cotangent, axis=0, keepdims=True)
+    grad_second = norm_back(cotangent * gain2, normed2, scale2)
+    grad_mixed = grad_second.astype(LOW)
+    gm_ref[...] = grad_mixed
+    for h in range(2):
+        for j in range(pieces):
+            k = h * pieces + j
+            raised = contract(grad_mixed, o_full[h, :, j * HIDDEN : (j + 1) * HIDDEN], 1, 0)
+            gi_ref[:, k * HIDDEN : (k + 1) * HIDDEN] = (
+                raised * slopes[:, k * HIDDEN : (k + 1) * HIDDEN]
+            ).astype(LOW)
+    grad_first = grad_second
+    for h in range(2):
+        width = pieces * HIDDEN
+        grad_first = grad_first + contract(
+            gi_ref[:, h * width : (h + 1) * width], m_full[h, :, part : part + width], 1, 1
+        )
+    first_gain = jnp.sum(grad_first * normed1, axis=0, keepdims=True)
+    first_bias = jnp.sum(grad_first, axis=0, keepdims=True)
+    grad_sum = norm_back(grad_first * gain1, normed1, scale1)
+    gfs_ref[...] = grad_sum
+    grad_attended = grad_sum.astype(LOW)
+    ga_ref[...] = grad_attended
+    for h in range(2):
+        gc_ref[h] = contract(grad_attended, m_full[h, :, 0:part], 1, 0).astype(LOW)
+    found = jnp.concatenate([first_gain, first_bias, second_gain, second_bias], axis=0)
+
+    @pl.when(pl.program_id(0) == 0)
+    def _():
+        sums[...] = found
+
+    @pl.when(pl.program_id(0) > 0)
+    def _():
+        sums[...] += found
+
+
+def middle_call(context, rows, cot, m_full, o_full, gains):
+    tile = 256
+    half, part = rows.shape[1:]
+    width = 2 * part
+    hidden = 2 * o_full.shape[2]
+    vmem = pl.BlockSpec(memory_space=pltpu.VMEM)
+    split = pl.BlockSpec((2, tile, part), lambda i: (0, i, 0))
+    flat = pl.BlockSpec((tile, width), lambda i: (i, 0))
+    wide = pl.BlockSpec((tile, hidden), lambda i: (i, 0))
+    low = lambda *shape: jax.ShapeDtypeStruct(shape, LOW)
+    return pl.pallas_call(
+        middle_kernel,
+        grid=(half // tile,),
+        out_shape=[
+            low(2, half, part),
+            low(2, half, part),
+            low(half, hidden),
+            low(half, hidden),
+            low(half, width),
+            low(half, width),
+            low(half, width),
+            jax.ShapeDtypeStruct((half, width), WIDE),
+            jax.ShapeDtypeStruct((4, width), WIDE),
+        ],
+        in_specs=[split, split, split, vmem, vmem, vmem],
+        out_specs=[
+            split,
+            split,
+            wide,
+            wide,
+            flat,
+            flat,
+            flat,
+            flat,
+            pl.BlockSpec((4, width), lambda i: (0, 0)),
+        ],
+        scratch_shapes=[pltpu.VMEM((tile, hidden), WIDE)],
+        compiler_params=pltpu.CompilerParams(vmem_limit_bytes=60 * MEGA),
+        name="middle",
+    )(context, rows, cot, m_full, o_full, gains)
+
+
+def backward_kernel(core, meta, base, jump, soft, grads, context, inverse, q_ref, k_ref, v_ref, rows,
+                    weight, kept, part_ref, dx_ref, ones, keys_sum, values_sum, made):
+    step = pl.program_id(0)
+    p = step // SPAN
+    i = step % SPAN
+    length = q_ref.shape[1]
+    scale = HEAD_DIM ** (-0.5)
+    lane = lanes(BLOCK)
+    here = pl.ds(i * BLOCK, BLOCK)
+
+    @pl.when(step == 0)
+    def _():
+        ones[...] = (lanes(length) < 2).astype(WIDE).astype(LOW)
+
+    grad = grads[p, here].astype(WIDE)
+    turned = grad * inverse[p, here]
+    both = turned * context[p, here].astype(WIDE)
+    turned_low = turned.astype(LOW)
+    queries = q_ref[p, here]
+    keys = k_ref[p]
+    values = jnp.concatenate([v_ref[p], ones[...]], axis=1)
+    turned_flip = jnp.transpose(turned).astype(LOW)
+    queries_flip = jnp.transpose(queries.astype(WIDE)).astype(LOW)
+    outs = []
+    for head in range(2):
+        chosen = (lane // HEAD_DIM) == head
+        centre = -jnp.sum(jnp.where(chosen, both, 0.0), axis=1, keepdims=True)
+        coarse = centre.astype(LOW).astype(WIDE)
+        fine = jnp.where(lane == 0, coarse, jnp.where(lane == 1, centre - coarse, 0.0))
+        ours = jnp.concatenate(
+            [jnp.where(chosen, turned_low, 0).astype(LOW), fine.astype(LOW)], axis=1
+        )
+        raised = soft[0, head]
+        scores = (contract(ours, values, 1, 1) * raised.astype(WIDE)).astype(LOW)
+        outs.append(contract(scores, keys, 1, 0))
+        mine = slice(head * HEAD_DIM, (head + 1) * HEAD_DIM)
+        values_add = contract(turned_flip[mine], raised, 1, 0)
+        keys_add = contract(queries_flip[mine], scores, 1, 0)
+
+        @pl.when(i == 0)
+        def _():
+            values_sum[mine] = values_add
+            keys_sum[mine] = keys_add
+
+        @pl.when(i > 0)
+        def _():
+            values_sum[mine] += values_add
+            keys_sum[mine] += keys_add
+
+    cosine, sine, low = turn_parts(meta, base, jump, i)
+    grad_queries = jnp.where(lane < HEAD_DIM, outs[0], outs[1]) * scale
+    made[p, here, 0:128] = turn(grad_queries, cosine, -sine, low).astype(LOW)
+
+    @pl.when(i == SPAN - 1)
+    def _():
+        grad_keys = jnp.transpose(keys_sum[...])
+        grad_values = jnp.transpose(values_sum[...])
+        for b in range(SPAN):
+            there = slice(b * BLOCK, (b + 1) * BLOCK)
+            cosine, sine, low = turn_parts(meta, base, jump, b)
+            made[p, there, 128:256] = turn(grad_keys[there], cosine, -sine, low).astype(LOW)
+        made[p, :, 256:384] = grad_values.astype(LOW)
+        for h in range(2):
+            part = rows.shape[2]
+            part_ref[p, h * part : (h + 1) * part] = contract(rows[h], made[p], 0, 0).astype(LOW)
+
+    @pl.when(step == 3 * SPAN - 1)
+    def _():
+        half = kept.shape[0]
+        part = rows.shape[2]
+        for other in range(2):
+            c = core[0] if other == 0 else 1 - core[0]
+            there = pl.ds(c * half, half)
+            gained = kept[...] if other == 0 else jnp.zeros(kept.shape, WIDE)
+            for pair in range(3):
+                gained = gained + contract(made[pair, there], weight[:, pair * 384 : pair * 384 + 384], 1, 1)
+            for h in range(2):
+                dx_ref[c, h] = gained[:, h * part : (h + 1) * part].astype(LOW)
+
+
+def backward_call(core, meta, base, jump, soft, grads, context, inverse, q, k, v, rows, weight, kept):
+    length = q.shape[1]
+    half, width = kept.shape
+    part = width // 2
+    vmem = pl.BlockSpec(memory_space=pltpu.VMEM)
+    smem = pl.BlockSpec(memory_space=pltpu.SMEM)
+    return pl.pallas_call(
+        backward_kernel,
+        grid=(3 * SPAN,),
+        out_shape=[
+            jax.ShapeDtypeStruct((3, width, 384), LOW),
+            jax.ShapeDtypeStruct((2, 2, half, part), LOW),
+        ],
+        in_specs=[smem, smem, vmem, vmem, pl.BlockSpec((1, 2, BLOCK, length), lambda s: (s, 0, 0, 0))]
+        + [vmem] * 9,
+        out_specs=[vmem, vmem],
+        scratch_shapes=[
+            pltpu.VMEM((length, 128), LOW),
+            pltpu.VMEM((128, length), WIDE),
+            pltpu.VMEM((128, length), WIDE),
+            pltpu.VMEM((3, length, 384), LOW),
+        ],
+        compiler_params=pltpu.CompilerParams(vmem_limit_bytes=60 * MEGA),
+        name="attend_back",
+    )(core, meta, base, jump, soft, grads, context, inverse, q, k, v, rows, weight, kept)
+
+
+def swap_halves(values, half, c):
+    mine = lax.dynamic_slice_in_dim(values, c * half, half, axis=1)
+    theirs = lax.dynamic_slice_in_dim(values, (1 - c) * half, half, axis=1)
+    n_wide = lax.axis_size("wide")
+    got = lax.ppermute(theirs, "wide", [(w, w ^ 1) for w in range(n_wide)])
+    mine, got = (jnp.moveaxis(item, 0, 1).reshape(half, -1) for item in (mine, got))
+    return jnp.where(c == 0, jnp.stack([mine, got]), jnp.stack([got, mine]))
+
+
+def swap_back(values, half, c):
+    n_wide = lax.axis_size("wide")
+    mine = lax.dynamic_index_in_dim(values, c, 0, keepdims=False)
+    theirs = lax.dynamic_index_in_dim(values, 1 - c, 0, keepdims=False)
+    got = lax.ppermute(theirs, "wide", [(w, w ^ 1) for w in range(n_wide)])
+    whole = jnp.where(c == 0, jnp.concatenate([mine, got]), jnp.concatenate([got, mine]))
+    return jnp.moveaxis(whole.reshape(whole.shape[0], -1, 128), 1, 0)
+
+
+def owned(
+    inputs,
+    block_segment,
+    query_weight,
+    key_weight,
+    value_weight,
+    output_weight,
+    inner_weight,
+    outer_weight,
+    first_gain,
+    first_bias,
+    second_gain,
+    second_bias,
+    output_cotangent,
+):
+    wide = lax.axis_size("wide")
+    depth = wide // 4
+    r = query_weight.shape[0]
+    part = query_weight.shape[1]
+    length = inputs.shape[0]
+    half = length // 2
+    x, w, c, _, _ = place()
+    pairs = part // 128
+    q_own = jnp.concatenate(
+        [
+            item[:, p * 128 : (p + 1) * 128]
+            for p in range(pairs)
+            for item in (query_weight, key_weight, value_weight)
+        ],
+        axis=1,
+    )
+    m_own = jnp.concatenate([output_weight.T, inner_weight], axis=1)
+    o_own = outer_weight.T
+    earlier = jnp.sum((block_segment[None, :] < block_segment[:, None]).astype(jnp.int32), axis=1)
+    offsets = jnp.arange(SPAN, dtype=jnp.int32) - earlier
+    meta = jnp.zeros((1, 128), jnp.int32)
+    meta = meta.at[0, 0:SPAN].set(block_segment).at[0, SPAN : 2 * SPAN].set(offsets)
+    widths = [item.shape[1] for item in (q_own, m_own, o_own)]
+    cuts = [(item // 128 // 2) * 128 for item in widths]
+    meta, cot, rows, q_full, m_full, o_full = gather_call(
+        depth, cuts, meta, output_cotangent, inputs, q_own, m_own, o_own
+    )
+    gains = jnp.stack([first_gain, first_bias, second_gain, second_bias])
+    gains = lax.all_gather(gains, "narrow", axis=1, tiled=True)
+    weight = lax.dynamic_index_in_dim(q_full, c, 0, keepdims=False).reshape(2 * part, widths[0])
+    m_full = m_full.reshape(2, 2 * part, widths[1])
+    o_full = o_full.reshape(2, 2 * part, widths[2])
+    base, jump = angle_tables()
+    q, k, v, soft, inverse, context = forward_call(meta, rows, weight, base, jump)
+    all_context = swap_halves(context, half, c)
+    own_rows = lax.dynamic_slice_in_dim(rows, c * half, half, axis=1)
+    lo, gc, act, gi, fl, gm, ga, kept, sums = middle_call(
+        all_context, own_rows, cot, m_full, o_full, gains
+    )
+    hidden = act.shape[1] // 2
+    o_part = jnp.stack(
+        [left_transposed(gm, act[:, h * hidden : (h + 1) * hidden]).astype(LOW) for h in range(2)]
+    )
+    m_part = jnp.stack(
+        [
+            jnp.concatenate(
+                [
+                    left_transposed(ga, all_context[h]).astype(LOW),
+                    left_transposed(fl, gi[:, h * hidden : (h + 1) * hidden]).astype(LOW),
+                ],
+                axis=1,
+            )
+            for h in range(2)
+        ]
+    )
+    grads = swap_back(gc, half, c)
+    core = jnp.reshape(c, (1,)).astype(jnp.int32)
+    q_part, dx = backward_call(
+        core, meta, base, jump, soft, grads, context, inverse, q, k, v, rows, weight, kept
+    )
+    q_part = jnp.moveaxis(q_part, 0, 1)
+    q_part = q_part.reshape(depth, 2, 2, r, widths[0])
+    m_part = m_part.reshape(2, depth, 2, 2, r, widths[1])
+    o_part = o_part.reshape(2, depth, 2, 2, r, widths[2])
+    layer_output, input_gradient, o_sum, m_sum, q_sum = scatter_call(
+        depth, [cuts[2], cuts[1], cuts[0]], lo, dx, o_part, m_part, q_part
+    )
+    q_sum = q_sum.reshape(r, pairs, 3, 128)
+    sums = lax.psum_scatter(sums, ("narrow", "wide"), scatter_dimension=1, tiled=True)
+    return (
+        layer_output,
+        input_gradient,
+        q_sum[:, :, 0].reshape(r, part),
+        q_sum[:, :, 1].reshape(r, part),
+        q_sum[:, :, 2].reshape(r, part),
+        m_sum[:, 0:part].T,
+        m_sum[:, part:],
+        o_sum.T,
+        sums[0],
+        sums[1],
+        sums[2],
+        sums[3],
+    )
+
+
+def program(*arrays):
+    rows = arrays[2].shape[0]
+    whole = rows % 16 == 0 and lax.axis_size("narrow") == 2 and lax.axis_size("wide") % 4 == 0
+    return owned(*arrays) if whole else shards(*arrays)
+
+
 def solution(mesh):
     placed = (
         P("wide", "narrow"),
@@ -348,7 +1312,7 @@
         P("wide", "narrow"),
     )
     return jax.shard_map(
-        shards,
+        program,
         mesh=mesh,
         in_specs=placed,
         out_specs=(

time: 1160 us -> 491 us (0.42)
  waiting for transfers between devices: 614 us -> 0.01 us
  Pallas kernels: 0 us -> 366 us
  matrix products: 224 us -> 18.7 us
  blocking collectives: 143 us -> 42.3 us
  other arithmetic: 113 us -> 16.9 us
  between operations: 17.3 us -> 1.25 us
    pallas_call x0 -> x5, Pallas kernels: none -> 366 us  [the longest x1 135 us: gather_call(): pl.pallas_call(functools.partial(gather_kernel, depth, cuts), out_shape=[...]
    unnamed x23 -> x0, waiting for transfers between devices: 285 us -> none
    dot_general x30 -> x0, matrix products: 196 us -> none  [the longest x3 37.7 us: one_group(): jnp.einsum('qhd,khd->hqk', block_grads, group_values, preferred_element_t...]
    reduce_scatter x3 -> x0, waiting for transfers between devices: 179 us -> none  [the longest x1 78.9 us: shards(): lax.psum_scatter(outer_grad, 'wide', scatter_dimension=1, tiled=True)]
    all_gather x6 -> x0, waiting for transfers between devices: 150 us -> none  [the longest x4 114 us: whole_features(): return lax.all_gather(values, 'narrow', axis=1, tiled=True)]
    all_gather x4 -> x1, blocking collectives: 86.4 us -> 3.83 us  [owned(): gains = lax.all_gather(gains, 'narrow', axis=1, tiled=True)]
    convert_element_type x8 -> x0, other arithmetic: 61.2 us -> none  [the longest x3 48.9 us: one_group(): scores_grad = (soft * (inner - centre)).astype(jnp.bfloat16)]
    reduce_sum x8 -> x1, other arithmetic: 41 us -> 0.91 us  [owned(): jnp.sum((block_segment[None, :] < block_segment[:, None]).astype(jnp.int3...]
  transfers between devices with their start and end apart: 16 -> 2, of which waited for: 13 -> 0; matrix products, arithmetic and copies ran while one was open for 5% -> 2% of each run, Pallas kernels for 0% -> 0%
where the time goes in v1:
time: 491 us; the launch traced here: 485 us
  Pallas kernels  366 us (75%)
  blocking collectives  42.3 us (9%)
  local copies, waits for them, and re-layouts  37.3 us (8%)
  matrix products  18.7 us (4%)
  other arithmetic  16.9 us (3%)
    pallas_call x1, Pallas kernels, gather_call(): pl.pallas_call(functools.partial(gather_kernel, depth, cuts), out_shape=[...  135 us
    pallas_call x1, Pallas kernels, scatter_call(): pl.pallas_call(functools.partial(scatter_kernel, depth, cuts), out_shape=...  108 us
    pallas_call x1, Pallas kernels, backward_call(): pl.pallas_call(backward_kernel, grid=(3 * SPAN,), out_shape=[jax.ShapeDty...  51.4 us
    pallas_call x1, Pallas kernels, forward_call(): pl.pallas_call(forward_kernel, grid=(SPAN + 3 * SPAN,), out_shape=[trio,...  40.2 us
    unnamed x1, blocking collectives  38.5 us
    pallas_call x1, Pallas kernels, middle_call(): pl.pallas_call(middle_kernel, grid=(half // tile,), out_shape=[low(2, hal...  31.6 us
    dot_general x6, matrix products, left_transposed(): lax.dot_general(left, right, (((0,), (0,)), ((), ())), preferred_element_...  18.7 us
    unnamed x57, local copies, waits for them, and re-layouts  13.1 us
  transfers between devices with their start and end apart: 2, of which 0 were waited for; matrix products, arithmetic and copies ran while one was open for 2% of the time, Pallas kernels for 0%

profile of v1, /device:TPU:1, one launch (start us, length us, event | category | flops | bytes accessed | tf_op | source)
XLA Modules:
  0.0 484.6 jit_solution(5889930318645894899)
XLA Ops:
  0.6 0.6 and_reduce_fusion
  1.3 0.9 convert_reduce_fusion
  2.2 1.3 fusion.5
  4.1 0.7 constant_dynamic-update-slice_fusion.8
  4.8 0.7 constant_dynamic-update-slice_fusion.7
  5.5 0.7 constant_dynamic-update-slice_fusion.6
  6.2 0.7 constant_dynamic-update-slice_fusion.5
  7.0 0.7 constant_dynamic-update-slice_fusion.4
  7.7 0.7 constant_dynamic-update-slice_fusion.3
  8.4 0.7 constant_dynamic-update-slice_fusion.2
  9.1 0.7 constant_dynamic-update-slice_fusion.1
  9.8 0.7 constant_dynamic-update-slice_fusion.q_own
  10.5 1.4 broadcast_select_fusion
  11.9 0.9 scatter.12.meta_in
  12.8 1.6 pad_maximum_fusion.4.m_own
  14.4 135.3 %gather.1 = (s32[1,128]{1,0:T(1,128)}, bf16[2,768,384]{2,1,0:T(8,128)(2,1)}, bf16[2,1536,384]{2,1,0:T(8,128)(2,1)}, bf16[2,4,2,2,48,1152]{5,4,3,2,1,0:T(8,128)(2...) custom-call(s32[1,128]{1,0:T(1,128)} %copy-done.15, bf16[1536,384]{1,0:T(8,128)(2,1)} %cot_in.1, ...), custom_call_target="tpu_custom_call" | custom-call | tf_op jit(solution)/shard_map/gather/pallas_call | solution.py:567
  149.7 2.8 constant_dynamic-slice_fusion.3
  152.6 40.2 %attend.1 = (bf16[3,1536,128]{2,1,0:T(8,128)(2,1)}, bf16[3,1536,128]{2,1,0:T(8,128)(2,1)}, bf16[3,1536,128]{2,1,0:T(8,128)(2,1)}, bf16[9,2,512,1536]{3,2,1,0:T(8...) custom-call(s32[1,128]{1,0:T(1,128)} %get-tuple-element.64.meta, ...), custom_call_target="tpu_custom_call" | custom-call | tf_op jit(solution)/shard_map/attend/pallas_call | solution.py:913
  192.8 2.3 dynamic-slice_bitcast_fusion.1
  195.9 3.8 all_gather.3.gains
  199.7 1.2 constant_dynamic-slice_fusion.1.rows
  200.9 1.3 copy.77
  202.5 1.3 maximum_select_fusion.context
  203.8 31.6 %middle.1 = (bf16[2,768,384]{2,1,0:T(8,128)(2,1)}, bf16[2,768,384]{2,1,0:T(8,128)(2,1)}, bf16[768,3072]{1,0:T(8,128)(2,1)}, bf16[768,3072]{1,0:T(8,128)(2,1)}, b...) custom-call(bf16[2,768,384]{2,1,0:T(8,128)(2,1)} %maximum_select_fus, ...), custom_call_target="tpu_custom_call" | custom-call | tf_op jit(solution)/shard_map/middle/pallas_call | solution.py:1035
  235.4 2.9 convolution_convert_fusion.5
  238.3 1.9 convolution_convert_fusion.4
  240.3 3.5 convolution_convert_fusion.1
  243.8 3.5 convolution_convert_fusion
  247.2 3.5 convolution_convert_fusion.3
  250.7 3.5 convolution_convert_fusion.2
  254.8 0.7 copy-done.5
  255.6 1.6 collective-permute-start.1
  257.8 38.5 %all-reduce.1 = f32[4,768]{1,0:T(4,128)S(1)} all-reduce(f32[4,768]{1,0:T(4,128)S(1)} %copy-done.10), channel_id=2, replica_groups=mesh['narrow'=2,'wide'=16] {'narrow','wide'}, use_global_device_ids=true, to_apply=%region_3.4.clone | all-reduce | flops 3072 | bytes 24576
  296.3 2.0 pad_maximum_fusion.2
  299.0 3.5 pad_maximum_fusion.m_part
  303.3 2.6 pad_maximum_fusion.1.o_part
  306.5 1.4 fusion.4.grads
  307.9 51.4 %attend_back.1 = (bf16[3,768,384]{2,1,0:T(8,128)(2,1)}, bf16[2,2,768,384]{3,2,1,0:T(8,128)(2,1)}) custom-call(s32[1]{0:T(128)} %bitcast.12.core, s32[1,128]{1,0:T(1,128)} %get-tuple-element.64.meta, f32[1024,128]{1,0:T(8,128)} %constant.83.clone.base, f32[8,128]{1,0:T(8,128)} %constant.84.clone.jump, bf16[9,2,512,1536]{3,2,1,0:T(8,128)(2,1)} %get-tuple-element.72.soft, ...), custom_call_target="tpu_custom_call" | custom-call | tf_op jit(solution)/shard_map/attend_back/pallas_call | solution.py:1153
  359.3 3.0 copy.90
  362.3 3.2 reshape.135.q_part
  365.4 107.8 %scatter.14 = (bf16[1536,384]{1,0:T(8,128)(2,1)}, bf16[1536,384]{1,0:T(8,128)(2,1)}, f32[48,1536]{1,0:T(8,128)}, f32[48,1920]{1,0:T(8,128)}, f32[48,1152]{1,0:T(8,128)}) custom-call(bf16[2,768,384]{2,1,0:T(8,128)(2,1)} %get-tuple-element.71.lo_in, bf16[2,2,768,384]{3,2,1,0:T(8,128)(2,1)} %get-tuple-element.79.dx_in, ...), custom_call_target="tpu_custom_call" | custom-call | tf_op jit(solution)/shard_map/scatter/pallas_call | solution.py:810
  473.3 1.8 slice.128
  475.1 1.5 slice_bitcast_fusion.4
  476.6 1.0 reshape.136
  478.2 0.6 copy.99
  480.2 2.4 copy.114
  482.6 1.0 copy.115
  483.6 0.7 copy.116
  (69 shorter events, 6.8 us)
Async XLA Ops:
  10.5 3.9 copy-start.9
  12.8 1.6 copy-start.15
  192.8 3.0 copy-start.11
  192.8 3.0 copy-start.12
  192.8 3.1 copy-start.13
  192.8 3.1 copy-start.14
  192.8 6.9 %copy-start = (bf16[2,1536,384]{2,1,0:T(8,128)(2,1)S(1)}, bf16[2,1536,384]{2,1,0:T(8,128)(2,1)}, u32[]{:S(2)}) copy-start(bf16[2,1536,384]{2,1,0:T(8,128)(2,1)} %get-tuple-element.65.rows) | copy-start | bytes 7077892
  195.1 5.8 %collective-permute-start = (bf16[3,768,128]{2,1,0:T(8,128)(2,1)}, bf16[3,768,128]{2,1,0:T(8,128)(2,1)}, u32[]{:S(2)}, u32[]{:S(2)}) collective-permute-start(bf16[3,768,128]{2,1,0:T(8,128)(2,1)} %get-tuple-element.98), channel_id=1, source_target_pairs={{0,1},{1,0},{2,3},{3,2},{4,5},{5,4},{6,7},{7,6},{8,9},{9,8},{10,11... | collective-permute-start | bytes 1769480 | tf_op jit(solution)/shard_map/ppermute | solution.py:1178
  203.7 31.6 %copy-start.1 = (bf16[2,768,384]{2,1,0:T(8,128)(2,1)S(1)}, bf16[2,768,384]{2,1,0:T(8,128)(2,1)}, u32[]{:S(2)}) copy-start(bf16[2,768,384]{2,1,0:T(8,128)(2,1)} %maximum_select_fusion.context) | copy-start | bytes 3538948
  235.4 4.9 %copy-start.16 = (bf16[768,3072]{1,0:T(8,128)(2,1)S(1)}, bf16[768,3072]{1,0:T(8,128)(2,1)}, u32[]{:S(2)}) copy-start(bf16[768,3072]{1,0:T(8,128)(2,1)} %get-tuple-element.84) | copy-start | bytes 14155780
  235.4 4.9 %copy-start.18 = (bf16[768,768]{1,0:T(8,128)(2,1)S(1)}, bf16[768,768]{1,0:T(8,128)(2,1)}, u32[]{:S(2)}) copy-start(bf16[768,768]{1,0:T(8,128)(2,1)} %get-tuple-element.83) | copy-start | bytes 3538948
  240.3 6.9 %slice-start = ((s8[4718592]{0:T(1024)(128)(4,1)}), s8[4194304]{0:T(1024)(128)(4,1)S(1)}, s32[]{:S(2)}) async-start(s8[4718592]{0:T(1024)(128)(4,1)} %bitcast.88), calls=%async_computation | async-start | bytes 8388608
  243.8 3.5 slice-start.1
  243.8 3.5 copy-start.17
  250.7 3.5 copy-start.7
  254.2 1.3 copy-start.5
  255.5 2.3 copy-start.10
  255.6 50.3 %collective-permute-start.1 = (bf16[768,384]{1,0:T(8,128)(2,1)S(1)}, bf16[768,384]{1,0:T(8,128)(2,1)S(1)}, u32[]{:S(2)}, u32[]{:S(2)}) collective-permute-start(bf16[768,384]{1,0:T(8,128)(2,1)S(1)} %get-tuple-element.96), channel_id=1, source_target_pairs={{0,1},{1,0},{2,3},{3,2},{4,5},{5,4},{6,7},{7,6},{8,9},{9,8},{10,11... | collective-permute-start | bytes 1769480 | tf_op jit(solution)/shard_map/ppermute | solution.py:1187
  296.3 2.4 copy-start.4
  298.9 4.1 copy-start.2
  298.9 4.4 copy-start.3
  473.3 9.3 %copy-start.6 = (bf16[1536,384]{1,0:T(8,128)(2,1)S(1)}, bf16[1536,384]{1,0:T(8,128)(2,1)}, u32[]{:S(2)}) copy-start(bf16[1536,384]{1,0:T(8,128)(2,1)} %get-tuple-element.118) | copy-start | bytes 3538948
  480.2 3.5 copy-start.8

commit v2 on v1

--- a/solution.py
+++ b/solution.py
@@ -403,187 +403,179 @@
         self.whole, self.local = whole, local
         self.send = lambda k: send.at[index, k]
         self.recv = lambda k: recv.at[index, k]
-        self.sent = []
         self.width = own.shape[-1]
 
     def slot(self, h, q, y):
         return self.full.at[h, q, y, self.links.c]
 
-    def go(self, source, mark, device):
-        copy = remote(source, source, self.send(mark), self.recv(mark), device)
-        copy.start()
-        self.sent.append(copy)
-
-    def arrived(self, target, mark):
-        remote(target, target, self.send(mark), self.recv(mark), self.links.sibling).wait_recv()
-
-    def begin(self):
+    def low(self, ref):
+        return ref.at[:, pl.ds(0, self.cut)]
+
+    def high(self, ref):
+        return ref.at[:, pl.ds(self.cut, self.width - self.cut)]
+
+    def copy(self, kind, step=0):
         n, d = self.links, self.links.depth
         mine = self.slot(n.x, n.q, n.y)
-        for step in range(1, d):
-            copy = remote(self.own, mine, self.send(step - 1), self.recv(step - 1), n.far(step))
-            copy.start()
-            self.sent.append(copy)
-        for mark, device in ((d, n.across), (2 * d, n.beside)):
-            copy = remote(self.own, mine, self.send(mark), self.recv(mark), device)
-            copy.start()
-            self.sent.append(copy)
-        self.keep = pltpu.make_async_copy(self.own, mine, self.local)
-        self.keep.start()
+        column = self.slot(n.x, n.row(step), n.y)
+        first = self.own if step == 0 else column
+        if kind == "far":
+            return self.move(self.own, mine, step - 1, n.far(step))
+        if kind == "across":
+            return self.move(first, column, d + step, n.across)
+        if kind == "beside":
+            return self.move(first, column, 2 * d + step, n.beside)
+        if kind == "high":
+            part = self.high(self.slot(1 - n.x, n.row(step), n.y))
+            return self.move(part, part, 3 * d + step, n.beside)
+        if kind == "low":
+            part = self.low(self.slot(n.x, n.row(step), 1 - n.y))
+            return self.move(part, part, 4 * d + step, n.across)
+        part = self.full.at[step if self.whole else 1 - n.c, :, :, n.c]
+        return self.move(part, part, 5 * d + step, n.sibling)
+
+    def move(self, source, target, mark, device):
+        return remote(source, target, self.send(mark), self.recv(mark), device)
+
+    def arrived(self, target, mark):
+        self.move(target, target, mark, self.links.sibling).wait_recv()
+
+    def keep(self):
+        n = self.links
+        return pltpu.make_async_copy(self.own, self.slot(n.x, n.q, n.y), self.local)
+
+    def begin(self):
+        self.keep().start()
+        self.copy("across").start()
+        self.copy("beside").start()
+        for step in range(1, self.links.depth):
+            self.copy("far", step).start()
 
     def second(self, step):
-        n, d = self.links, self.links.depth
-        got = self.slot(n.x, n.row(step), n.y)
-        self.arrived(got, step - 1)
-        self.go(got, d + step, n.across)
-        self.go(got, 2 * d + step, n.beside)
+        n = self.links
+        self.arrived(self.slot(n.x, n.row(step), n.y), step - 1)
+        self.copy("across", step).start()
+        self.copy("beside", step).start()
 
     def third(self, step):
         n, d = self.links, self.links.depth
-        got = self.slot(1 - n.x, n.row(step), n.y)
-        self.arrived(got, d + step)
-        part = got.at[:, pl.ds(self.cut, self.width - self.cut)]
-        self.go(part, 3 * d + step, n.beside)
-        got = self.slot(n.x, n.row(step), 1 - n.y)
-        self.arrived(got, 2 * d + step)
-        part = got.at[:, pl.ds(0, self.cut)]
-        self.go(part, 4 * d + step, n.across)
+        self.arrived(self.slot(1 - n.x, n.row(step), n.y), d + step)
+        self.copy("high", step).start()
+        self.arrived(self.slot(n.x, n.row(step), 1 - n.y), 2 * d + step)
+        self.copy("low", step).start()
 
     def fourth(self):
         n, d = self.links, self.links.depth
         for step in range(d):
             got = self.slot(1 - n.x, n.row(step), 1 - n.y)
-            self.arrived(got.at[:, pl.ds(self.cut, self.width - self.cut)], 3 * d + step)
-            self.arrived(got.at[:, pl.ds(0, self.cut)], 4 * d + step)
-        self.keep.wait()
-        if self.whole:
-            for h in range(2):
-                self.go(self.full.at[h, :, :, n.c], 5 * d + h, n.sibling)
-        else:
-            self.go(self.full.at[1 - n.c, :, :, n.c], 5 * d, n.sibling)
+            self.arrived(self.high(got), 3 * d + step)
+            self.arrived(self.low(got), 4 * d + step)
+        self.keep().wait()
+        for h in range(2 if self.whole else 1):
+            self.copy("sibling", h).start()
 
     def finish(self):
         n, d = self.links, self.links.depth
-        if self.whole:
-            for h in range(2):
-                self.arrived(self.full.at[h, :, :, 1 - n.c], 5 * d + h)
-        else:
-            self.arrived(self.full.at[n.c, :, :, 1 - n.c], 5 * d)
+        for h in range(2 if self.whole else 1):
+            self.arrived(self.full.at[h if self.whole else n.c, :, :, 1 - n.c], 5 * d + h)
 
     def close(self):
-        for copy in self.sent:
-            copy.wait_send()
-
-
-def gather_kernel(depth, cuts, meta_in, cot_in, in_ref, q_own, m_own, o_own,
-                  meta, cot, rows, q_full, m_full, o_full, send, recv, local, extra_send, extra_recv):
-    n = Links(depth)
-    n.meet()
-    half = in_ref.shape[0] // 2
-    home = n.x == n.c
-    gathers = [
-        Gather(n, own, full, cut, whole, send, recv, k, local.at[k])
-        for k, (own, full, cut, whole) in enumerate(
-            zip((q_own, m_own, o_own), (q_full, m_full, o_full), cuts, (False, True, True))
-        )
-    ]
-    es = lambda k: extra_send.at[k]
-    er = lambda k: extra_recv.at[k]
-
-    @pl.when(jnp.logical_not(home))
-    def _():
-        remote(in_ref, rows.at[n.x], es(0), er(0), n.across).start()
-
-    gathers[0].begin()
-
-    @pl.when(home)
-    def _():
-        keep = pltpu.make_async_copy(in_ref, rows.at[n.x], local.at[3])
-        keep.start()
-        first = remote(in_ref, rows.at[n.x], es(1), er(1), n.sibling)
-        first.start()
-        note = remote(meta_in, meta, es(3), er(3), n.sibling)
-        note.start()
-        own = pltpu.make_async_copy(meta_in, meta, local.at[4])
-        own.start()
-        mine = pltpu.make_async_copy(cot_in.at[pl.ds(n.c * half, half)], cot.at[n.x], local.at[5])
-        mine.start()
-        theirs = remote(
-            cot_in.at[pl.ds((1 - n.c) * half, half)], cot.at[n.x], es(4), er(4), n.sibling
-        )
-        theirs.start()
-        remote(in_ref, rows.at[1 - n.x], es(0), er(0), n.across).wait_recv()
-        second = remote(rows.at[1 - n.x], rows.at[1 - n.x], es(2), er(2), n.sibling)
-        second.start()
-        keep.wait()
-        own.wait()
-        mine.wait()
-        first.wait_send()
-        note.wait_send()
-        theirs.wait_send()
-        second.wait_send()
-
-    @pl.when(jnp.logical_not(home))
-    def _():
-        remote(in_ref, rows.at[n.x], es(0), er(0), n.across).wait_send()
-        one = remote(
-            cot_in.at[pl.ds((1 - n.c) * half, half)], cot.at[n.x], es(6), er(6), n.corner
-        )
-        two = remote(cot_in.at[pl.ds(n.c * half, half)], cot.at[n.x], es(5), er(5), n.across)
-        one.start()
-        two.start()
-        remote(in_ref, rows.at[n.x], es(1), er(1), n.sibling).wait_recv()
-        remote(in_ref, rows.at[1 - n.x], es(2), er(2), n.sibling).wait_recv()
-        remote(meta_in, meta, es(3), er(3), n.sibling).wait_recv()
-        remote(cot_in.at[pl.ds(0, half)], cot.at[n.x], es(4), er(4), n.sibling).wait_recv()
-        one.wait_send()
-        two.wait_send()
-
-    for k in (0, 1, 2):
-        if k:
-            gathers[k].begin()
-        for step in range(1, depth):
-            gathers[k].second(step)
-        for step in range(depth):
-            gathers[k].third(step)
-        gathers[k].fourth()
-
-    @pl.when(home)
-    def _():
-        remote(cot_in.at[pl.ds(0, half)], cot.at[1 - n.x], es(5), er(5), n.across).wait_recv()
-
-    @pl.when(jnp.logical_not(home))
-    def _():
-        remote(cot_in.at[pl.ds(0, half)], cot.at[1 - n.x], es(6), er(6), n.corner).wait_recv()
-
-    for k in (0, 1, 2):
-        gathers[k].finish()
-        gathers[k].close()
-
-
-def gather_call(depth, cuts, meta, cot, rows, q_own, m_own, o_own):
-    r = q_own.shape[0]
-    shapes = [jax.ShapeDtypeStruct((2, depth, 2, 2) + own.shape, LOW) for own in (q_own, m_own, o_own)]
-    return pl.pallas_call(
-        functools.partial(gather_kernel, depth, cuts),
-        out_shape=[
-            jax.ShapeDtypeStruct(meta.shape, meta.dtype),
-            jax.ShapeDtypeStruct((2, cot.shape[0] // 2, cot.shape[1]), LOW),
-            jax.ShapeDtypeStruct((2,) + rows.shape, LOW),
+        d = self.links.depth
+        for step in range(d):
+            if step:
+                self.copy("far", step).wait_send()
+            for kind in ("across", "beside", "high", "low"):
+                self.copy(kind, step).wait_send()
+        for h in range(2 if self.whole else 1):
+            self.copy("sibling", h).wait_send()
+
+
+class Share:
+    def __init__(self, links, in_ref, rows, cot_in, cot, note_in, note, gain_in, gain, send, recv, local):
+        n = self.links = links
+        half = cot_in.shape[0] // 2
+        self.home = n.x == n.c
+        s, r = (lambda k: send.at[k]), (lambda k: recv.at[k])
+        mine, theirs = pl.ds(n.c * half, half), pl.ds((1 - n.c) * half, half)
+        near, far = rows.at[n.x], rows.at[1 - n.x]
+        self.rows_across = lambda: remote(in_ref, near, s(0), r(0), n.across)
+        self.rows_beside = lambda: remote(in_ref, near, s(1), r(1), n.sibling)
+        self.rows_further = lambda: remote(far, far, s(2), r(2), n.sibling)
+        self.note = lambda: remote(note_in, note, s(3), r(3), n.sibling)
+        self.cot_beside = lambda: remote(cot_in.at[theirs], cot.at[n.x], s(4), r(4), n.sibling)
+        self.cot_across = lambda: remote(cot_in.at[mine], cot.at[n.x], s(5), r(5), n.across)
+        self.cot_corner = lambda: remote(cot_in.at[theirs], cot.at[n.x], s(6), r(6), n.corner)
+        self.gain = lambda: remote(gain_in, gain.at[n.x], s(7), r(7), n.across)
+        self.keep = lambda: [
+            pltpu.make_async_copy(gain_in, gain.at[n.x], local.at[0]),
         ]
-        + shapes,
-        in_specs=[ANY] * 6,
-        out_specs=[ANY] * 6,
-        scratch_shapes=[
-            pltpu.SemaphoreType.DMA((3, gather_marks(depth))),
-            pltpu.SemaphoreType.DMA((3, gather_marks(depth))),
-            pltpu.SemaphoreType.DMA((6,)),
-            pltpu.SemaphoreType.DMA((7,)),
-            pltpu.SemaphoreType.DMA((7,)),
-        ],
-        compiler_params=pltpu.CompilerParams(collective_id=0, has_side_effects=True),
-        name="gather",
-    )(meta, cot, rows, q_own, m_own, o_own)
+        self.keep_home = lambda: [
+            pltpu.make_async_copy(in_ref, near, local.at[1]),
+            pltpu.make_async_copy(note_in, note, local.at[2]),
+            pltpu.make_async_copy(cot_in.at[mine], cot.at[n.x], local.at[3]),
+        ]
+
+    def begin(self):
+        @pl.when(self.home)
+        def _():
+            self.note().start()
+            self.rows_beside().start()
+            for item in self.keep_home():
+                item.start()
+
+        @pl.when(jnp.logical_not(self.home))
+        def _():
+            self.rows_across().start()
+
+        self.gain().start()
+        for item in self.keep():
+            item.start()
+
+    def further(self):
+        @pl.when(self.home)
+        def _():
+            self.rows_across().wait_recv()
+            self.rows_further().start()
+            for item in self.keep_home():
+                item.wait()
+
+        @pl.when(jnp.logical_not(self.home))
+        def _():
+            self.note().wait_recv()
+            self.rows_beside().wait_recv()
+            self.rows_further().wait_recv()
+
+        for item in self.keep():
+            item.wait()
+
+    def later(self):
+        @pl.when(self.home)
+        def _():
+            self.cot_beside().start()
+
+        @pl.when(jnp.logical_not(self.home))
+        def _():
+            self.cot_across().start()
+            self.cot_corner().start()
+
+    def finish(self):
+        self.gain().wait()
+
+        @pl.when(self.home)
+        def _():
+            self.note().wait_send()
+            self.rows_beside().wait_send()
+            self.rows_further().wait_send()
+            self.cot_beside().wait_send()
+            self.cot_across().wait_recv()
+
+        @pl.when(jnp.logical_not(self.home))
+        def _():
+            self.rows_across().wait_send()
+            self.cot_across().wait_send()
+            self.cot_corner().wait_send()
+            self.cot_beside().wait_recv()
+            self.cot_corner().wait_recv()
 
 
 def plus(left, right):
@@ -860,15 +852,91 @@
     return values * cosine + swapped * sine
 
 
-def forward_kernel(meta, rows, weight, base, jump, q_ref, k_ref, v_ref, p_ref, r_ref, c_ref, marks):
+def weight_loads(full, h, flat, marks):
+    depth, r = full.shape[1], full.shape[4]
+    return [
+        pltpu.make_async_copy(
+            full.at[h, q, y, c], flat.at[pl.ds(k * r, r)], marks.at[k]
+        )
+        for k, (q, y, c) in enumerate(
+            (q, y, c) for q in range(depth) for y in range(2) for c in range(2)
+        )
+    ]
+
+
+def forward_kernel(depth, cuts, note_in, gain_in, cot_in, in_ref, q_own, m_own, o_own, base, jump,
+                   note, gain, cot, rows, q_full, m_full, o_full, all_context, q_ref, k_ref, v_ref,
+                   p_ref, r_ref, c_ref, marks, meta, held, weight, piece, send, recv, local, extra_send,
+                   extra_recv, context_send, context_recv):
     step = pl.program_id(0)
     scale = HEAD_DIM ** (-0.5)
+    n = Links(depth)
+    half = in_ref.shape[0] // 2
+    gathers = [
+        Gather(n, own, full, cut, whole, send, recv, k, local.at[k])
+        for k, (own, full, cut, whole) in enumerate(
+            zip((q_own, m_own, o_own), (q_full, m_full, o_full), cuts, (False, True, True))
+        )
+    ]
+    share = Share(
+        n, in_ref, rows, cot_in, cot, note_in, note, gain_in, gain, extra_send, extra_recv,
+        local.at[pl.ds(3, 4)],
+    )
+
+    def context_copy(p):
+        there = c_ref.at[p, pl.ds((1 - n.c) * half, half)]
+        return remote(there, all_context.at[n.c, p], context_send.at[p], context_recv.at[p], n.sibling)
+
+    def context_keep(p):
+        here = c_ref.at[p, pl.ds(n.c * half, half)]
+        return pltpu.make_async_copy(here, all_context.at[n.c, p], local.at[10 + p])
+
+    @pl.when(step == 0)
+    def _():
+        n.meet()
+        share.begin()
+        gathers[0].begin()
+        for k in range(1, depth):
+            gathers[0].second(k)
+        for k in range(depth):
+            gathers[0].third(k)
+        gathers[1].begin()
+        share.further()
+        loads = [
+            pltpu.make_async_copy(rows, held, local.at[7]),
+            pltpu.make_async_copy(note, meta, local.at[8]),
+        ]
+        for item in loads:
+            item.start()
+        gathers[0].fourth()
+        gathers[0].finish()
+        loads += weight_loads(q_full, n.c, weight, piece)
+        for item in loads[2:]:
+            item.start()
+        for item in loads:
+            item.wait()
+
+    hooks = {
+        1: [gathers[2].begin],
+        2: [functools.partial(gathers[1].second, k) for k in range(1, depth)],
+        5: [functools.partial(gathers[1].third, k) for k in range(depth)],
+        6: [functools.partial(gathers[2].second, k) for k in range(1, depth)] + [share.later],
+        8: [gathers[1].fourth],
+        9: [functools.partial(gathers[2].third, k) for k in range(depth)],
+    }
+    for at, actions in hooks.items():
+
+        @pl.when(step == at)
+        def _():
+            for action in actions:
+                action()
 
     @pl.when(step < SPAN)
     def _():
         here = pl.ds(step * BLOCK, BLOCK)
         cosine, sine, low = turn_parts(meta, base, jump, step)
-        values = jnp.concatenate([rows[0, here], rows[1, here]], axis=1)
+        values = jnp.concatenate([held[0, here], held[1, here]], axis=1)
+
         for p in range(3):
             made = contract(values, weight[:, p * 384 : p * 384 + 384], 1, 0)
             q_ref[p, here] = (turn(made[:, 0:128], cosine, sine, low) * scale).astype(LOW)
@@ -904,36 +972,81 @@
         r_ref[p, here] = inverse
         c_ref[p, here] = (jnp.where(lane < HEAD_DIM, outs[0], outs[1]) * inverse).astype(LOW)
 
-
-def forward_call(meta, rows, weight, base, jump):
-    length = rows.shape[1]
-    trio = jax.ShapeDtypeStruct((3, length, 128), LOW)
+    for p in range(3):
+
+        @pl.when(step == 2 * SPAN - 1 + p * SPAN)
+        def _():
+            context_copy(p).start()
+            context_keep(p).start()
+
+    @pl.when(step == 4 * SPAN - 1)
+    def _():
+        gathers[2].fourth()
+        gathers[1].finish()
+        gathers[2].finish()
+        for item in gathers:
+            item.close()
+        share.finish()
+        for p in range(3):
+            context_copy(p).wait()
+            context_keep(p).wait()
+
+
+def forward_call(depth, cuts, note, gain, cot, rows, q_own, m_own, o_own, base, jump):
+    length, part = rows.shape
+    half = length // 2
+    r = q_own.shape[0]
+    low = lambda *shape: jax.ShapeDtypeStruct(shape, LOW)
+    full = [low(2, depth, 2, 2, r, own.shape[1]) for own in (q_own, m_own, o_own)]
+    trio = low(3, length, 128)
     vmem = pl.BlockSpec(memory_space=pltpu.VMEM)
-    soft_shape = (SPAN * 3, 2, BLOCK, length)
+    marks = pltpu.SemaphoreType.DMA((3, gather_marks(depth)))
     return pl.pallas_call(
-        forward_kernel,
+        functools.partial(forward_kernel, depth, cuts),
         grid=(SPAN + 3 * SPAN,),
         out_shape=[
+            jax.ShapeDtypeStruct(note.shape, note.dtype),
+            jax.ShapeDtypeStruct((2,) + gain.shape, WIDE),
+            low(2, half, part),
+            low(2, length, part),
+        ]
+        + full
+        + [
+            low(2, 3, half, 128),
             trio,
             trio,
             trio,
-            jax.ShapeDtypeStruct(soft_shape, LOW),
+            low(SPAN * 3, 2, BLOCK, length),
             jax.ShapeDtypeStruct((3, length, 128), WIDE),
             trio,
         ],
-        in_specs=[pl.BlockSpec(memory_space=pltpu.SMEM)] + [vmem] * 4,
-        out_specs=[
-            vmem,
-            vmem,
-            vmem,
+        in_specs=[ANY] * 7 + [vmem] * 2,
+        out_specs=[ANY] * 8
+        + [vmem] * 3
+        + [
             pl.BlockSpec((1, 2, BLOCK, length), lambda s: (jnp.maximum(s - SPAN, 0), 0, 0, 0)),
             vmem,
             vmem,
         ],
-        scratch_shapes=[pltpu.VMEM((length, 128), LOW)],
-        compiler_params=pltpu.CompilerParams(vmem_limit_bytes=60 * MEGA),
+        scratch_shapes=[
+            pltpu.VMEM((length, 128), LOW),
+            pltpu.SMEM(note.shape, note.dtype),
+            pltpu.VMEM((2, length, part), LOW),
+            pltpu.VMEM((4 * depth * r, q_own.shape[1]), LOW),
+            pltpu.SemaphoreType.DMA((4 * depth,)),
+            marks,
+            marks,
+            pltpu.SemaphoreType.DMA((13,)),
+            pltpu.SemaphoreType.DMA((8,)),
+            pltpu.SemaphoreType.DMA((8,)),
+            pltpu.SemaphoreType.DMA((3,)),
+            pltpu.SemaphoreType.DMA((3,)),
+        ],
+        compiler_params=pltpu.CompilerParams(
+            collective_id=0, has_side_effects=True, vmem_limit_bytes=60 * MEGA
+        ),
         name="attend",
-    )(meta, rows, weight, base, jump)
+    )(note, gain, cot, rows, q_own, m_own, o_own, base, jump)
 
 
 def norm_of(summed):
@@ -958,10 +1071,12 @@
     tile = rows.shape[1]
     part = rows.shape[2]
     pieces = o_full.shape[2] // HIDDEN
-    gain1, bias1, gain2, bias2 = (gains[k : k + 1, :] for k in range(4))
+    whole = jnp.concatenate([gains[0], gains[1]], axis=1)
+    gain1, bias1, gain2, bias2 = (whole[k : k + 1, :] for k in range(4))
     summed = jnp.concatenate([rows[0], rows[1]], axis=1).astype(WIDE)
     for h in range(2):
-        summed = summed + contract(context[h], m_full[h, :, 0:part], 1, 1)
+        seen = jnp.concatenate([context[h, p] for p in range(3)], axis=1)
+        summed = summed + contract(seen, m_full[h, :, 0:part], 1, 1)
     normed1, scale1 = norm_of(summed)
     first = normed1 * gain1 + bias1
     first_low = first.astype(LOW)
@@ -1046,7 +1161,14 @@
             jax.ShapeDtypeStruct((half, width), WIDE),
             jax.ShapeDtypeStruct((4, width), WIDE),
         ],
-        in_specs=[split, split, split, vmem, vmem, vmem],
+        in_specs=[
+            pl.BlockSpec((2, 3, tile, 128), lambda i: (0, 0, i, 0)),
+            split,
+            split,
+            vmem,
+            vmem,
+            vmem,
+        ],
         out_specs=[
             split,
             split,
@@ -1169,15 +1291,6 @@
         compiler_params=pltpu.CompilerParams(vmem_limit_bytes=60 * MEGA),
         name="attend_back",
     )(core, meta, base, jump, soft, grads, context, inverse, q, k, v, rows, weight, kept)
-
-
-def swap_halves(values, half, c):
-    mine = lax.dynamic_slice_in_dim(values, c * half, half, axis=1)
-    theirs = lax.dynamic_slice_in_dim(values, (1 - c) * half, half, axis=1)
-    n_wide = lax.axis_size("wide")
-    got = lax.ppermute(theirs, "wide", [(w, w ^ 1) for w in range(n_wide)])
-    mine, got = (jnp.moveaxis(item, 0, 1).reshape(half, -1) for item in (mine, got))
-    return jnp.where(c == 0, jnp.stack([mine, got]), jnp.stack([got, mine]))
 
 
 def swap_back(values, half, c):
@@ -1227,22 +1340,23 @@
     meta = jnp.zeros((1, 128), jnp.int32)
     meta = meta.at[0, 0:SPAN].set(block_segment).at[0, SPAN : 2 * SPAN].set(offsets)
     widths = [item.shape[1] for item in (q_own, m_own, o_own)]
-    cuts = [(item // 128 // 2) * 128 for item in widths]
-    meta, cot, rows, q_full, m_full, o_full = gather_call(
-        depth, cuts, meta, output_cotangent, inputs, q_own, m_own, o_own
-    )
+    cuts = [(item // 128 // 5) * 128 for item in widths]
     gains = jnp.stack([first_gain, first_bias, second_gain, second_bias])
-    gains = lax.all_gather(gains, "narrow", axis=1, tiled=True)
+    gains = jnp.concatenate([gains, gains], axis=0)
+    base, jump = angle_tables()
+    meta, gains, cot, rows, q_full, m_full, o_full, pairs_context, q, k, v, soft, inverse, context = (
+        forward_call(
+            depth, cuts, meta, gains, output_cotangent, inputs, q_own, m_own, o_own, base, jump
+        )
+    )
     weight = lax.dynamic_index_in_dim(q_full, c, 0, keepdims=False).reshape(2 * part, widths[0])
     m_full = m_full.reshape(2, 2 * part, widths[1])
     o_full = o_full.reshape(2, 2 * part, widths[2])
-    base, jump = angle_tables()
-    q, k, v, soft, inverse, context = forward_call(meta, rows, weight, base, jump)
-    all_context = swap_halves(context, half, c)
     own_rows = lax.dynamic_slice_in_dim(rows, c * half, half, axis=1)
     lo, gc, act, gi, fl, gm, ga, kept, sums = middle_call(
-        all_context, own_rows, cot, m_full, o_full, gains
-    )
+        pairs_context, own_rows, cot, m_full, o_full, gains
+    )
+    all_context = jnp.moveaxis(pairs_context, 1, 2).reshape(2, half, part)
     hidden = act.shape[1] // 2
     o_part = jnp.stack(
         [left_transposed(gm, act[:, h * hidden : (h + 1) * hidden]).astype(LOW) for h in range(2)]

time: 491 us -> 434 us (0.88)
  Pallas kernels: 366 us -> 312 us
  blocking collectives: 42.3 us -> 37.3 us
    pallas_call x2 -> x1, Pallas kernels: 175 us -> 130 us  [forward_call(): pl.pallas_call(functools.partial(forward_kernel, depth, cuts), grid=(SPAN...]
    pallas_call x1, Pallas kernels: 108 us -> 98.5 us  [scatter_call(): pl.pallas_call(functools.partial(scatter_kernel, depth, cuts), out_shape=...]
    unnamed x57 -> x45, local copies, waits for them, and re-layouts: 13.1 us -> 13.4 us
  transfers between devices with their start and end apart: 2 -> 1, of which waited for: 0 -> 0; matrix products, arithmetic and copies ran while one was open for 2% -> 8% of each run, Pallas kernels for 0% -> 0%
where the time goes in v2:
time: 434 us; the launch traced here: 426 us
  Pallas kernels  312 us (72%)
  local copies, waits for them, and re-layouts  40.4 us (9%)
  blocking collectives  37.3 us (9%)
  matrix products  18.3 us (4%)
  other arithmetic  15.9 us (4%)
    pallas_call x1, Pallas kernels, forward_call(): pl.pallas_call(functools.partial(forward_kernel, depth, cuts), grid=(SPAN...  130 us
    pallas_call x1, Pallas kernels, scatter_call(): pl.pallas_call(functools.partial(scatter_kernel, depth, cuts), out_shape=...  98.5 us
    pallas_call x1, Pallas kernels, backward_call(): pl.pallas_call(backward_kernel, grid=(3 * SPAN,), out_shape=[jax.ShapeDty...  51.4 us
    unnamed x1, blocking collectives  37.3 us
    pallas_call x1, Pallas kernels, middle_call(): pl.pallas_call(middle_kernel, grid=(half // tile,), out_shape=[low(2, hal...  32.1 us
    dot_general x6, matrix products, left_transposed(): lax.dot_general(left, right, (((0,), (0,)), ((), ())), preferred_element_...  18.3 us
    unnamed x45, local copies, waits for them, and re-layouts  13.4 us
  transfers between devices with their start and end apart: 1, of which 0 were waited for; matrix products, arithmetic and copies ran while one was open for 8% of the time, Pallas kernels for 0%

profile of v2, /device:TPU:1, one launch (start us, length us, event | category | flops | bytes accessed | tf_op | source)
XLA Modules:
  0.0 425.8 jit_solution(5864663137036391647)
XLA Ops:
  0.7 0.6 and_reduce_fusion
  1.3 0.9 convert_reduce_fusion
  2.8 1.3 fusion.5
  4.1 0.7 stack.31
  4.8 0.7 stack.32
  5.5 0.7 stack.33
  6.2 0.7 stack.34
  6.8 0.7 constant_dynamic-update-slice_fusion.8
  7.6 0.7 constant_dynamic-update-slice_fusion.7
  8.3 0.7 constant_dynamic-update-slice_fusion.6
  9.0 0.7 constant_dynamic-update-slice_fusion.5
  9.7 0.7 constant_dynamic-update-slice_fusion.4
  10.4 0.7 constant_dynamic-update-slice_fusion.3
  11.1 0.7 constant_dynamic-update-slice_fusion.2
  11.8 0.7 constant_dynamic-update-slice_fusion.1
  12.6 0.7 constant_dynamic-update-slice_fusion.q_own
  13.3 1.4 broadcast_select_fusion
  14.6 0.9 scatter.12.note_in
  15.5 1.6 pad_maximum_fusion.4.m_own
  17.8 130.3 %attend.1 = (s32[1,128]{1,0:T(1,128)}, f32[2,8,384]{2,1,0:T(8,128)}, bf16[2,768,384]{2,1,0:T(8,128)(2,1)}, bf16[2,1536,384]{2,1,0:T(8,128)(2,1)}, bf16[2,4,2,2,4...) custom-call(s32[1,128]{1,0:T(1,128)} %copy-done.7, ...), custom_call_target="tpu_custom_call" | custom-call | tf_op jit(solution)/shard_map/attend/pallas_call | solution.py:1004
  148.1 2.4 constant_dynamic-slice_fusion.2.rows
  150.5 32.1 %middle.1 = (bf16[2,768,384]{2,1,0:T(8,128)(2,1)}, bf16[2,768,384]{2,1,0:T(8,128)(2,1)}, bf16[768,3072]{1,0:T(8,128)(2,1)}, bf16[768,3072]{1,0:T(8,128)(2,1)}, b...) custom-call(bf16[2,3,768,128]{3,2,1,0:T(8,128)(2,1)} %get-tuple-elem, ...), custom_call_target="tpu_custom_call" | custom-call | tf_op jit(solution)/shard_map/middle/pallas_call | solution.py:1150
  182.7 2.3 constant_dynamic-slice_fusion.1
  185.4 5.4 %convolution_convert_fusion.2 = bf16[768,1536]{1,0:T(8,128)(2,1)} fusion(bf16[768,768]{1,0:T(8,128)(2,1)S(1)} %copy-done.11, bf16[768,3072]{1,0:T(8,128)(2,1)} %get-tuple-element.85), kind=kOutput, calls=%fused_computation.4 | convolution fusion | flops 1813118976 | bytes 5898240 | tf_op jit(solution)/shard_map/dot_general | solution.py:28
  190.8 3.5 convolution_convert_fusion.3
  194.3 3.4 convolution_convert_fusion
  197.7 3.5 convolution_convert_fusion.1
  201.8 2.9 constant_dynamic-slice_fusion
  205.6 1.9 convolution_convert_fusion.4
  207.9 37.3 %all-reduce.1 = f32[4,768]{1,0:T(4,128)S(1)} all-reduce(f32[4,768]{1,0:T(4,128)S(1)} %copy-done.6), channel_id=2, replica_groups=mesh['narrow'=2,'wide'=16] {'narrow','wide'}, use_global_device_ids=true, to_apply=%region_3.4.clone | all-reduce | flops 3072 | bytes 24576
  245.8 5.2 %pad_maximum_fusion.1.o_part = bf16[2,4,2,2,48,1536]{5,4,3,2,1,0:T(8,128)(2,1)} fusion(bf16[1,4,2,2,48,1536]{5,4,3,2,1,0:T(8,128)(2,1)} %bitcast.68, bf16[1,4,2,2,48,1536]{5,4,3,2,1,0:T(8,128)(2,1)} %bitcast.69), kind=kLoop, calls=%fused_computation.1 | loop fusion | flops 2359296 | bytes 9437184 | tf_op jit(solution)/shard_map/stack | solution.py:1361
  251.2 1.4 copy-done.1
  253.4 3.1 pad_maximum_fusion.m_part
  257.0 1.3 fusion.4.grads
  258.4 51.4 %attend_back.1 = (bf16[3,768,384]{2,1,0:T(8,128)(2,1)}, bf16[2,2,768,384]{3,2,1,0:T(8,128)(2,1)}) custom-call(s32[1]{0:T(128)} %bitcast.7.core, s32[1,128]{1,0:T(1,128)} %get-tuple-element.73.meta, f32[1024,128]{1,0:T(8,128)} %constant.83.clone.base, f32[8,128]{1,0:T(8,128)} %constant.84.clone.jump, bf16[9,2,512,1536]{3,2,1,0:T(8,128)(2,1)} %get-tuple-element.74.soft, ...), custom_call_target="tpu_custom_call" | custom-call | tf_op jit(solution)/shard_map/attend_back/pallas_call | solution.py:1275
  309.8 3.0 copy.72
  312.8 3.2 reshape.140.q_part
  316.0 98.5 %scatter.14 = (bf16[1536,384]{1,0:T(8,128)(2,1)}, bf16[1536,384]{1,0:T(8,128)(2,1)}, f32[48,1536]{1,0:T(8,128)}, f32[48,1920]{1,0:T(8,128)}, f32[48,1152]{1,0:T(8,128)}) custom-call(bf16[2,768,384]{2,1,0:T(8,128)(2,1)} %get-tuple-element.72.lo_in, bf16[2,2,768,384]{3,2,1,0:T(8,128)(2,1)} %get-tuple-element.83.dx_in, ...), custom_call_target="tpu_custom_call" | custom-call | tf_op jit(solution)/shard_map/scatter/pallas_call | solution.py:802
  414.5 1.6 slice_bitcast_fusion
  416.1 1.7 slice.130
  417.8 1.0 reshape.141
  418.8 0.6 slice_reduce_fusion
  419.5 0.6 copy.81
  420.1 0.6 copy.82
  420.7 0.6 copy.83
  421.4 2.4 copy.96
  423.8 1.0 copy.97
  424.9 0.7 copy.98
  (50 shorter events, 5.7 us)
Async XLA Ops:
  13.3 4.5 %copy-start.5 = (bf16[48,1152]{1,0:T(8,128)(2,1)}, bf16[48,1152]{1,0:T(8,128)(2,1)S(1)}, u32[]{:S(2)}) copy-start(bf16[48,1152]{1,0:T(8,128)(2,1)S(1)} %constant_dynamic-update-slice_fusion.q_own) | copy-start | bytes 331780
  15.5 2.2 copy-start.7
  182.6 2.8 copy-start.11
  184.9 71.6 %collective-permute-start = (bf16[768,384]{1,0:T(8,128)(2,1)}, bf16[768,384]{1,0:T(8,128)(2,1)S(1)}, u32[]{:S(2)}, u32[]{:S(2)}) collective-permute-start(bf16[768,384]{1,0:T(8,128)(2,1)} %get-tuple-element.102), channel_id=1, source_target_pairs={{0,1},{1,0},{2,3},{3,2},{4,5},{5,4},{6,7},{7,6},{8,9},{9,8},{10,11... | collective-permute-start | bytes 1769480 | tf_op jit(solution)/shard_map/ppermute | solution.py:1300
  185.4 5.4 %copy-start.8 = (bf16[768,3072]{1,0:T(8,128)(2,1)S(1)}, bf16[768,3072]{1,0:T(8,128)(2,1)}, u32[]{:S(2)}) copy-start(bf16[768,3072]{1,0:T(8,128)(2,1)} %get-tuple-element.85) | copy-start | bytes 14155780
  185.4 5.4 %copy-start.12 = (bf16[768,768]{1,0:T(8,128)(2,1)S(1)}, bf16[768,768]{1,0:T(8,128)(2,1)}, u32[]{:S(2)}) copy-start(bf16[768,768]{1,0:T(8,128)(2,1)} %get-tuple-element.84) | copy-start | bytes 3538948
  185.4 8.9 %slice-start = ((s8[4718592]{0:T(1024)(128)(4,1)}), s8[4194304]{0:T(1024)(128)(4,1)S(1)}, s32[]{:S(2)}) async-start(s8[4718592]{0:T(1024)(128)(4,1)} %bitcast.82), calls=%async_computation | async-start | bytes 8388608
  190.8 3.5 slice-start.1
  190.8 3.5 copy-start.10
  197.7 3.5 copy-start
  201.8 2.9 copy-start.9
  205.3 2.5 copy-start.6
  245.8 5.2 %copy-start.2 = (bf16[768,1536]{1,0:T(8,128)(2,1)S(1)}, bf16[768,1536]{1,0:T(8,128)(2,1)}, u32[]{:S(2)}) copy-start(bf16[768,1536]{1,0:T(8,128)(2,1)} %convolution_convert_fusion.1) | copy-start | bytes 7077892
  251.0 1.7 copy-start.1
  414.5 9.3 %copy-start.3 = (bf16[1536,384]{1,0:T(8,128)(2,1)S(1)}, bf16[1536,384]{1,0:T(8,128)(2,1)}, u32[]{:S(2)}) copy-start(bf16[1536,384]{1,0:T(8,128)(2,1)} %get-tuple-element.122) | copy-start | bytes 3538948
  421.4 3.5 copy-start.4

commit v3 on v2

--- a/solution.py
+++ b/solution.py
@@ -373,10 +373,12 @@
     def row(self, step):
         return lax.rem(self.q + self.depth - step, self.depth)
 
-    def meet(self):
+    def meet(self, chip_only=False):
         barrier = pltpu.get_barrier_semaphore()
-        others = [self.across, self.beside, self.sibling, self.corner]
-        others += [self.far(step) for step in range(1, self.depth)]
+        others = [self.sibling]
+        if not chip_only:
+            others += [self.across, self.beside, self.corner]
+            others += [self.far(step) for step in range(1, self.depth)]
         for other in others:
             pl.semaphore_signal(barrier, 1, device_id=other, device_id_type=MESH)
         pl.semaphore_wait(barrier, len(others))
@@ -579,7 +581,7 @@
 
 
 def plus(left, right):
-    return (left.astype(WIDE) + right.astype(WIDE)).astype(LOW)
+    return (left.astype(WIDE) + right.astype(WIDE)).astype(left.dtype)
 
 
 def scatter_marks(depth):
@@ -587,54 +589,67 @@
 
 
 class Scatter:
-    def __init__(self, links, part, cut, whole, bufs, out, send, recv, index, local):
-        self.links, self.part, self.cut, self.whole, self.out = links, part, cut, whole, out
+    def __init__(self, links, kind, part, cut, bufs, out, send, recv, index, local):
+        self.links, self.kind, self.part, self.cut, self.out = links, kind, part, cut, out
         self.held, self.other, self.x1, self.y1, self.x2, self.y2, self.z = bufs
         self.send = lambda k: send.at[index, k]
         self.recv = lambda k: recv.at[index, k]
         self.local = local
-        self.sent = []
-        self.rest = part.shape[-1] - cut
-
-    def go(self, source, target, mark, device):
-        copy = remote(source, target, self.send(mark), self.recv(mark), device)
-        copy.start()
-        self.sent.append(copy)
+        self.rest = self.held.shape[-1] - cut
+
+    def low(self, ref):
+        return ref.at[:, :, pl.ds(0, self.cut)]
+
+    def high(self, ref):
+        return ref.at[:, :, pl.ds(self.cut, self.rest)]
+
+    def move(self, source, target, mark, device):
+        return remote(source, target, self.send(mark), self.recv(mark), device)
+
+    def copy(self, kind, step=0):
+        n = self.links
+        corner = self.held.at[1 - n.x, :, 1 - n.y]
+        if kind == "sibling" and self.kind == "join":
+            return self.move(self.part.at[:, :, :, 1 - n.c], self.other, 0, n.sibling)
+        if kind == "sibling":
+            return self.move(self.part.at[:, :, 1 - n.c], self.held.at[n.c], 0, n.sibling)
+        if kind == "x1":
+            return self.move(self.low(corner), self.x1, 1, n.across)
+        if kind == "y1":
+            return self.move(self.high(corner), self.y1, 2, n.beside)
+        if kind == "y2":
+            return self.move(self.held.at[n.x, :, 1 - n.y], self.y2, 3, n.beside)
+        if kind == "x2":
+            return self.move(self.held.at[1 - n.x, :, n.y], self.x2, 4, n.across)
+        q = lax.rem(n.q + step, n.depth)
+        return self.move(self.held.at[n.x, q, n.y], self.z.at[step - 1], 4 + step, n.far(step))
+
+    def keep(self):
+        n = self.links
+        if self.kind == "held":
+            return pltpu.make_async_copy(self.part, self.held, self.local)
+        if self.kind == "join":
+            return pltpu.make_async_copy(self.part.at[:, :, :, n.c], self.held, self.local)
+        return pltpu.make_async_copy(self.part.at[:, :, n.c], self.held.at[n.c], self.local)
 
     def arrived(self, target, mark):
-        remote(target, target, self.send(mark), self.recv(mark), self.links.sibling).wait_recv()
+        self.move(target, target, mark, self.links.sibling).wait_recv()
 
     def begin(self):
-        n = self.links
-        if self.whole:
-            self.go(self.part.at[:, :, :, 1 - n.c], self.other, 0, n.sibling)
-            self.keep = pltpu.make_async_copy(self.part.at[:, :, :, n.c], self.held, self.local)
-        else:
-            self.go(self.part.at[:, :, 1 - n.c], self.held.at[n.c], 0, n.sibling)
-            self.keep = pltpu.make_async_copy(
-                self.part.at[:, :, n.c], self.held.at[n.c], self.local
-            )
-        self.keep.start()
-
-    def join(self, h, y):
-        for q in range(self.links.depth):
-            self.held[h, q, y] = plus(self.held[h, q, y], self.other[h, q, y])
+        self.keep().start()
+        if self.kind != "held":
+            self.copy("sibling").start()
 
     def first(self):
         n = self.links
-        self.keep.wait()
-        if self.whole:
+        self.keep().wait()
+        if self.kind == "join":
             self.arrived(self.other, 0)
-            self.join(1 - n.x, 1 - n.y)
-        else:
+            self.held[...] = plus(self.held[...], self.other[...])
+        if self.kind == "swap":
             self.arrived(self.held.at[1 - n.c], 0)
-        corner = self.held.at[1 - n.x, :, 1 - n.y]
-        self.go(corner.at[:, :, pl.ds(0, self.cut)], self.x1, 1, n.across)
-        self.go(corner.at[:, :, pl.ds(self.cut, self.rest)], self.y1, 2, n.beside)
-        if self.whole:
-            self.join(n.x, 1 - n.y)
-            self.join(1 - n.x, n.y)
-            self.join(n.x, n.y)
+        self.copy("x1").start()
+        self.copy("y1").start()
 
     def second(self):
         n = self.links
@@ -644,13 +659,13 @@
             self.held[n.x, q, 1 - n.y, :, low] = plus(
                 self.held[n.x, q, 1 - n.y, :, low], self.x1[q]
             )
-        self.go(self.held.at[n.x, :, 1 - n.y], self.y2, 3, n.beside)
+        self.copy("y2").start()
         self.arrived(self.y1, 2)
         for q in range(n.depth):
             self.held[1 - n.x, q, n.y, :, high] = plus(
                 self.held[1 - n.x, q, n.y, :, high], self.y1[q]
             )
-        self.go(self.held.at[1 - n.x, :, n.y], self.x2, 4, n.across)
+        self.copy("x2").start()
 
     def third(self):
         n = self.links
@@ -658,10 +673,8 @@
         self.arrived(self.x2, 4)
         for step in range(1, n.depth):
             q = lax.rem(n.q + step, n.depth)
-            self.held[n.x, q, n.y] = plus(
-                plus(self.held[n.x, q, n.y], self.x2[q]), self.y2[q]
-            )
-            self.go(self.held.at[n.x, q, n.y], self.z.at[step - 1], 4 + step, n.far(step))
+            self.held[n.x, q, n.y] = plus(plus(self.held[n.x, q, n.y], self.x2[q]), self.y2[q])
+            self.copy("z", step).start()
 
     def fourth(self):
         n = self.links
@@ -676,19 +689,24 @@
         self.out[...] = total
 
     def close(self):
-        for copy in self.sent:
-            copy.wait_send()
-
-
-def scatter_scratch(depth, r, columns, cut):
+        if self.kind != "held":
+            self.copy("sibling").wait_send()
+        for kind in ("x1", "y1", "x2", "y2"):
+            self.copy(kind).wait_send()
+        for step in range(1, self.links.depth):
+            self.copy("z", step).wait_send()
+
+
+def scatter_scratch(depth, r, columns, cut, join=False, kind=LOW):
+    small = (1, 1, 1, 8, 128)
     return [
-        pltpu.VMEM((2, depth, 2, r, columns), LOW),
-        pltpu.VMEM((2, depth, 2, r, columns), LOW),
-        pltpu.VMEM((depth, r, cut), LOW),
-        pltpu.VMEM((depth, r, columns - cut), LOW),
-        pltpu.VMEM((depth, r, columns), LOW),
-        pltpu.VMEM((depth, r, columns), LOW),
-        pltpu.VMEM((depth - 1, r, columns), LOW),
+        pltpu.VMEM((2, depth, 2, r, columns), kind),
+        pltpu.VMEM((2, depth, 2, r, columns) if join else small, kind),
+        pltpu.VMEM((depth, r, cut), kind),
+        pltpu.VMEM((depth, r, columns - cut), kind),
+        pltpu.VMEM((depth, r, columns), kind),
+        pltpu.VMEM((depth, r, columns), kind),
+        pltpu.VMEM((depth - 1, r, columns), kind),
     ]
 
 
@@ -744,82 +762,6 @@
             corner.wait_send()
             remote(mine, mine, self.send(0), self.recv(0), n.across).wait_recv()
             remote(theirs, theirs, self.send(2), self.recv(2), n.corner).wait_recv()
-
-
-def scatter_kernel(depth, cuts, lo_in, dx_in, o_part, m_part, q_part,
-                   lo_out, dx_out, o_out, m_out, q_out, *scratch):
-    bufs = [scratch[7 * k : 7 * k + 7] for k in range(3)]
-    dx_own, dx_other, send, recv, local, extra_send, extra_recv = scratch[21:]
-    n = Links(depth)
-    n.meet()
-    spread_out = remote(
-        dx_in.at[1 - n.c], dx_other, extra_send.at[6], extra_recv.at[6], n.sibling
-    )
-    spread_out.start()
-    spread_own = pltpu.make_async_copy(dx_in.at[n.c], dx_own, local.at[3])
-    spread_own.start()
-    scatters = [
-        Scatter(n, part, cut, whole, buf, out, send, recv, k, local.at[k])
-        for k, (part, out, cut, whole, buf) in enumerate(
-            zip(
-                (o_part, m_part, q_part), (o_out, m_out, q_out), cuts, (True, True, False), bufs
-            )
-        )
-    ]
-    for item in scatters:
-        item.begin()
-    spread_own.wait()
-    spread_out.wait_recv()
-    for h in range(2):
-        dx_own[h] = plus(dx_own[h], dx_other[h])
-    lo_over = HandOver(n, lo_in, lo_out, extra_send, extra_recv, 0, local.at[4])
-    dx_over = HandOver(n, dx_own, dx_out, extra_send, extra_recv, 3, local.at[5])
-    dx_over.begin()
-    lo_over.begin()
-    for item in scatters:
-        item.first()
-    for item in scatters:
-        item.second()
-    for item in scatters:
-        item.third()
-    for item in scatters:
-        item.fourth()
-    for item in scatters:
-        item.close()
-    spread_out.wait_send()
-    lo_over.finish()
-    dx_over.finish()
-
-
-def scatter_call(depth, cuts, lo, dx, o_part, m_part, q_part):
-    r = o_part.shape[-2]
-    half, part = lo.shape[1:]
-    widths = [item.shape[-1] for item in (o_part, m_part, q_part)]
-    scratch = []
-    for columns, cut in zip(widths, cuts):
-        scratch += scatter_scratch(depth, r, columns, cut)
-    vmem = pl.BlockSpec(memory_space=pltpu.VMEM)
-    return pl.pallas_call(
-        functools.partial(scatter_kernel, depth, cuts),
-        out_shape=[jax.ShapeDtypeStruct((2 * half, part), LOW)] * 2
-        + [jax.ShapeDtypeStruct((r, columns), WIDE) for columns in widths],
-        in_specs=[ANY] * 5,
-        out_specs=[ANY] * 2 + [vmem] * 3,
-        scratch_shapes=scratch
-        + [
-            pltpu.VMEM((2, half, part), LOW),
-            pltpu.VMEM((2, half, part), LOW),
-            pltpu.SemaphoreType.DMA((3, scatter_marks(depth))),
-            pltpu.SemaphoreType.DMA((3, scatter_marks(depth))),
-            pltpu.SemaphoreType.DMA((6,)),
-            pltpu.SemaphoreType.DMA((7,)),
-            pltpu.SemaphoreType.DMA((7,)),
-        ],
-        compiler_params=pltpu.CompilerParams(
-            collective_id=1, has_side_effects=True, vmem_limit_bytes=56 * MEGA
-        ),
-        name="scatter",
-    )(lo, dx, o_part, m_part, q_part)
 
 
 def angle_tables():
@@ -1066,128 +1008,245 @@
 HIDDEN = 512
 
 
-def middle_kernel(context, rows, cot, m_full, o_full, gains, lo_ref, gc_ref, act_ref, gi_ref, fl_ref,
-                  gm_ref, ga_ref, gfs_ref, sums, slopes):
-    tile = rows.shape[1]
-    part = rows.shape[2]
-    pieces = o_full.shape[2] // HIDDEN
-    whole = jnp.concatenate([gains[0], gains[1]], axis=1)
-    gain1, bias1, gain2, bias2 = (whole[k : k + 1, :] for k in range(4))
-    summed = jnp.concatenate([rows[0], rows[1]], axis=1).astype(WIDE)
-    for h in range(2):
-        seen = jnp.concatenate([context[h, p] for p in range(3)], axis=1)
-        summed = summed + contract(seen, m_full[h, :, 0:part], 1, 1)
-    normed1, scale1 = norm_of(summed)
-    first = normed1 * gain1 + bias1
-    first_low = first.astype(LOW)
-    fl_ref[...] = first_low
-    mixed = jnp.zeros(first.shape, WIDE)
-    for h in range(2):
-        for j in range(pieces):
-            k = h * pieces + j
-            lo_end = part + j * HIDDEN
-            inner = contract(first_low, m_full[h, :, lo_end : lo_end + HIDDEN], 1, 0)
-            share = 0.5 * (1.0 + lax.erf(inner * ROOT_HALF))
-            slopes[:, k * HIDDEN : (k + 1) * HIDDEN] = (
-                share + inner * jnp.exp(-0.5 * inner * inner) * INVERSE_ROOT
+def middle_kernel(depth, context, rows, cot, gains, m_full, o_full, lo_ref, gfs_ref, sums, grads,
+                  o_held, m_held, m_mat, o_mat, act, gi, fl, gm, ga, gc, slopes, o_part, m_part,
+                  o_other, m_other, local, send, recv):
+    step = pl.program_id(0)
+    tile, part = rows.shape[1:]
+    half = fl.shape[0]
+    tiles = half // tile
+    r = o_part.shape[-2]
+    pieces = o_mat.shape[2] // HIDDEN
+    width = pieces * HIDDEN
+    n = Links(depth)
+    here = pl.ds(step * tile, tile)
+    loads = lambda: (
+        pltpu.make_async_copy(m_full, m_mat, local.at[0]),
+        pltpu.make_async_copy(o_full, o_mat, local.at[1]),
+    )
+
+    def grads_keep():
+        own = grads.at[:, pl.ds(n.c * half, half)]
+        return pltpu.make_async_copy(gc.at[n.c], own, local.at[2])
+
+    def grads_copy():
+        own = grads.at[:, pl.ds(n.c * half, half)]
+        return remote(gc.at[1 - n.c], own, send.at[4], recv.at[4], n.sibling)
+
+    def part_copy(k):
+        source, target = ((o_part, o_other) if k < 2 else (m_part, m_other))
+        h = k % 2
+        return remote(
+            source.at[h, :, :, 1 - n.c], target.at[h], send.at[k], recv.at[k], n.sibling
+        )
+
+    def join(k):
+        source, target = ((o_part, o_other) if k < 2 else (m_part, m_other))
+        h = k % 2
+        part_copy(k).wait_recv()
+        for q in range(depth):
+            for y in range(2):
+                target[h, q, y] = plus(source[h, q, y, n.c], target[h, q, y])
+
+    def held_copy(k):
+        source, target = ((o_other, o_held) if k < 2 else (m_other, m_held))
+        return pltpu.make_async_copy(source.at[k % 2], target.at[k % 2], local.at[3 + k])
+
+    @pl.when(step == 0)
+    def _():
+        for item in loads():
+            item.start()
+        n.meet(True)
+        loads()[0].wait()
+
+    @pl.when(step < tiles)
+    def _():
+        whole = jnp.concatenate([gains[0], gains[1]], axis=1)
+        gain1, bias1, gain2, bias2 = (whole[k : k + 1, :] for k in range(4))
+        summed = jnp.concatenate([rows[0], rows[1]], axis=1).astype(WIDE)
+        for h in range(2):
+            seen = jnp.concatenate([context[h, p, here] for p in range(3)], axis=1)
+            summed = summed + contract(seen, m_mat[h, :, 0:part], 1, 1)
+        normed1, scale1 = norm_of(summed)
+        first = normed1 * gain1 + bias1
+        first_low = first.astype(LOW)
+        fl[here] = first_low
+        for h in range(2):
+            for j in range(pieces):
+                lo_end = part + j * HIDDEN
+                there = slice(h * width + j * HIDDEN, h * width + (j + 1) * HIDDEN)
+                inner = contract(first_low, m_mat[h, :, lo_end : lo_end + HIDDEN], 1, 0)
+                share = 0.5 * (1.0 + lax.erf(inner * ROOT_HALF))
+                slopes[:, there] = share + inner * jnp.exp(-0.5 * inner * inner) * INVERSE_ROOT
+                act[here, there] = (inner * share).astype(LOW)
+
+        @pl.when(step == 0)
+        def _():
+            loads()[1].wait()
+
+        mixed = first
+        for h in range(2):
+            mixed = mixed + contract(act[here, h * width : (h + 1) * width], o_mat[h], 1, 1)
+        normed2, scale2 = norm_of(mixed)
+        result = (normed2 * gain2 + bias2).astype(LOW)
+        for h in range(2):
+            lo_ref[h] = result[:, h * part : (h + 1) * part]
+        cotangent = jnp.concatenate([cot[0], cot[1]], axis=1).astype(WIDE)
+        second_gain = jnp.sum(cotangent * normed2, axis=0, keepdims=True)
+        second_bias = jnp.sum(cotangent, axis=0, keepdims=True)
+        grad_second = norm_back(cotangent * gain2, normed2, scale2)
+        grad_mixed = grad_second.astype(LOW)
+        gm[here] = grad_mixed
+        for h in range(2):
+            for j in range(pieces):
+                there = slice(h * width + j * HIDDEN, h * width + (j + 1) * HIDDEN)
+                raised = contract(grad_mixed, o_mat[h, :, j * HIDDEN : (j + 1) * HIDDEN], 1, 0)
+                gi[here, there] = (raised * slopes[:, there]).astype(LOW)
+        grad_first = grad_second
+        for h in range(2):
+            grad_first = grad_first + contract(
+                gi[here, h * width : (h + 1) * width], m_mat[h, :, part : part + width], 1, 1
             )
-            act_ref[:, k * HIDDEN : (k + 1) * HIDDEN] = (inner * share).astype(LOW)
-    for h in range(2):
-        width = pieces * HIDDEN
-        mixed = mixed + contract(act_ref[:, h * width : (h + 1) * width], o_full[h], 1, 1)
-    normed2, scale2 = norm_of(first + mixed)
-    result = (normed2 * gain2 + bias2).astype(LOW)
-    for h in range(2):
-        lo_ref[h] = result[:, h * part : (h + 1) * part]
-    cotangent = jnp.concatenate([cot[0], cot[1]], axis=1).astype(WIDE)
-    second_gain = jnp.sum(cotangent * normed2, axis=0, keepdims=True)
-    second_bias = jnp.sum(cotangent, axis=0, keepdims=True)
-    grad_second = norm_back(cotangent * gain2, normed2, scale2)
-    grad_mixed = grad_second.astype(LOW)
-    gm_ref[...] = grad_mixed
-    for h in range(2):
-        for j in range(pieces):
-            k = h * pieces + j
-            raised = contract(grad_mixed, o_full[h, :, j * HIDDEN : (j + 1) * HIDDEN], 1, 0)
-            gi_ref[:, k * HIDDEN : (k + 1) * HIDDEN] = (
-                raised * slopes[:, k * HIDDEN : (k + 1) * HIDDEN]
-            ).astype(LOW)
-    grad_first = grad_second
-    for h in range(2):
-        width = pieces * HIDDEN
-        grad_first = grad_first + contract(
-            gi_ref[:, h * width : (h + 1) * width], m_full[h, :, part : part + width], 1, 1
-        )
-    first_gain = jnp.sum(grad_first * normed1, axis=0, keepdims=True)
-    first_bias = jnp.sum(grad_first, axis=0, keepdims=True)
-    grad_sum = norm_back(grad_first * gain1, normed1, scale1)
-    gfs_ref[...] = grad_sum
-    grad_attended = grad_sum.astype(LOW)
-    ga_ref[...] = grad_attended
-    for h in range(2):
-        gc_ref[h] = contract(grad_attended, m_full[h, :, 0:part], 1, 0).astype(LOW)
-    found = jnp.concatenate([first_gain, first_bias, second_gain, second_bias], axis=0)
-
-    @pl.when(pl.program_id(0) == 0)
+        first_gain = jnp.sum(grad_first * normed1, axis=0, keepdims=True)
+        first_bias = jnp.sum(grad_first, axis=0, keepdims=True)
+        grad_sum = norm_back(grad_first * gain1, normed1, scale1)
+        gfs_ref[...] = grad_sum
+        grad_attended = grad_sum.astype(LOW)
+        ga[here] = grad_attended
+        for h in range(2):
+            made = contract(grad_attended, m_mat[h, :, 0:part], 1, 0).astype(LOW)
+            for p in range(3):
+                gc[h, p, here] = made[:, p * 128 : (p + 1) * 128]
+        found = jnp.concatenate([first_gain, first_bias, second_gain, second_bias], axis=0)
+
+        @pl.when(step == 0)
+        def _():
+            sums[...] = found
+
+        @pl.when(step > 0)
+        def _():
+            sums[...] += found
+
+    @pl.when(step == tiles - 1)
     def _():
-        sums[...] = found
-
-    @pl.when(pl.program_id(0) > 0)
-    def _():
-        sums[...] += found
-
-
-def middle_call(context, rows, cot, m_full, o_full, gains):
+        grads_keep().start()
+        grads_copy().start()
+
+    def put(target, h, row, column, values):
+        shards = values.shape[0] // r
+        for k in range(shards):
+            w = row // r + k
+            target[h, w // 4, (w // 2) % 2, w % 2, :, column : column + values.shape[1]] = values[
+                k * r : (k + 1) * r
+            ]
+
+    for k in range(4):
+
+        @pl.when(step == tiles + k)
+        def _():
+            h = k % 2
+            target = o_part if k < 2 else m_part
+            for row in range(0, 2 * part, part):
+                for j in range(pieces):
+                    there = slice(h * width + j * HIDDEN, h * width + (j + 1) * HIDDEN)
+                    if k < 2:
+                        made = contract(gm[:, row : row + part], act[:, there], 0, 0)
+                        put(target, h, row, j * HIDDEN, made.astype(LOW))
+                    else:
+                        made = contract(fl[:, row : row + part], gi[:, there], 0, 0)
+                        put(target, h, row, part + j * HIDDEN, made.astype(LOW))
+                if k >= 2:
+                    seen = jnp.concatenate([context[h, p] for p in range(3)], axis=1)
+                    made = contract(ga[:, row : row + part], seen, 0, 0)
+                    put(target, h, row, 0, made.astype(LOW))
+            part_copy(k).start()
+            if k:
+                join(k - 1)
+                held_copy(k - 1).start()
+            if k == 3:
+                join(3)
+                held_copy(3).start()
+                for item in range(4):
+                    held_copy(item).wait()
+                    part_copy(item).wait_send()
+                grads_keep().wait()
+                grads_copy().wait()
+
+
+def once(shape):
+    zeros = (0,) * len(shape)
+    return pl.BlockSpec(shape, lambda *_: zeros, pipeline_mode=pl.Buffered(1))
+
+
+def middle_call(depth, context, rows, cot, m_full, o_full, gains):
     tile = 256
-    half, part = rows.shape[1:]
+    half, part = cot.shape[1:]
+    tiles = half // tile
     width = 2 * part
     hidden = 2 * o_full.shape[2]
-    vmem = pl.BlockSpec(memory_space=pltpu.VMEM)
-    split = pl.BlockSpec((2, tile, part), lambda i: (0, i, 0))
-    flat = pl.BlockSpec((tile, width), lambda i: (i, 0))
-    wide = pl.BlockSpec((tile, hidden), lambda i: (i, 0))
+    r = width // (4 * depth)
+    columns = (o_full.shape[2], m_full.shape[2])
     low = lambda *shape: jax.ShapeDtypeStruct(shape, LOW)
+    held = [(2, depth, 2, r, item) for item in columns]
+    last = lambda i: jnp.minimum(i, tiles - 1)
+    c = lambda: lax.rem(lax.axis_index("wide"), 2)
     return pl.pallas_call(
-        middle_kernel,
-        grid=(half // tile,),
+        functools.partial(middle_kernel, depth),
+        grid=(tiles + 4,),
         out_shape=[
             low(2, half, part),
-            low(2, half, part),
-            low(half, hidden),
-            low(half, hidden),
-            low(half, width),
-            low(half, width),
-            low(half, width),
             jax.ShapeDtypeStruct((half, width), WIDE),
             jax.ShapeDtypeStruct((4, width), WIDE),
-        ],
+            low(3, 2 * half, 128),
+        ]
+        + [low(*item) for item in held],
         in_specs=[
-            pl.BlockSpec((2, 3, tile, 128), lambda i: (0, 0, i, 0)),
-            split,
-            split,
-            vmem,
-            vmem,
-            vmem,
+            once((2, 3, half, 128)),
+            pl.BlockSpec((2, tile, part), lambda i: (0, c() * tiles + last(i), 0)),
+            pl.BlockSpec((2, tile, part), lambda i: (0, last(i), 0)),
+            once(gains.shape),
+            ANY,
+            ANY,
         ],
         out_specs=[
-            split,
-            split,
-            wide,
-            wide,
-            flat,
-            flat,
-            flat,
-            flat,
+            pl.BlockSpec((2, tile, part), lambda i: (0, last(i), 0)),
+            pl.BlockSpec((tile, width), lambda i: (last(i), 0)),
             pl.BlockSpec((4, width), lambda i: (0, 0)),
+            ANY,
+            ANY,
+            ANY,
         ],
-        scratch_shapes=[pltpu.VMEM((tile, hidden), WIDE)],
-        compiler_params=pltpu.CompilerParams(vmem_limit_bytes=60 * MEGA),
+        scratch_shapes=[
+            pltpu.VMEM(m_full.shape, LOW),
+            pltpu.VMEM(o_full.shape, LOW),
+            pltpu.VMEM((half, hidden), LOW),
+            pltpu.VMEM((half, hidden), LOW),
+            pltpu.VMEM((half, width), LOW),
+            pltpu.VMEM((half, width), LOW),
+            pltpu.VMEM((half, width), LOW),
+            pltpu.VMEM((2, 3, half, 128), LOW),
+            pltpu.VMEM((tile, hidden), WIDE),
+        ]
+        + [pltpu.VMEM((2, depth, 2, 2, r, item), LOW) for item in columns]
+        + [pltpu.VMEM(item, LOW) for item in held]
+        + [
+            pltpu.SemaphoreType.DMA((7,)),
+            pltpu.SemaphoreType.DMA((5,)),
+            pltpu.SemaphoreType.DMA((5,)),
+        ],
+        compiler_params=pltpu.CompilerParams(
+            collective_id=1, has_side_effects=True, vmem_limit_bytes=62 * MEGA
+        ),
         name="middle",
-    )(context, rows, cot, m_full, o_full, gains)
-
-
-def backward_kernel(core, meta, base, jump, soft, grads, context, inverse, q_ref, k_ref, v_ref, rows,
-                    weight, kept, part_ref, dx_ref, ones, keys_sum, values_sum, made):
+    )(context, rows, cot, gains, m_full, o_full)
+
+
+def backward_kernel(depth, cuts, meta, base, jump, soft, grads, context, inverse, q_ref, k_ref, v_ref,
+                    rows, kept, q_full, lo_in, o_in, m_in, t_in, lo_out, dx_out, o_out, m_out, q_out,
+                    t_out, *scratch):
+    ones, keys_sum, values_sum, made, weight, q_part, dx_own, dx_give, dx_other = scratch[:9]
+    bufs = [scratch[9 + 7 * k : 16 + 7 * k] for k in range(6)]
+    piece, send, recv, local, extra_send, extra_recv = scratch[51:]
     step = pl.program_id(0)
     p = step // SPAN
     i = step % SPAN
@@ -1195,10 +1254,53 @@
     scale = HEAD_DIM ** (-0.5)
     lane = lanes(BLOCK)
     here = pl.ds(i * BLOCK, BLOCK)
+    n = Links(depth)
+    r = o_in.shape[-2]
+    half, width = kept.shape
+    part = width // 2
+    kinds = ("held", "held", "swap", "swap", "swap", "join")
+    parts = (o_in, m_in) + tuple(q_part.at[k] for k in range(3)) + (t_in,)
+    outs = (o_out, m_out) + tuple(q_out.at[k] for k in range(3)) + (t_out,)
+    every = [
+        Scatter(n, kind, item, cut, buf, out, send, recv, k, local.at[k])
+        for k, (kind, item, cut, buf, out) in enumerate(zip(kinds, parts, cuts, bufs, outs))
+    ]
+    outer, inner, pair0, pair1, pair2, small = every
+    lo_over = HandOver(n, lo_in, lo_out, extra_send, extra_recv, 0, local.at[6])
+    dx_over = HandOver(n, dx_own, dx_out, extra_send, extra_recv, 3, local.at[7])
+    dx_swap = lambda: remote(dx_give, dx_other, extra_send.at[6], extra_recv.at[6], n.sibling)
 
     @pl.when(step == 0)
     def _():
         ones[...] = (lanes(length) < 2).astype(WIDE).astype(LOW)
+        for item in weight_loads(q_full, n.c, weight, piece):
+            item.start()
+        outer.begin()
+        inner.begin()
+        n.meet()
+        small.begin()
+        outer.first()
+        inner.first()
+        small.first()
+        for item in weight_loads(q_full, n.c, weight, piece):
+            item.wait()
+
+    hooks = {
+        1: [outer.second, small.second, lo_over.begin],
+        2: [inner.second, small.third],
+        3: [small.fourth, pair0.first],
+        4: [outer.third, pair0.second],
+        5: [pair0.third],
+        6: [inner.third, outer.fourth, pair1.first],
+        7: [pair1.second, pair0.fourth],
+        8: [pair1.third, inner.fourth],
+    }
+    for at, actions in hooks.items():
+
+        @pl.when(step == at)
+        def _():
+            for action in actions:
+                action()
 
     grad = grads[p, here].astype(WIDE)
     turned = grad * inverse[p, here]
@@ -1209,7 +1311,7 @@
     values = jnp.concatenate([v_ref[p], ones[...]], axis=1)
     turned_flip = jnp.transpose(turned).astype(LOW)
     queries_flip = jnp.transpose(queries.astype(WIDE)).astype(LOW)
-    outs = []
+    found = []
     for head in range(2):
         chosen = (lane // HEAD_DIM) == head
         centre = -jnp.sum(jnp.where(chosen, both, 0.0), axis=1, keepdims=True)
@@ -1220,7 +1322,7 @@
         )
         raised = soft[0, head]
         scores = (contract(ours, values, 1, 1) * raised.astype(WIDE)).astype(LOW)
-        outs.append(contract(scores, keys, 1, 0))
+        found.append(contract(scores, keys, 1, 0))
         mine = slice(head * HEAD_DIM, (head + 1) * HEAD_DIM)
         values_add = contract(turned_flip[mine], raised, 1, 0)
         keys_add = contract(queries_flip[mine], scores, 1, 0)
@@ -1236,7 +1338,7 @@
             keys_sum[mine] += keys_add
 
     cosine, sine, low = turn_parts(meta, base, jump, i)
-    grad_queries = jnp.where(lane < HEAD_DIM, outs[0], outs[1]) * scale
+    grad_queries = jnp.where(lane < HEAD_DIM, found[0], found[1]) * scale
     made[p, here, 0:128] = turn(grad_queries, cosine, -sine, low).astype(LOW)
 
     @pl.when(i == SPAN - 1)
@@ -1249,57 +1351,108 @@
             made[p, there, 128:256] = turn(grad_keys[there], cosine, -sine, low).astype(LOW)
         made[p, :, 256:384] = grad_values.astype(LOW)
         for h in range(2):
-            part = rows.shape[2]
-            part_ref[p, h * part : (h + 1) * part] = contract(rows[h], made[p], 0, 0).astype(LOW)
+            found = contract(rows[h], made[p], 0, 0).astype(LOW)
+            for k in range(part // r):
+                w = h * (part // r) + k
+                q_part[p, w // 4, (w // 2) % 2, w % 2] = found[k * r : (k + 1) * r]
+
+    for k in range(3):
+
+        @pl.when(step == k * SPAN + SPAN - 1)
+        def _():
+            every[2 + k].begin()
 
     @pl.when(step == 3 * SPAN - 1)
     def _():
-        half = kept.shape[0]
-        part = rows.shape[2]
-        for other in range(2):
-            c = core[0] if other == 0 else 1 - core[0]
-            there = pl.ds(c * half, half)
-            gained = kept[...] if other == 0 else jnp.zeros(kept.shape, WIDE)
-            for pair in range(3):
-                gained = gained + contract(made[pair, there], weight[:, pair * 384 : pair * 384 + 384], 1, 1)
+        for own in (False, True):
+            there = pl.ds((n.c if own else 1 - n.c) * half, half)
+            gained = kept[...] if own else jnp.zeros(kept.shape, WIDE)
+            for k in range(3):
+                gained = gained + contract(
+                    made[k, there], weight[:, k * 384 : k * 384 + 384], 1, 1
+                )
+            target = dx_own if own else dx_give
             for h in range(2):
-                dx_ref[c, h] = gained[:, h * part : (h + 1) * part].astype(LOW)
-
-
-def backward_call(core, meta, base, jump, soft, grads, context, inverse, q, k, v, rows, weight, kept):
+                target[h] = gained[:, h * part : (h + 1) * part].astype(LOW)
+            if own:
+                pair2.second()
+            else:
+                dx_swap().start()
+                pair2.first()
+        dx_swap().wait_recv()
+        for h in range(2):
+            dx_own[h] = plus(dx_own[h], dx_other[h])
+        dx_over.begin()
+        pair2.third()
+        pair1.fourth()
+        pair2.fourth()
+        for item in every:
+            item.close()
+        dx_swap().wait_send()
+        lo_over.finish()
+        dx_over.finish()
+
+
+def backward_call(depth, cuts, meta, base, jump, soft, grads, context, inverse, q, k, v, rows, kept,
+                  q_full, lo, o_held, m_held, t_part):
     length = q.shape[1]
     half, width = kept.shape
     part = width // 2
-    vmem = pl.BlockSpec(memory_space=pltpu.VMEM)
-    smem = pl.BlockSpec(memory_space=pltpu.SMEM)
+    r = o_held.shape[-2]
+    trio = once((3, length, 128))
+    low = lambda *shape: jax.ShapeDtypeStruct(shape, LOW)
+    widths = (o_held.shape[-1], m_held.shape[-1])
+    shape = lambda *item: jax.ShapeDtypeStruct(item, WIDE)
+    outs = [shape(r, widths[0]), shape(r, widths[1]), shape(3, r, 384), shape(*t_part.shape[-2:])]
+    scratch = [
+        pltpu.VMEM((length, 128), LOW),
+        pltpu.VMEM((128, length), WIDE),
+        pltpu.VMEM((128, length), WIDE),
+        pltpu.VMEM((3, length, 384), LOW),
+        pltpu.VMEM((width, 3 * 384), LOW),
+        pltpu.VMEM((3, depth, 2, 2, r, 384), LOW),
+        pltpu.VMEM((2, half, part), LOW),
+        pltpu.VMEM((2, half, part), LOW),
+        pltpu.VMEM((2, half, part), LOW),
+    ]
+    for at, columns in enumerate(widths + (384,) * 3):
+        scratch += scatter_scratch(depth, r, columns, cuts[at])
+    scratch += scatter_scratch(depth, t_part.shape[-2], t_part.shape[-1], cuts[5], True, WIDE)
+    marks = pltpu.SemaphoreType.DMA((6, scatter_marks(depth)))
     return pl.pallas_call(
-        backward_kernel,
+        functools.partial(backward_kernel, depth, cuts),
         grid=(3 * SPAN,),
-        out_shape=[
-            jax.ShapeDtypeStruct((3, width, 384), LOW),
-            jax.ShapeDtypeStruct((2, 2, half, part), LOW),
+        out_shape=[low(2 * half, part)] * 2 + outs,
+        in_specs=[
+            pl.BlockSpec(memory_space=pltpu.SMEM),
+            once(base.shape),
+            once(jump.shape),
+            pl.BlockSpec((1, 2, BLOCK, length), lambda s: (s, 0, 0, 0)),
+            trio,
+            trio,
+            trio,
+            trio,
+            trio,
+            trio,
+            once(rows.shape),
+            once(kept.shape),
+        ]
+        + [ANY] * 5,
+        out_specs=[ANY] * 2 + [once(item.shape) for item in outs],
+        scratch_shapes=scratch
+        + [
+            pltpu.SemaphoreType.DMA((4 * depth,)),
+            marks,
+            marks,
+            pltpu.SemaphoreType.DMA((8,)),
+            pltpu.SemaphoreType.DMA((7,)),
+            pltpu.SemaphoreType.DMA((7,)),
         ],
-        in_specs=[smem, smem, vmem, vmem, pl.BlockSpec((1, 2, BLOCK, length), lambda s: (s, 0, 0, 0))]
-        + [vmem] * 9,
-        out_specs=[vmem, vmem],
-        scratch_shapes=[
-            pltpu.VMEM((length, 128), LOW),
-            pltpu.VMEM((128, length), WIDE),
-            pltpu.VMEM((128, length), WIDE),
-            pltpu.VMEM((3, length, 384), LOW),
-        ],
-        compiler_params=pltpu.CompilerParams(vmem_limit_bytes=60 * MEGA),
+        compiler_params=pltpu.CompilerParams(
+            collective_id=2, has_side_effects=True, vmem_limit_bytes=63 * MEGA
+        ),
         name="attend_back",
-    )(core, meta, base, jump, soft, grads, context, inverse, q, k, v, rows, weight, kept)
-
-
-def swap_back(values, half, c):
-    n_wide = lax.axis_size("wide")
-    mine = lax.dynamic_index_in_dim(values, c, 0, keepdims=False)
-    theirs = lax.dynamic_index_in_dim(values, 1 - c, 0, keepdims=False)
-    got = lax.ppermute(theirs, "wide", [(w, w ^ 1) for w in range(n_wide)])
-    whole = jnp.where(c == 0, jnp.concatenate([mine, got]), jnp.concatenate([got, mine]))
-    return jnp.moveaxis(whole.reshape(whole.shape[0], -1, 128), 1, 0)
+    )(meta, base, jump, soft, grads, context, inverse, q, k, v, rows, kept, q_full, lo, o_held, m_held, t_part)
 
 
 def owned(
@@ -1349,44 +1502,41 @@
             depth, cuts, meta, gains, output_cotangent, inputs, q_own, m_own, o_own, base, jump
         )
     )
-    weight = lax.dynamic_index_in_dim(q_full, c, 0, keepdims=False).reshape(2 * part, widths[0])
-    m_full = m_full.reshape(2, 2 * part, widths[1])
-    o_full = o_full.reshape(2, 2 * part, widths[2])
-    own_rows = lax.dynamic_slice_in_dim(rows, c * half, half, axis=1)
-    lo, gc, act, gi, fl, gm, ga, kept, sums = middle_call(
-        pairs_context, own_rows, cot, m_full, o_full, gains
-    )
-    all_context = jnp.moveaxis(pairs_context, 1, 2).reshape(2, half, part)
-    hidden = act.shape[1] // 2
-    o_part = jnp.stack(
-        [left_transposed(gm, act[:, h * hidden : (h + 1) * hidden]).astype(LOW) for h in range(2)]
-    )
-    m_part = jnp.stack(
-        [
-            jnp.concatenate(
-                [
-                    left_transposed(ga, all_context[h]).astype(LOW),
-                    left_transposed(fl, gi[:, h * hidden : (h + 1) * hidden]).astype(LOW),
-                ],
-                axis=1,
-            )
-            for h in range(2)
-        ]
-    )
-    grads = swap_back(gc, half, c)
-    core = jnp.reshape(c, (1,)).astype(jnp.int32)
-    q_part, dx = backward_call(
-        core, meta, base, jump, soft, grads, context, inverse, q, k, v, rows, weight, kept
-    )
-    q_part = jnp.moveaxis(q_part, 0, 1)
-    q_part = q_part.reshape(depth, 2, 2, r, widths[0])
-    m_part = m_part.reshape(2, depth, 2, 2, r, widths[1])
-    o_part = o_part.reshape(2, depth, 2, 2, r, widths[2])
-    layer_output, input_gradient, o_sum, m_sum, q_sum = scatter_call(
-        depth, [cuts[2], cuts[1], cuts[0]], lo, dx, o_part, m_part, q_part
-    )
-    q_sum = q_sum.reshape(r, pairs, 3, 128)
-    sums = lax.psum_scatter(sums, ("narrow", "wide"), scatter_dimension=1, tiled=True)
+    lo, kept, sums, grads, o_held, m_held = middle_call(
+        depth,
+        pairs_context,
+        rows,
+        cot,
+        m_full.reshape(2, 2 * part, widths[1]),
+        o_full.reshape(2, 2 * part, widths[2]),
+        gains,
+    )
+    few = 2 * part // (2 * wide)
+    spots = jnp.moveaxis(sums.reshape(2, 2, 2, wide, few), (2, 3), (0, 1))
+    spots = jnp.pad(jnp.moveaxis(spots, 2, 3), ((0, 0), (0, 0), (0, 6), (0, 0), (0, 128 - few)))
+    spots = spots.reshape(2, depth, 2, 2, 8, 256)
+    layer_output, input_gradient, o_sum, m_sum, q_sum, found = backward_call(
+        depth,
+        [cuts[2], cuts[1], 128, 128, 128, 128],
+        meta,
+        base,
+        jump,
+        soft,
+        grads,
+        context,
+        inverse,
+        q,
+        k,
+        v,
+        rows,
+        kept,
+        q_full,
+        lo,
+        o_held,
+        m_held,
+        spots,
+    )
+    q_sum = jnp.moveaxis(q_sum, 0, 1).reshape(r, pairs, 3, 128)
     return (
         layer_output,
         input_gradient,
@@ -1396,10 +1546,10 @@
         m_sum[:, 0:part].T,
         m_sum[:, part:],
         o_sum.T,
-        sums[0],
-        sums[1],
-        sums[2],
-        sums[3],
+        found[0, 0:few],
+        found[1, 0:few],
+        found[0, 128 : 128 + few],
+        found[1, 128 : 128 + few],
     )
 
 

time: 434 us -> 335 us (0.77)
  blocking collectives: 37.3 us -> 0 us
  matrix products: 18.3 us -> 0 us
  local copies, waits for them, and re-layouts: 40.4 us -> 23.6 us
  Pallas kernels: 312 us -> 300 us
  other arithmetic: 15.9 us -> 6.51 us
    unnamed x1 -> x0, blocking collectives: 37.3 us -> none
    dot_general x6 -> x0, matrix products: 18.3 us -> none  [left_transposed(): lax.dot_general(left, right, (((0,), (0,)), ((), ())), preferred_element_...]
    pallas_call x3 -> x2, Pallas kernels: 182 us -> 170 us  [the longest x1 121 us: backward_call(): pl.pallas_call(functools.partial(backward_kernel, depth, cuts), grid=(3 *...]
    dynamic_slice x4 -> x0, local copies, waits for them, and re-layouts: 7.83 us -> none  [the longest x1 2.89 us: owned(): lax.dynamic_index_in_dim(q_full, c, 0, keepdims=False)]
    another operation x6 -> x5, other arithmetic: 11.6 us -> 3.96 us  [the longest x1 5.19 us: owned(): jnp.stack([left_transposed(gm, act[:, h * hidden:(h + 1) * hidden]).astyp...]
    unnamed x45 -> x22, local copies, waits for them, and re-layouts: 13.4 us -> 9.91 us
  transfers between devices with their start and end apart: 1 -> 0, of which waited for: 0 -> 0; matrix products, arithmetic and copies ran while one was open for 8% -> 0% of each run, Pallas kernels for 0% -> 0%
where the time goes in v3:
time: 335 us; the launch traced here: 331 us
  Pallas kernels  300 us (90%)
  local copies, waits for them, and re-layouts  23.6 us (7%)
  other arithmetic  6.51 us (2%)
    pallas_call x1, Pallas kernels, forward_call(): pl.pallas_call(functools.partial(forward_kernel, depth, cuts), grid=(SPAN...  130 us
    pallas_call x1, Pallas kernels, backward_call(): pl.pallas_call(functools.partial(backward_kernel, depth, cuts), grid=(3 *...  121 us
    pallas_call x1, Pallas kernels, middle_call(): pl.pallas_call(functools.partial(middle_kernel, depth), grid=(tiles + 4,)...  48.2 us
    unnamed x22, local copies, waits for them, and re-layouts  9.91 us

profile of v3, /device:TPU:1, one launch (start us, length us, event | category | flops | bytes accessed | tf_op | source)
XLA Modules:
  0.0 330.7 jit_solution(9945499346573458178)
XLA Ops:
  0.6 0.6 compare_reduce_fusion
  1.3 0.6 and_reduce_fusion
  1.9 1.3 fusion
  3.2 0.9 convert_reduce_fusion
  4.2 0.6 slice.90
  4.7 1.4 broadcast_select_fusion
  6.1 0.9 scatter.9.note_in
  7.0 0.0 copy-start.4
  7.0 0.7 stack.13
  7.7 0.7 stack.14
  8.4 0.7 stack.15
  9.1 0.7 stack.16
  9.7 0.6 concatenate.14.gain_in
  10.4 0.7 constant_dynamic-update-slice_fusion.8
  11.1 0.7 constant_dynamic-update-slice_fusion.7
  11.8 0.7 constant_dynamic-update-slice_fusion.6
  12.5 0.7 constant_dynamic-update-slice_fusion.5
  13.2 0.7 constant_dynamic-update-slice_fusion.4
  13.9 0.7 constant_dynamic-update-slice_fusion.3
  14.6 0.7 constant_dynamic-update-slice_fusion.2
  15.4 0.7 constant_dynamic-update-slice_fusion.1
  16.1 0.7 constant_dynamic-update-slice_fusion.q_own
  16.8 0.0 copy-start.3
  16.8 1.6 pad_maximum_fusion.m_own
  18.4 0.0 copy-done.4
  18.5 0.0 copy-done.3
  18.5 130.3 %attend.1 = (s32[1,128]{1,0:T(1,128)}, f32[2,8,384]{2,1,0:T(8,128)}, bf16[2,768,384]{2,1,0:T(8,128)(2,1)}, bf16[2,1536,384]{2,1,0:T(8,128)(2,1)}, bf16[2,4,2,2,4...) custom-call(s32[1,128]{1,0:T(1,128)} %copy-done.4, ...), custom_call_target="tpu_custom_call" | custom-call | tf_op jit(solution)/shard_map/attend/pallas_call | solution.py:946
  148.8 48.2 %middle.1 = (bf16[2,768,384]{2,1,0:T(8,128)(2,1)}, f32[768,768]{1,0:T(8,128)}, f32[4,768]{1,0:T(4,128)}, bf16[3,1536,128]{2,1,0:T(8,128)(2,1)}, bf16[2,4,2,48,15...) custom-call(bf16[2,3,768,128]{3,2,1,0:T(8,128)(2,1)} %get-tuple-element.64.context, ...), custom_call_target="tpu_custom_call" | custom-call | tf_op jit(solution)/shard_map/middle/pallas_call | solution.py:1193
  197.0 0.8 reshape.112
  197.8 0.1 copy.47
  197.9 0.7 pad.12
  198.6 121.3 %attend_back.1 = (bf16[1536,384]{1,0:T(8,128)(2,1)}, bf16[1536,384]{1,0:T(8,128)(2,1)}, f32[48,1536]{1,0:T(8,128)}, f32[48,1920]{1,0:T(8,128)}, f32[3,48,384]{2,1,0:T(8,128)}, /*index=5*/f32[8,256]{1,0:T(8,128)}) custom-call(s32[1,128]{1,0:T(1,128)} %get-tuple-element.62.meta, f32[1024,128]{1,0:T(8,128)} %constant.60.clone.base, ...), custom_call_target="tpu_custom_call" | custom-call | tf_op jit(solution)/shard_map/attend_back/pallas_call | solution.py:1422
  319.9 1.3 slice_bitcast_fusion.1
  321.2 1.5 slice_bitcast_fusion
  322.7 0.0 copy-start.1
  322.7 1.8 slice.104
  324.5 1.0 reshape.114
  325.5 0.2 fusion.1
  325.8 0.7 copy_bitcast_fusion
  326.5 0.6 copy.46
  327.1 0.0 copy-done.1
  327.1 0.0 copy-start
  327.1 1.0 copy.60
  328.1 0.7 copy-done
  328.8 0.0 copy-start.2
  328.8 1.0 copy.61
  329.8 0.1 copy-done.2
  329.9 0.7 copy.62
  (5 shorter events, 0.1 us)
Async XLA Ops:
  7.0 11.5 %copy-start.4 = (s32[1,128]{1,0:T(1,128)}, s32[1,128]{1,0:T(1,128)S(1)}, u32[]{:S(2)}) copy-start(s32[1,128]{1,0:T(1,128)S(1)} %scatter.9.note_in) | copy-start | bytes 1540
  16.8 1.6 copy-start.3
  322.7 4.4 %copy-start.1 = (bf16[1536,384]{1,0:T(8,128)(2,1)S(1)}, bf16[1536,384]{1,0:T(8,128)(2,1)}, u32[]{:S(2)}) copy-start(bf16[1536,384]{1,0:T(8,128)(2,1)} %get-tuple-element.109) | copy-start | bytes 3538948
  327.1 1.7 copy-start
  328.8 1.1 copy-start.2

commit v4 on v3

--- a/solution.py
+++ b/solution.py
@@ -373,11 +373,11 @@
     def row(self, step):
         return lax.rem(self.q + self.depth - step, self.depth)
 
-    def meet(self, chip_only=False):
+    def meet(self, pair_only=False):
         barrier = pltpu.get_barrier_semaphore()
-        others = [self.sibling]
-        if not chip_only:
-            others += [self.across, self.beside, self.corner]
+        others = [self.sibling, self.across, self.corner]
+        if not pair_only:
+            others += [self.beside]
             others += [self.far(step) for step in range(1, self.depth)]
         for other in others:
             pl.semaphore_signal(barrier, 1, device_id=other, device_id_type=MESH)
@@ -447,11 +447,17 @@
         return pltpu.make_async_copy(self.own, self.slot(n.x, n.q, n.y), self.local)
 
     def begin(self):
+        self.begin_far()
+        self.begin_near()
+
+    def begin_far(self):
+        for step in range(1, self.links.depth):
+            self.copy("far", step).start()
+
+    def begin_near(self):
         self.keep().start()
         self.copy("across").start()
         self.copy("beside").start()
-        for step in range(1, self.links.depth):
-            self.copy("far", step).start()
 
     def second(self, step):
         n = self.links
@@ -481,6 +487,17 @@
         for h in range(2 if self.whole else 1):
             self.arrived(self.full.at[h if self.whole else n.c, :, :, 1 - n.c], 5 * d + h)
 
+    def halfway(self):
+        n, d = self.links, self.links.depth
+        self.keep().wait()
+        for step in range(d):
+            self.arrived(self.slot(1 - n.x, n.row(step), n.y), d + step)
+            self.arrived(self.slot(n.x, n.row(step), 1 - n.y), 2 * d + step)
+            if step:
+                self.copy("far", step).wait_send()
+            for kind in ("across", "beside"):
+                self.copy(kind, step).wait_send()
+
     def close(self):
         d = self.links.depth
         for step in range(d):
@@ -492,54 +509,125 @@
             self.copy("sibling", h).wait_send()
 
 
+class Finish:
+    def __init__(self, links, full, flat, cut, send, recv, base, local):
+        self.links, self.full, self.flat, self.cut, self.local = links, full, flat, cut, local
+        self.send = lambda k: send.at[base + k]
+        self.recv = lambda k: recv.at[base + k]
+        self.r, self.width = full.shape[-2:]
+
+    def slot(self, h, q, y, c):
+        w = (q * 2 + y) * 2 + c
+        return self.flat.at[h, pl.ds(pl.multiple_of(w * self.r, self.r), self.r)]
+
+    def low(self, ref):
+        return ref.at[:, pl.ds(0, self.cut)]
+
+    def high(self, ref):
+        return ref.at[:, pl.ds(self.cut, self.width - self.cut)]
+
+    def hop(self, kind, step):
+        n, d = self.links, self.links.depth
+        q = n.row(step)
+        h, y, part, mark, device = {
+            "high": (1 - n.x, n.y, self.high, step, n.beside),
+            "low": (n.x, 1 - n.y, self.low, d + step, n.across),
+        }[kind]
+        source, target = part(self.full.at[h, q, y, n.c]), part(self.slot(h, q, y, n.c))
+        return remote(source, target, self.send(mark), self.recv(mark), device)
+
+    def spread(self, h, q, y):
+        n, d = self.links, self.links.depth
+        mark = 2 * d + (h * d + q) * 2 + y
+        part = self.slot(h, q, y, n.c)
+        return remote(part, part, self.send(mark), self.recv(mark), n.sibling)
+
+    def loads(self):
+        n, d = self.links, self.links.depth
+        return [
+            pltpu.make_async_copy(
+                self.full.at[h, q, y, n.c], self.slot(h, q, y, n.c), self.local.at[k * d + q]
+            )
+            for k, (h, y) in enumerate(((n.x, n.y), (1 - n.x, n.y), (n.x, 1 - n.y)))
+            for q in range(d)
+        ]
+
+    def everywhere(self, act):
+        for h in range(2):
+            for q in range(self.links.depth):
+                for y in range(2):
+                    act(self.spread(h, q, y))
+
+    def begin(self):
+        for step in range(self.links.depth):
+            self.hop("high", step).start()
+            self.hop("low", step).start()
+        for item in self.loads():
+            item.start()
+
+    def fourth(self):
+        n, d = self.links, self.links.depth
+        for item in self.loads():
+            item.wait()
+        for step in range(d):
+            got = self.slot(1 - n.x, n.row(step), 1 - n.y, n.c)
+            for part, mark in ((self.high(got), step), (self.low(got), d + step)):
+                remote(part, part, self.send(mark), self.recv(mark), n.sibling).wait_recv()
+        self.everywhere(lambda item: item.start())
+
+    def finish(self):
+        n = self.links
+        for h in range(2):
+            for q in range(n.depth):
+                for y in range(2):
+                    mark = 2 * n.depth + (h * n.depth + q) * 2 + y
+                    got = self.slot(h, q, y, 1 - n.c)
+                    remote(got, got, self.send(mark), self.recv(mark), n.sibling).wait_recv()
+
+    def close(self):
+        for step in range(self.links.depth):
+            self.hop("high", step).wait_send()
+            self.hop("low", step).wait_send()
+        self.everywhere(lambda item: item.wait_send())
+
+
 class Share:
-    def __init__(self, links, in_ref, rows, cot_in, cot, note_in, note, gain_in, gain, send, recv, local):
+    def __init__(self, links, in_ref, rows, note_in, note, gain_in, gain, send, recv, local):
         n = self.links = links
-        half = cot_in.shape[0] // 2
         self.home = n.x == n.c
         s, r = (lambda k: send.at[k]), (lambda k: recv.at[k])
-        mine, theirs = pl.ds(n.c * half, half), pl.ds((1 - n.c) * half, half)
         near, far = rows.at[n.x], rows.at[1 - n.x]
         self.rows_across = lambda: remote(in_ref, near, s(0), r(0), n.across)
         self.rows_beside = lambda: remote(in_ref, near, s(1), r(1), n.sibling)
         self.rows_further = lambda: remote(far, far, s(2), r(2), n.sibling)
         self.note = lambda: remote(note_in, note, s(3), r(3), n.sibling)
-        self.cot_beside = lambda: remote(cot_in.at[theirs], cot.at[n.x], s(4), r(4), n.sibling)
-        self.cot_across = lambda: remote(cot_in.at[mine], cot.at[n.x], s(5), r(5), n.across)
-        self.cot_corner = lambda: remote(cot_in.at[theirs], cot.at[n.x], s(6), r(6), n.corner)
-        self.gain = lambda: remote(gain_in, gain.at[n.x], s(7), r(7), n.across)
-        self.keep = lambda: [
-            pltpu.make_async_copy(gain_in, gain.at[n.x], local.at[0]),
-        ]
-        self.keep_home = lambda: [
-            pltpu.make_async_copy(in_ref, near, local.at[1]),
-            pltpu.make_async_copy(note_in, note, local.at[2]),
-            pltpu.make_async_copy(cot_in.at[mine], cot.at[n.x], local.at[3]),
-        ]
+        self.gain = lambda: remote(gain_in, gain.at[n.x], s(4), r(4), n.across)
+        self.gain_keep = lambda: pltpu.make_async_copy(gain_in, gain.at[n.x], local.at[0])
+        self.rows_keep = lambda: pltpu.make_async_copy(in_ref, near, local.at[1])
+        self.note_keep = lambda: pltpu.make_async_copy(note_in, note, local.at[2])
 
     def begin(self):
         @pl.when(self.home)
         def _():
             self.note().start()
             self.rows_beside().start()
-            for item in self.keep_home():
-                item.start()
+            self.rows_keep().start()
+            self.note_keep().start()
 
         @pl.when(jnp.logical_not(self.home))
         def _():
             self.rows_across().start()
 
+    def further(self):
         self.gain().start()
-        for item in self.keep():
-            item.start()
-
-    def further(self):
+        self.gain_keep().start()
+
         @pl.when(self.home)
         def _():
             self.rows_across().wait_recv()
             self.rows_further().start()
-            for item in self.keep_home():
-                item.wait()
+            self.rows_keep().wait()
+            self.note_keep().wait()
 
         @pl.when(jnp.logical_not(self.home))
         def _():
@@ -547,18 +635,7 @@
             self.rows_beside().wait_recv()
             self.rows_further().wait_recv()
 
-        for item in self.keep():
-            item.wait()
-
-    def later(self):
-        @pl.when(self.home)
-        def _():
-            self.cot_beside().start()
-
-        @pl.when(jnp.logical_not(self.home))
-        def _():
-            self.cot_across().start()
-            self.cot_corner().start()
+        self.gain_keep().wait()
 
     def finish(self):
         self.gain().wait()
@@ -568,16 +645,49 @@
             self.note().wait_send()
             self.rows_beside().wait_send()
             self.rows_further().wait_send()
-            self.cot_beside().wait_send()
-            self.cot_across().wait_recv()
 
         @pl.when(jnp.logical_not(self.home))
         def _():
             self.rows_across().wait_send()
-            self.cot_across().wait_send()
-            self.cot_corner().wait_send()
-            self.cot_beside().wait_recv()
-            self.cot_corner().wait_recv()
+
+
+class Pull:
+    def __init__(self, links, source, target, send, recv, base, local):
+        n = self.links = links
+        half = source.shape[0] // 2
+        self.home = n.x == n.c
+        s, r = (lambda k: send.at[base + k]), (lambda k: recv.at[base + k])
+        mine, theirs = source.at[pl.ds(n.c * half, half)], source.at[pl.ds((1 - n.c) * half, half)]
+        near = target.at[n.x]
+        self.keep = lambda: pltpu.make_async_copy(mine, near, local)
+        self.beside = lambda: remote(theirs, near, s(0), r(0), n.sibling)
+        self.across = lambda: remote(mine, near, s(1), r(1), n.across)
+        self.corner = lambda: remote(theirs, near, s(2), r(2), n.corner)
+
+    def begin(self):
+        @pl.when(self.home)
+        def _():
+            self.keep().start()
+            self.beside().start()
+
+        @pl.when(jnp.logical_not(self.home))
+        def _():
+            self.across().start()
+            self.corner().start()
+
+    def finish(self):
+        @pl.when(self.home)
+        def _():
+            self.keep().wait()
+            self.beside().wait_send()
+            self.across().wait_recv()
+
+        @pl.when(jnp.logical_not(self.home))
+        def _():
+            self.across().wait_send()
+            self.corner().wait_send()
+            self.beside().wait_recv()
+            self.corner().wait_recv()
 
 
 def plus(left, right):
@@ -608,26 +718,30 @@
 
     def copy(self, kind, step=0):
         n = self.links
-        corner = self.held.at[1 - n.x, :, 1 - n.y]
         if kind == "sibling" and self.kind == "join":
             return self.move(self.part.at[:, :, :, 1 - n.c], self.other, 0, n.sibling)
         if kind == "sibling":
             return self.move(self.part.at[:, :, 1 - n.c], self.held.at[n.c], 0, n.sibling)
         if kind == "x1":
-            return self.move(self.low(corner), self.x1, 1, n.across)
+            return self.move(self.low(self.held.at[1 - n.x, :, 1 - n.y]), self.x1, 1, n.across)
         if kind == "y1":
-            return self.move(self.high(corner), self.y1, 2, n.beside)
+            return self.move(self.high(self.held.at[1 - n.x, :, 1 - n.y]), self.y1, 2, n.beside)
+        source = self.part if self.kind == "later" else self.held
         if kind == "y2":
-            return self.move(self.held.at[n.x, :, 1 - n.y], self.y2, 3, n.beside)
+            return self.move(source.at[n.x, :, 1 - n.y], self.y2, 3, n.beside)
         if kind == "x2":
-            return self.move(self.held.at[1 - n.x, :, n.y], self.x2, 4, n.across)
+            return self.move(source.at[1 - n.x, :, n.y], self.x2, 4, n.across)
         q = lax.rem(n.q + step, n.depth)
-        return self.move(self.held.at[n.x, q, n.y], self.z.at[step - 1], 4 + step, n.far(step))
+        return self.move(self.mine(q), self.z.at[step - 1], 4 + step, n.far(step))
+
+    def mine(self, q):
+        n = self.links
+        return self.held.at[q] if self.kind == "later" else self.held.at[n.x, q, n.y]
 
     def keep(self):
         n = self.links
-        if self.kind == "held":
-            return pltpu.make_async_copy(self.part, self.held, self.local)
+        if self.kind == "later":
+            return pltpu.make_async_copy(self.part.at[n.x, :, n.y], self.held, self.local)
         if self.kind == "join":
             return pltpu.make_async_copy(self.part.at[:, :, :, n.c], self.held, self.local)
         return pltpu.make_async_copy(self.part.at[:, :, n.c], self.held.at[n.c], self.local)
@@ -637,8 +751,11 @@
 
     def begin(self):
         self.keep().start()
-        if self.kind != "held":
+        if self.kind != "later":
             self.copy("sibling").start()
+        else:
+            self.copy("x2").start()
+            self.copy("y2").start()
 
     def first(self):
         n = self.links
@@ -669,44 +786,47 @@
 
     def third(self):
         n = self.links
+        if self.kind == "later":
+            self.keep().wait()
         self.arrived(self.y2, 3)
         self.arrived(self.x2, 4)
         for step in range(1, n.depth):
             q = lax.rem(n.q + step, n.depth)
-            self.held[n.x, q, n.y] = plus(plus(self.held[n.x, q, n.y], self.x2[q]), self.y2[q])
+            mine = self.mine(q)
+            mine[...] = plus(plus(mine[...], self.x2[q]), self.y2[q])
             self.copy("z", step).start()
 
     def fourth(self):
         n = self.links
         total = (
-            self.held[n.x, n.q, n.y].astype(WIDE)
+            self.mine(n.q)[...].astype(WIDE)
             + self.x2[n.q].astype(WIDE)
             + self.y2[n.q].astype(WIDE)
         )
         for step in range(1, n.depth):
             self.arrived(self.z.at[step - 1], 4 + step)
             total = total + self.z[step - 1].astype(WIDE)
-        self.out[...] = total
+        self.out(total)
 
     def close(self):
-        if self.kind != "held":
-            self.copy("sibling").wait_send()
-        for kind in ("x1", "y1", "x2", "y2"):
+        first = () if self.kind == "later" else ("sibling", "x1", "y1")
+        for kind in first + ("x2", "y2"):
             self.copy(kind).wait_send()
         for step in range(1, self.links.depth):
             self.copy("z", step).wait_send()
 
 
-def scatter_scratch(depth, r, columns, cut, join=False, kind=LOW):
-    small = (1, 1, 1, 8, 128)
+def scatter_scratch(depth, r, columns, cut, kind="swap", of=LOW):
+    small = (8, 128)
+    later = kind == "later"
     return [
-        pltpu.VMEM((2, depth, 2, r, columns), kind),
-        pltpu.VMEM((2, depth, 2, r, columns) if join else small, kind),
-        pltpu.VMEM((depth, r, cut), kind),
-        pltpu.VMEM((depth, r, columns - cut), kind),
-        pltpu.VMEM((depth, r, columns), kind),
-        pltpu.VMEM((depth, r, columns), kind),
-        pltpu.VMEM((depth - 1, r, columns), kind),
+        pltpu.VMEM((depth, r, columns) if later else (2, depth, 2, r, columns), of),
+        pltpu.VMEM((2, depth, 2, r, columns) if kind == "join" else small, of),
+        pltpu.VMEM(small if later else (depth, r, cut), of),
+        pltpu.VMEM(small if later else (depth, r, columns - cut), of),
+        pltpu.VMEM((depth, r, columns), of),
+        pltpu.VMEM((depth, r, columns), of),
+        pltpu.VMEM((depth - 1, r, columns), of),
     ]
 
 
@@ -779,7 +899,9 @@
 
 
 def turn_parts(meta, base, jump, block):
-    offset = meta[0, SPAN + block]
+    segment = meta[0, block]
+    earlier = [(meta[0, other] < segment).astype(jnp.int32) for other in range(SPAN)]
+    offset = block - sum(earlier)
     far_cos = jump[pl.ds(offset, 1), :]
     far_sin = jump[pl.ds(SPAN + offset, 1), :]
     near_cos, near_sin = base[0:BLOCK], base[BLOCK : 2 * BLOCK]
@@ -806,9 +928,10 @@
     ]
 
 
-def forward_kernel(depth, cuts, note_in, gain_in, cot_in, in_ref, q_own, m_own, o_own, base, jump,
-                   note, gain, cot, rows, q_full, m_full, o_full, all_context, q_ref, k_ref, v_ref,
-                   p_ref, r_ref, c_ref, marks, meta, held, weight, piece, send, recv, local, extra_send,
+def forward_kernel(depth, cuts, note_in, in_ref, gain1, gain2, gain3, gain4, query, key, value, output,
+                   inner, o_own, base, jump,
+                   note, gain, rows, q_full, m_full, o_full, all_context, q_ref, k_ref, v_ref,
+                   p_ref, r_ref, c_ref, marks, meta, held, weight, gain_in, q_own, m_own, piece, send, recv, local, extra_send,
                    extra_recv, context_send, context_recv):
     step = pl.program_id(0)
     scale = HEAD_DIM ** (-0.5)
@@ -821,9 +944,9 @@
         )
     ]
     share = Share(
-        n, in_ref, rows, cot_in, cot, note_in, note, gain_in, gain, extra_send, extra_recv,
-        local.at[pl.ds(3, 4)],
-    )
+        n, in_ref, held, note_in, note, gain_in, gain, extra_send, extra_recv, local.at[pl.ds(3, 3)]
+    )
+    rows_keep = lambda: pltpu.make_async_copy(held, rows, local.at[7])
 
     def context_copy(p):
         there = c_ref.at[p, pl.ds((1 - n.c) * half, half)]
@@ -835,36 +958,43 @@
 
     @pl.when(step == 0)
     def _():
+        for k, item in enumerate((gain1, gain2, gain3, gain4)):
+            gain_in[k : k + 1] = item[...].reshape(1, -1)
+            gain_in[4 + k : 5 + k] = item[...].reshape(1, -1)
+        for p in range(3):
+            for k, item in enumerate((query, key, value)):
+                column = p * 384 + k * 128
+                q_own[:, column : column + 128] = item[:, p * 128 : (p + 1) * 128]
+        m_own[:, 0 : output.shape[1]] = output[...]
+        m_own[:, output.shape[1] :] = inner[...]
         n.meet()
+        gathers[0].begin()
         share.begin()
-        gathers[0].begin()
+        gathers[1].begin_far()
+        gathers[2].begin_far()
         for k in range(1, depth):
             gathers[0].second(k)
         for k in range(depth):
             gathers[0].third(k)
-        gathers[1].begin()
+        gathers[1].begin_near()
+        gathers[2].begin_near()
         share.further()
-        loads = [
-            pltpu.make_async_copy(rows, held, local.at[7]),
-            pltpu.make_async_copy(note, meta, local.at[8]),
-        ]
-        for item in loads:
-            item.start()
+        rows_keep().start()
+        loads = [pltpu.make_async_copy(note, meta, local.at[8])]
+        loads[0].start()
         gathers[0].fourth()
         gathers[0].finish()
         loads += weight_loads(q_full, n.c, weight, piece)
-        for item in loads[2:]:
+        for item in loads[1:]:
             item.start()
         for item in loads:
             item.wait()
 
     hooks = {
-        1: [gathers[2].begin],
         2: [functools.partial(gathers[1].second, k) for k in range(1, depth)],
-        5: [functools.partial(gathers[1].third, k) for k in range(depth)],
-        6: [functools.partial(gathers[2].second, k) for k in range(1, depth)] + [share.later],
-        8: [gathers[1].fourth],
-        9: [functools.partial(gathers[2].third, k) for k in range(depth)],
+        4: [functools.partial(gathers[2].second, k) for k in range(1, depth)],
+        6: [functools.partial(gathers[1].third, k) for k in range(depth)],
+        10: [gathers[1].fourth],
     }
     for at, actions in hooks.items():
 
@@ -923,23 +1053,24 @@
 
     @pl.when(step == 4 * SPAN - 1)
     def _():
-        gathers[2].fourth()
         gathers[1].finish()
-        gathers[2].finish()
-        for item in gathers:
-            item.close()
+        gathers[2].halfway()
+        gathers[0].close()
+        gathers[1].close()
         share.finish()
+        rows_keep().wait()
         for p in range(3):
             context_copy(p).wait()
             context_keep(p).wait()
 
 
-def forward_call(depth, cuts, note, gain, cot, rows, q_own, m_own, o_own, base, jump):
+def forward_call(depth, cuts, note, gains, rows, weights, base, jump):
     length, part = rows.shape
     half = length // 2
-    r = q_own.shape[0]
+    r, hidden = weights[-1].shape
+    columns = (3 * part, part + hidden, hidden)
     low = lambda *shape: jax.ShapeDtypeStruct(shape, LOW)
-    full = [low(2, depth, 2, 2, r, own.shape[1]) for own in (q_own, m_own, o_own)]
+    full = [low(2, depth, 2, 2, r, item) for item in columns]
     trio = low(3, length, 128)
     vmem = pl.BlockSpec(memory_space=pltpu.VMEM)
     marks = pltpu.SemaphoreType.DMA((3, gather_marks(depth)))
@@ -948,8 +1079,7 @@
         grid=(SPAN + 3 * SPAN,),
         out_shape=[
             jax.ShapeDtypeStruct(note.shape, note.dtype),
-            jax.ShapeDtypeStruct((2,) + gain.shape, WIDE),
-            low(2, half, part),
+            jax.ShapeDtypeStruct((2, 8, part), WIDE),
             low(2, length, part),
         ]
         + full
@@ -962,8 +1092,8 @@
             jax.ShapeDtypeStruct((3, length, 128), WIDE),
             trio,
         ],
-        in_specs=[ANY] * 7 + [vmem] * 2,
-        out_specs=[ANY] * 8
+        in_specs=[ANY] * 2 + [once(item.shape) for item in (*gains, *weights, base, jump)],
+        out_specs=[ANY] * 7
         + [vmem] * 3
         + [
             pl.BlockSpec((1, 2, BLOCK, length), lambda s: (jnp.maximum(s - SPAN, 0), 0, 0, 0)),
@@ -974,7 +1104,10 @@
             pltpu.VMEM((length, 128), LOW),
             pltpu.SMEM(note.shape, note.dtype),
             pltpu.VMEM((2, length, part), LOW),
-            pltpu.VMEM((4 * depth * r, q_own.shape[1]), LOW),
+            pltpu.VMEM((4 * depth * r, columns[0]), LOW),
+            pltpu.VMEM((8, part), WIDE),
+            pltpu.VMEM((r, columns[0]), LOW),
+            pltpu.VMEM((r, columns[1]), LOW),
             pltpu.SemaphoreType.DMA((4 * depth,)),
             marks,
             marks,
@@ -988,7 +1121,7 @@
             collective_id=0, has_side_effects=True, vmem_limit_bytes=60 * MEGA
         ),
         name="attend",
-    )(note, gain, cot, rows, q_own, m_own, o_own, base, jump)
+    )(note, rows, *gains, *weights, base, jump)
 
 
 def norm_of(summed):
@@ -1008,9 +1141,9 @@
 HIDDEN = 512
 
 
-def middle_kernel(depth, context, rows, cot, gains, m_full, o_full, lo_ref, gfs_ref, sums, grads,
-                  o_held, m_held, m_mat, o_mat, act, gi, fl, gm, ga, gc, slopes, o_part, m_part,
-                  o_other, m_other, local, send, recv):
+def middle_kernel(depth, cuts, context, rows, gains, cot_in, m_full, o_full, lo_out, gfs_ref, sums, grads,
+                  o_held, m_held, m_mat, o_mat, act, gi, fl, gm, ga, gc, n1, n2, scales, cot, lo,
+                  o_part, m_part, o_other, m_other, ox, oy, mx, my, local, send, recv, load):
     step = pl.program_id(0)
     tile, part = rows.shape[1:]
     half = fl.shape[0]
@@ -1019,11 +1152,11 @@
     pieces = o_mat.shape[2] // HIDDEN
     width = pieces * HIDDEN
     n = Links(depth)
-    here = pl.ds(step * tile, tile)
-    loads = lambda: (
-        pltpu.make_async_copy(m_full, m_mat, local.at[0]),
-        pltpu.make_async_copy(o_full, o_mat, local.at[1]),
-    )
+    here = pl.ds(lax.rem(step, tiles) * tile, tile)
+    pull = Pull(n, cot_in, cot, send, recv, 5, local.at[7])
+    lo_over = HandOver(n, lo, lo_out, send, recv, 8, local.at[8])
+    finish = Finish(n, o_full, o_mat, cuts[0], send, recv, 15, load)
+    m_load = lambda: pltpu.make_async_copy(m_full, m_mat, local.at[0])
 
     def grads_keep():
         own = grads.at[:, pl.ds(n.c * half, half)]
@@ -1033,31 +1166,53 @@
         own = grads.at[:, pl.ds(n.c * half, half)]
         return remote(gc.at[1 - n.c], own, send.at[4], recv.at[4], n.sibling)
 
+    order = ((0, 1 - n.x), (1, 1 - n.x), (0, n.x), (1, n.x))
+    chunks = ((o_part, o_other, ox, oy, o_held), (m_part, m_other, mx, my, m_held))
+
     def part_copy(k):
-        source, target = ((o_part, o_other) if k < 2 else (m_part, m_other))
-        h = k % 2
+        chunk, h = order[k]
+        source, target = chunks[chunk][:2]
         return remote(
             source.at[h, :, :, 1 - n.c], target.at[h], send.at[k], recv.at[k], n.sibling
         )
 
     def join(k):
-        source, target = ((o_part, o_other) if k < 2 else (m_part, m_other))
-        h = k % 2
+        chunk, h = order[k]
+        source, target = chunks[chunk][:2]
         part_copy(k).wait_recv()
         for q in range(depth):
             for y in range(2):
                 target[h, q, y] = plus(source[h, q, y, n.c], target[h, q, y])
 
-    def held_copy(k):
-        source, target = ((o_other, o_held) if k < 2 else (m_other, m_held))
-        return pltpu.make_async_copy(source.at[k % 2], target.at[k % 2], local.at[3 + k])
+    def hop(chunk, across):
+        target, x1, y1 = chunks[chunk][1:4]
+        corner = target.at[1 - n.x, :, 1 - n.y]
+        mark = 11 + 2 * chunk + across
+        if across:
+            part = corner.at[:, :, pl.ds(0, x1.shape[-1])]
+            return remote(part, x1, send.at[mark], recv.at[mark], n.across)
+        part = corner.at[:, :, pl.ds(x1.shape[-1], y1.shape[-1])]
+        return remote(part, y1, send.at[mark], recv.at[mark], n.beside)
+
+    def land(chunk):
+        target, x1, y1, held = chunks[chunk][1:5]
+        low, high = pl.ds(0, x1.shape[-1]), pl.ds(x1.shape[-1], y1.shape[-1])
+        hop(chunk, True).wait_recv()
+        hop(chunk, False).wait_recv()
+        for q in range(depth):
+            target[n.x, q, 1 - n.y, :, low] = plus(target[n.x, q, 1 - n.y, :, low], x1[q])
+            target[1 - n.x, q, n.y, :, high] = plus(target[1 - n.x, q, n.y, :, high], y1[q])
+
+    def held_copy(chunk):
+        return pltpu.make_async_copy(chunks[chunk][1], chunks[chunk][4], local.at[3 + chunk])
 
     @pl.when(step == 0)
     def _():
-        for item in loads():
-            item.start()
-        n.meet(True)
-        loads()[0].wait()
+        m_load().start()
+        n.meet()
+        finish.begin()
+        pull.begin()
+        m_load().wait()
 
     @pl.when(step < tiles)
     def _():
@@ -1068,6 +1223,8 @@
             seen = jnp.concatenate([context[h, p, here] for p in range(3)], axis=1)
             summed = summed + contract(seen, m_mat[h, :, 0:part], 1, 1)
         normed1, scale1 = norm_of(summed)
+        n1[here] = normed1
+        scales[here, 0:1] = scale1
         first = normed1 * gain1 + bias1
         first_low = first.astype(LOW)
         fl[here] = first_low
@@ -1077,21 +1234,41 @@
                 there = slice(h * width + j * HIDDEN, h * width + (j + 1) * HIDDEN)
                 inner = contract(first_low, m_mat[h, :, lo_end : lo_end + HIDDEN], 1, 0)
                 share = 0.5 * (1.0 + lax.erf(inner * ROOT_HALF))
-                slopes[:, there] = share + inner * jnp.exp(-0.5 * inner * inner) * INVERSE_ROOT
+                slope = share + inner * jnp.exp(-0.5 * inner * inner) * INVERSE_ROOT
+                gi[here, there] = slope.astype(LOW)
                 act[here, there] = (inner * share).astype(LOW)
 
-        @pl.when(step == 0)
-        def _():
-            loads()[1].wait()
-
-        mixed = first
+    @pl.when(step == tiles)
+    def _():
+        finish.fourth()
+        finish.finish()
+
+    @pl.when((step >= tiles) & (step < 2 * tiles))
+    def _():
+        whole = jnp.concatenate([gains[0], gains[1]], axis=1)
+        gain1, bias1, gain2, bias2 = (whole[k : k + 1, :] for k in range(4))
+        mixed = n1[here] * gain1 + bias1
         for h in range(2):
             mixed = mixed + contract(act[here, h * width : (h + 1) * width], o_mat[h], 1, 1)
         normed2, scale2 = norm_of(mixed)
+        n2[here] = normed2
+        scales[here, 1:2] = scale2
         result = (normed2 * gain2 + bias2).astype(LOW)
         for h in range(2):
-            lo_ref[h] = result[:, h * part : (h + 1) * part]
-        cotangent = jnp.concatenate([cot[0], cot[1]], axis=1).astype(WIDE)
+            lo[h, here] = result[:, h * part : (h + 1) * part]
+
+    @pl.when(step == 2 * tiles)
+    def _():
+        pull.finish()
+        lo_over.begin()
+
+    @pl.when((step >= 2 * tiles) & (step < 3 * tiles))
+    def _():
+        whole = jnp.concatenate([gains[0], gains[1]], axis=1)
+        gain1, bias1, gain2, bias2 = (whole[k : k + 1, :] for k in range(4))
+        normed1, scale1 = n1[here], scales[here, 0:1]
+        normed2, scale2 = n2[here], scales[here, 1:2]
+        cotangent = jnp.concatenate([cot[0, here], cot[1, here]], axis=1).astype(WIDE)
         second_gain = jnp.sum(cotangent * normed2, axis=0, keepdims=True)
         second_bias = jnp.sum(cotangent, axis=0, keepdims=True)
         grad_second = norm_back(cotangent * gain2, normed2, scale2)
@@ -1101,7 +1278,7 @@
             for j in range(pieces):
                 there = slice(h * width + j * HIDDEN, h * width + (j + 1) * HIDDEN)
                 raised = contract(grad_mixed, o_mat[h, :, j * HIDDEN : (j + 1) * HIDDEN], 1, 0)
-                gi[here, there] = (raised * slopes[:, there]).astype(LOW)
+                gi[here, there] = (raised * gi[here, there].astype(WIDE)).astype(LOW)
         grad_first = grad_second
         for h in range(2):
             grad_first = grad_first + contract(
@@ -1119,15 +1296,15 @@
                 gc[h, p, here] = made[:, p * 128 : (p + 1) * 128]
         found = jnp.concatenate([first_gain, first_bias, second_gain, second_bias], axis=0)
 
-        @pl.when(step == 0)
+        @pl.when(step == 2 * tiles)
         def _():
             sums[...] = found
 
-        @pl.when(step > 0)
+        @pl.when(step > 2 * tiles)
         def _():
             sums[...] += found
 
-    @pl.when(step == tiles - 1)
+    @pl.when(step == 3 * tiles - 1)
     def _():
         grads_keep().start()
         grads_copy().start()
@@ -1142,35 +1319,46 @@
 
     for k in range(4):
 
-        @pl.when(step == tiles + k)
-        def _():
-            h = k % 2
-            target = o_part if k < 2 else m_part
+        @pl.when(step == 3 * tiles + k)
+        def _():
+            chunk, h = order[k]
+            target = chunks[chunk][0]
             for row in range(0, 2 * part, part):
                 for j in range(pieces):
-                    there = slice(h * width + j * HIDDEN, h * width + (j + 1) * HIDDEN)
-                    if k < 2:
+                    start = pl.multiple_of(h * width + j * HIDDEN, HIDDEN)
+                    there = pl.ds(start, HIDDEN)
+                    if chunk == 0:
                         made = contract(gm[:, row : row + part], act[:, there], 0, 0)
                         put(target, h, row, j * HIDDEN, made.astype(LOW))
                     else:
                         made = contract(fl[:, row : row + part], gi[:, there], 0, 0)
                         put(target, h, row, part + j * HIDDEN, made.astype(LOW))
-                if k >= 2:
+                if chunk == 1:
                     seen = jnp.concatenate([context[h, p] for p in range(3)], axis=1)
                     made = contract(ga[:, row : row + part], seen, 0, 0)
                     put(target, h, row, 0, made.astype(LOW))
             part_copy(k).start()
             if k:
                 join(k - 1)
-                held_copy(k - 1).start()
+            if k in (1, 2):
+                hop(k - 1, True).start()
+                hop(k - 1, False).start()
             if k == 3:
+                land(0)
+                held_copy(0).start()
                 join(3)
-                held_copy(3).start()
-                for item in range(4):
-                    held_copy(item).wait()
-                    part_copy(item).wait_send()
+                land(1)
+                held_copy(1).start()
                 grads_keep().wait()
                 grads_copy().wait()
+                for item in range(4):
+                    part_copy(item).wait_send()
+                for item in range(2):
+                    hop(item, True).wait_send()
+                    hop(item, False).wait_send()
+                    held_copy(item).wait()
+                lo_over.finish()
+                finish.close()
 
 
 def once(shape):
@@ -1178,23 +1366,24 @@
     return pl.BlockSpec(shape, lambda *_: zeros, pipeline_mode=pl.Buffered(1))
 
 
-def middle_call(depth, context, rows, cot, m_full, o_full, gains):
+def middle_call(depth, cuts, context, rows, cot, m_full, o_full, gains):
     tile = 256
-    half, part = cot.shape[1:]
+    half, part = cot.shape[0] // 2, cot.shape[1]
     tiles = half // tile
     width = 2 * part
-    hidden = 2 * o_full.shape[2]
+    hidden = 2 * o_full.shape[-1]
     r = width // (4 * depth)
-    columns = (o_full.shape[2], m_full.shape[2])
+    columns = (o_full.shape[-1], m_full.shape[2])
     low = lambda *shape: jax.ShapeDtypeStruct(shape, LOW)
     held = [(2, depth, 2, r, item) for item in columns]
     last = lambda i: jnp.minimum(i, tiles - 1)
+    later = lambda i: jnp.clip(i - 2 * tiles, 0, tiles - 1)
     c = lambda: lax.rem(lax.axis_index("wide"), 2)
     return pl.pallas_call(
-        functools.partial(middle_kernel, depth),
-        grid=(tiles + 4,),
+        functools.partial(middle_kernel, depth, cuts),
+        grid=(3 * tiles + 4,),
         out_shape=[
-            low(2, half, part),
+            low(2 * half, part),
             jax.ShapeDtypeStruct((half, width), WIDE),
             jax.ShapeDtypeStruct((4, width), WIDE),
             low(3, 2 * half, 128),
@@ -1203,14 +1392,14 @@
         in_specs=[
             once((2, 3, half, 128)),
             pl.BlockSpec((2, tile, part), lambda i: (0, c() * tiles + last(i), 0)),
-            pl.BlockSpec((2, tile, part), lambda i: (0, last(i), 0)),
             once(gains.shape),
+            ANY,
             ANY,
             ANY,
         ],
         out_specs=[
-            pl.BlockSpec((2, tile, part), lambda i: (0, last(i), 0)),
-            pl.BlockSpec((tile, width), lambda i: (last(i), 0)),
+            ANY,
+            pl.BlockSpec((tile, width), lambda i: (later(i), 0)),
             pl.BlockSpec((4, width), lambda i: (0, 0)),
             ANY,
             ANY,
@@ -1218,32 +1407,42 @@
         ],
         scratch_shapes=[
             pltpu.VMEM(m_full.shape, LOW),
-            pltpu.VMEM(o_full.shape, LOW),
+            pltpu.VMEM((2, width, columns[0]), LOW),
             pltpu.VMEM((half, hidden), LOW),
             pltpu.VMEM((half, hidden), LOW),
             pltpu.VMEM((half, width), LOW),
             pltpu.VMEM((half, width), LOW),
             pltpu.VMEM((half, width), LOW),
             pltpu.VMEM((2, 3, half, 128), LOW),
-            pltpu.VMEM((tile, hidden), WIDE),
+            pltpu.VMEM((half, width), WIDE),
+            pltpu.VMEM((half, width), WIDE),
+            pltpu.VMEM((half, 2), WIDE),
+            pltpu.VMEM((2, half, part), LOW),
+            pltpu.VMEM((2, half, part), LOW),
         ]
         + [pltpu.VMEM((2, depth, 2, 2, r, item), LOW) for item in columns]
         + [pltpu.VMEM(item, LOW) for item in held]
         + [
-            pltpu.SemaphoreType.DMA((7,)),
-            pltpu.SemaphoreType.DMA((5,)),
-            pltpu.SemaphoreType.DMA((5,)),
+            pltpu.VMEM((depth, r, item), LOW)
+            for whole, cut in zip(columns, cuts)
+            for item in (cut, whole - cut)
+        ]
+        + [
+            pltpu.SemaphoreType.DMA((9,)),
+            pltpu.SemaphoreType.DMA((15 + 6 * depth,)),
+            pltpu.SemaphoreType.DMA((15 + 6 * depth,)),
+            pltpu.SemaphoreType.DMA((3 * depth,)),
         ],
         compiler_params=pltpu.CompilerParams(
             collective_id=1, has_side_effects=True, vmem_limit_bytes=62 * MEGA
         ),
         name="middle",
-    )(context, rows, cot, gains, m_full, o_full)
+    )(context, rows, gains, cot, m_full, o_full)
 
 
 def backward_kernel(depth, cuts, meta, base, jump, soft, grads, context, inverse, q_ref, k_ref, v_ref,
-                    rows, kept, q_full, lo_in, o_in, m_in, t_in, lo_out, dx_out, o_out, m_out, q_out,
-                    t_out, *scratch):
+                    rows, kept, q_full, o_in, m_in, t_in, dx_out, o_out, m_out,
+                    i_out, q_out, k_out, v_out, t_out, *scratch):
     ones, keys_sum, values_sum, made, weight, q_part, dx_own, dx_give, dx_other = scratch[:9]
     bufs = [scratch[9 + 7 * k : 16 + 7 * k] for k in range(6)]
     piece, send, recv, local, extra_send, extra_recv = scratch[51:]
@@ -1258,42 +1457,51 @@
     r = o_in.shape[-2]
     half, width = kept.shape
     part = width // 2
-    kinds = ("held", "held", "swap", "swap", "swap", "join")
+    kinds = ("later", "later", "swap", "swap", "swap", "join")
     parts = (o_in, m_in) + tuple(q_part.at[k] for k in range(3)) + (t_in,)
-    outs = (o_out, m_out) + tuple(q_out.at[k] for k in range(3)) + (t_out,)
+
+    def put_pair(p, total):
+        for k, item in enumerate((q_out, k_out, v_out)):
+            item[:, p * 128 : (p + 1) * 128] = total[:, k * 128 : (k + 1) * 128]
+
+    def put_whole(target, total):
+        target[...] = total
+
+    def put_inner(total):
+        m_out[...] = total[:, 0:part]
+        i_out[...] = total[:, part:]
+
+    outs = [functools.partial(put_whole, o_out), put_inner]
+    outs += [functools.partial(put_pair, k) for k in range(3)]
+    outs += [functools.partial(put_whole, t_out)]
     every = [
         Scatter(n, kind, item, cut, buf, out, send, recv, k, local.at[k])
         for k, (kind, item, cut, buf, out) in enumerate(zip(kinds, parts, cuts, bufs, outs))
     ]
     outer, inner, pair0, pair1, pair2, small = every
-    lo_over = HandOver(n, lo_in, lo_out, extra_send, extra_recv, 0, local.at[6])
-    dx_over = HandOver(n, dx_own, dx_out, extra_send, extra_recv, 3, local.at[7])
-    dx_swap = lambda: remote(dx_give, dx_other, extra_send.at[6], extra_recv.at[6], n.sibling)
+    dx_over = HandOver(n, dx_own, dx_out, extra_send, extra_recv, 0, local.at[6])
+    dx_swap = lambda: remote(dx_give, dx_other, extra_send.at[3], extra_recv.at[3], n.sibling)
 
     @pl.when(step == 0)
     def _():
         ones[...] = (lanes(length) < 2).astype(WIDE).astype(LOW)
         for item in weight_loads(q_full, n.c, weight, piece):
             item.start()
+        n.meet()
+        small.begin()
+        small.first()
         outer.begin()
         inner.begin()
-        n.meet()
-        small.begin()
-        outer.first()
-        inner.first()
-        small.first()
         for item in weight_loads(q_full, n.c, weight, piece):
             item.wait()
 
     hooks = {
-        1: [outer.second, small.second, lo_over.begin],
-        2: [inner.second, small.third],
-        3: [small.fourth, pair0.first],
-        4: [outer.third, pair0.second],
-        5: [pair0.third],
-        6: [inner.third, outer.fourth, pair1.first],
-        7: [pair1.second, pair0.fourth],
-        8: [pair1.third, inner.fourth],
+        1: [small.second],
+        3: [outer.third, pair0.first],
+        5: [inner.third, small.third],
+        6: [outer.fourth, pair0.second, pair1.first],
+        7: [pair0.third, pair1.second],
+        8: [pair1.third, inner.fourth, small.fourth],
     }
     for at, actions in hooks.items():
 
@@ -1384,17 +1592,17 @@
             dx_own[h] = plus(dx_own[h], dx_other[h])
         dx_over.begin()
         pair2.third()
+        pair0.fourth()
         pair1.fourth()
         pair2.fourth()
         for item in every:
             item.close()
         dx_swap().wait_send()
-        lo_over.finish()
         dx_over.finish()
 
 
 def backward_call(depth, cuts, meta, base, jump, soft, grads, context, inverse, q, k, v, rows, kept,
-                  q_full, lo, o_held, m_held, t_part):
+                  q_full, o_held, m_held, t_part):
     length = q.shape[1]
     half, width = kept.shape
     part = width // 2
@@ -1403,7 +1611,8 @@
     low = lambda *shape: jax.ShapeDtypeStruct(shape, LOW)
     widths = (o_held.shape[-1], m_held.shape[-1])
     shape = lambda *item: jax.ShapeDtypeStruct(item, WIDE)
-    outs = [shape(r, widths[0]), shape(r, widths[1]), shape(3, r, 384), shape(*t_part.shape[-2:])]
+    outs = [shape(r, widths[0]), shape(r, part), shape(r, widths[1] - part)]
+    outs += [shape(r, part)] * 3 + [shape(*t_part.shape[-2:])]
     scratch = [
         pltpu.VMEM((length, 128), LOW),
         pltpu.VMEM((128, length), WIDE),
@@ -1416,13 +1625,13 @@
         pltpu.VMEM((2, half, part), LOW),
     ]
     for at, columns in enumerate(widths + (384,) * 3):
-        scratch += scatter_scratch(depth, r, columns, cuts[at])
-    scratch += scatter_scratch(depth, t_part.shape[-2], t_part.shape[-1], cuts[5], True, WIDE)
+        scratch += scatter_scratch(depth, r, columns, cuts[at], "later" if at < 2 else "swap")
+    scratch += scatter_scratch(depth, t_part.shape[-2], t_part.shape[-1], cuts[5], "join", WIDE)
     marks = pltpu.SemaphoreType.DMA((6, scatter_marks(depth)))
     return pl.pallas_call(
         functools.partial(backward_kernel, depth, cuts),
         grid=(3 * SPAN,),
-        out_shape=[low(2 * half, part)] * 2 + outs,
+        out_shape=[low(2 * half, part)] + outs,
         in_specs=[
             pl.BlockSpec(memory_space=pltpu.SMEM),
             once(base.shape),
@@ -1437,8 +1646,8 @@
             once(rows.shape),
             once(kept.shape),
         ]
-        + [ANY] * 5,
-        out_specs=[ANY] * 2 + [once(item.shape) for item in outs],
+        + [ANY] * 4,
+        out_specs=[ANY] + [once(item.shape) for item in outs],
         scratch_shapes=scratch
         + [
             pltpu.SemaphoreType.DMA((4 * depth,)),
@@ -1452,7 +1661,7 @@
             collective_id=2, has_side_effects=True, vmem_limit_bytes=63 * MEGA
         ),
         name="attend_back",
-    )(meta, base, jump, soft, grads, context, inverse, q, k, v, rows, kept, q_full, lo, o_held, m_held, t_part)
+    )(meta, base, jump, soft, grads, context, inverse, q, k, v, rows, kept, q_full, o_held, m_held, t_part)
 
 
 def owned(
@@ -1478,46 +1687,34 @@
     half = length // 2
     x, w, c, _, _ = place()
     pairs = part // 128
-    q_own = jnp.concatenate(
-        [
-            item[:, p * 128 : (p + 1) * 128]
-            for p in range(pairs)
-            for item in (query_weight, key_weight, value_weight)
-        ],
-        axis=1,
-    )
-    m_own = jnp.concatenate([output_weight.T, inner_weight], axis=1)
-    o_own = outer_weight.T
-    earlier = jnp.sum((block_segment[None, :] < block_segment[:, None]).astype(jnp.int32), axis=1)
-    offsets = jnp.arange(SPAN, dtype=jnp.int32) - earlier
-    meta = jnp.zeros((1, 128), jnp.int32)
-    meta = meta.at[0, 0:SPAN].set(block_segment).at[0, SPAN : 2 * SPAN].set(offsets)
-    widths = [item.shape[1] for item in (q_own, m_own, o_own)]
-    cuts = [(item // 128 // 5) * 128 for item in widths]
-    gains = jnp.stack([first_gain, first_bias, second_gain, second_bias])
-    gains = jnp.concatenate([gains, gains], axis=0)
+    meta = jnp.pad(block_segment[None], ((0, 0), (0, 128 - SPAN)))
+    hidden = inner_weight.shape[1]
+    widths = [3 * part, part + hidden, hidden]
+    cuts = [(item // 256) * 128 for item in widths]
+    cuts[0] = 128
+    gains = [first_gain, first_bias, second_gain, second_bias]
+    weights = [query_weight, key_weight, value_weight, output_weight.T, inner_weight, outer_weight.T]
     base, jump = angle_tables()
-    meta, gains, cot, rows, q_full, m_full, o_full, pairs_context, q, k, v, soft, inverse, context = (
-        forward_call(
-            depth, cuts, meta, gains, output_cotangent, inputs, q_own, m_own, o_own, base, jump
-        )
-    )
-    lo, kept, sums, grads, o_held, m_held = middle_call(
+    meta, gains, rows, q_full, m_full, o_full, pairs_context, q, k, v, soft, inverse, context = (
+        forward_call(depth, cuts, meta, gains, inputs, weights, base, jump)
+    )
+    layer_output, kept, sums, grads, o_held, m_held = middle_call(
         depth,
+        [cuts[2], cuts[1]],
         pairs_context,
         rows,
-        cot,
+        output_cotangent,
         m_full.reshape(2, 2 * part, widths[1]),
-        o_full.reshape(2, 2 * part, widths[2]),
+        o_full,
         gains,
     )
     few = 2 * part // (2 * wide)
     spots = jnp.moveaxis(sums.reshape(2, 2, 2, wide, few), (2, 3), (0, 1))
     spots = jnp.pad(jnp.moveaxis(spots, 2, 3), ((0, 0), (0, 0), (0, 6), (0, 0), (0, 128 - few)))
     spots = spots.reshape(2, depth, 2, 2, 8, 256)
-    layer_output, input_gradient, o_sum, m_sum, q_sum, found = backward_call(
+    input_gradient, o_sum, m_sum, i_sum, q_sum, k_sum, v_sum, found = backward_call(
         depth,
-        [cuts[2], cuts[1], 128, 128, 128, 128],
+        [(item // 256) * 128 for item in (widths[2], widths[1])] + [128] * 4,
         meta,
         base,
         jump,
@@ -1531,20 +1728,18 @@
         rows,
         kept,
         q_full,
-        lo,
         o_held,
         m_held,
         spots,
     )
-    q_sum = jnp.moveaxis(q_sum, 0, 1).reshape(r, pairs, 3, 128)
     return (
         layer_output,
         input_gradient,
-        q_sum[:, :, 0].reshape(r, part),
-        q_sum[:, :, 1].reshape(r, part),
-        q_sum[:, :, 2].reshape(r, part),
-        m_sum[:, 0:part].T,
-        m_sum[:, part:],
+        q_sum,
+        k_sum,
+        v_sum,
+        m_sum.T,
+        i_sum,
         o_sum.T,
         found[0, 0:few],
         found[1, 0:few],

time: 335 us -> 259 us (0.77); the launches traced: 331 us -> 258 us
  Pallas kernels: 300 us -> 246 us
  local copies, waits for them, and re-layouts: 23.6 us -> 11.5 us
  other arithmetic: 6.51 us -> 0 us
    pallas_call x1, Pallas kernels: 130 us -> 87.3 us  [forward_call(): pl.pallas_call(functools.partial(forward_kernel, depth, cuts), grid=(SPAN...]
    pallas_call x1, Pallas kernels: 121 us -> 93.1 us  [backward_call(): pl.pallas_call(functools.partial(backward_kernel, depth, cuts), grid=(3 *...]
    pallas_call x1, Pallas kernels: 48.2 us -> 65.7 us  [middle_call(): pl.pallas_call(functools.partial(middle_kernel, depth, cuts), grid=(3 * t...]
    another operation x6 -> x0, local copies, waits for them, and re-layouts: 3.99 us -> none  [the longest x4 2.74 us: owned(): gains = jnp.stack([first_gain, first_bias, second_gain, second_bias])]
    another operation x5 -> x0, other arithmetic: 3.96 us -> none
where the time goes in v4:
time: 259 us; the launch traced here: 258 us
  Pallas kernels  246 us (95%)
  local copies, waits for them, and re-layouts  11.5 us (4%)
    pallas_call x1, Pallas kernels, backward_call(): pl.pallas_call(functools.partial(backward_kernel, depth, cuts), grid=(3 *...  93.1 us
    pallas_call x1, Pallas kernels, forward_call(): pl.pallas_call(functools.partial(forward_kernel, depth, cuts), grid=(SPAN...  87.3 us
    pallas_call x1, Pallas kernels, middle_call(): pl.pallas_call(functools.partial(middle_kernel, depth, cuts), grid=(3 * t...  65.7 us
    unnamed x22, local copies, waits for them, and re-layouts  7.5 us

profile of v4, /device:TPU:1, one launch (start us, length us, event | category | flops | bytes accessed | tf_op | source)
XLA Modules:
  0.0 258.5 jit_solution(12472792938467720324)
XLA Ops:
  0.6 1.2 pad.8.note_in
  1.8 87.3 %attend.1 = (s32[1,128]{1,0:T(1,128)}, f32[2,8,384]{2,1,0:T(8,128)}, bf16[2,1536,384]{2,1,0:T(8,128)(2,1)}, bf16[2,4,2,2,48,1152]{5,4,3,2,1,0:T(8,128)(2,1)}, bf...) custom-call(s32[1,128]{1,0:T(1,128)} %pad.8.note_in, ...), custom_call_target="tpu_custom_call" | custom-call | tf_op jit(solution)/shard_map/attend/pallas_call | solution.py:1077
  89.2 65.7 %middle.1 = (bf16[1536,384]{1,0:T(8,128)(2,1)}, f32[768,768]{1,0:T(8,128)}, f32[4,768]{1,0:T(4,128)}, bf16[3,1536,128]{2,1,0:T(8,128)(2,1)}, bf16[2,4,2,48,1536]...) custom-call(bf16[2,3,768,128]{3,2,1,0:T(8,128)(2,1)} %get-tuple-element.39.context, ...), custom_call_target="tpu_custom_call" | custom-call | tf_op jit(solution)/shard_map/middle/pallas_call | solution.py:1382
  154.9 0.8 reshape.34
  155.7 0.1 copy.29
  155.8 0.7 pad.9
  156.5 93.1 %attend_back.1 = (bf16[1536,384]{1,0:T(8,128)(2,1)}, f32[48,1536]{1,0:T(8,128)}, f32[48,384]{1,0:T(8,128)}, f32[48,1536]{1,0:T(8,128)}, f32[48,384]{1,0:T(8,128)...) custom-call(s32[1,128]{1,0:T(1,128)} %get-tuple-element.45.meta, f32[1024,128]{1,0:T(8,128)} %constant.8.clone.base, ...), custom_call_target="tpu_custom_call" | custom-call | tf_op jit(solution)/shard_map/attend_back/pallas_call | solution.py:1631
  249.7 1.3 slice_bitcast_fusion
  250.9 0.0 copy-start
  250.9 2.5 copy.38
  253.4 0.0 copy-done
  253.4 0.0 copy-start.6
  253.5 0.0 copy-start.5
  253.5 0.0 copy-start.4
  253.5 0.0 copy-start.3
  253.5 0.0 copy-start.2
  253.5 1.0 copy.39
  254.5 0.0 copy-done.6
  254.5 0.0 copy-start.1
  254.5 0.6 copy.40
  255.1 0.0 copy-done.5
  255.1 0.6 copy.41
  255.8 0.0 copy-done.4
  255.8 0.6 copy.42
  256.4 0.0 copy-done.3
  256.4 0.6 copy.43
  257.0 0.0 copy-done.2
  257.0 0.7 copy.44
  257.8 0.0 copy-done.1
  257.8 0.7 copy.45
Async XLA Ops:
  250.9 2.5 copy-start
  253.4 1.0 copy-start.6
  253.5 1.7 copy-start.5
  253.5 2.3 copy-start.4
  253.5 2.9 %copy-start.3 = (f32[48,384]{1,0:T(8,128)S(1)}, f32[48,384]{1,0:T(8,128)}, u32[]{:S(2)}) copy-start(f32[48,384]{1,0:T(8,128)} %get-tuple-element.62) | copy-start | bytes 221188
  253.5 3.6 %copy-start.2 = (f32[48,1536]{1,0:T(8,128)S(1)}, f32[48,1536]{1,0:T(8,128)}, u32[]{:S(2)}) copy-start(f32[48,1536]{1,0:T(8,128)} %get-tuple-element.88) | copy-start | bytes 884740
  254.5 3.3 %copy-start.1 = (f32[48,1536]{1,0:T(8,128)S(1)}, f32[48,1536]{1,0:T(8,128)}, u32[]{:S(2)}) copy-start(f32[48,1536]{1,0:T(8,128)} %get-tuple-element.64) | copy-start | bytes 884740

commit v5 on v4

--- a/solution.py
+++ b/solution.py
@@ -652,14 +652,13 @@
 
 
 class Pull:
-    def __init__(self, links, source, target, send, recv, base, local):
+    def __init__(self, links, source, target, send, recv, base):
         n = self.links = links
         half = source.shape[0] // 2
         self.home = n.x == n.c
         s, r = (lambda k: send.at[base + k]), (lambda k: recv.at[base + k])
         mine, theirs = source.at[pl.ds(n.c * half, half)], source.at[pl.ds((1 - n.c) * half, half)]
         near = target.at[n.x]
-        self.keep = lambda: pltpu.make_async_copy(mine, near, local)
         self.beside = lambda: remote(theirs, near, s(0), r(0), n.sibling)
         self.across = lambda: remote(mine, near, s(1), r(1), n.across)
         self.corner = lambda: remote(theirs, near, s(2), r(2), n.corner)
@@ -667,7 +666,6 @@
     def begin(self):
         @pl.when(self.home)
         def _():
-            self.keep().start()
             self.beside().start()
 
         @pl.when(jnp.logical_not(self.home))
@@ -678,7 +676,6 @@
     def finish(self):
         @pl.when(self.home)
         def _():
-            self.keep().wait()
             self.beside().wait_send()
             self.across().wait_recv()
 
@@ -726,22 +723,21 @@
             return self.move(self.low(self.held.at[1 - n.x, :, 1 - n.y]), self.x1, 1, n.across)
         if kind == "y1":
             return self.move(self.high(self.held.at[1 - n.x, :, 1 - n.y]), self.y1, 2, n.beside)
-        source = self.part if self.kind == "later" else self.held
         if kind == "y2":
-            return self.move(source.at[n.x, :, 1 - n.y], self.y2, 3, n.beside)
+            return self.move(self.held.at[n.x, :, 1 - n.y], self.y2, 3, n.beside)
         if kind == "x2":
-            return self.move(source.at[1 - n.x, :, n.y], self.x2, 4, n.across)
+            return self.move(self.held.at[1 - n.x, :, n.y], self.x2, 4, n.across)
         q = lax.rem(n.q + step, n.depth)
         return self.move(self.mine(q), self.z.at[step - 1], 4 + step, n.far(step))
 
     def mine(self, q):
         n = self.links
-        return self.held.at[q] if self.kind == "later" else self.held.at[n.x, q, n.y]
+        return self.held.at[q] if self.kind == "last" else self.held.at[n.x, q, n.y]
 
     def keep(self):
         n = self.links
-        if self.kind == "later":
-            return pltpu.make_async_copy(self.part.at[n.x, :, n.y], self.held, self.local)
+        if self.kind in ("held", "last"):
+            return pltpu.make_async_copy(self.part, self.held, self.local)
         if self.kind == "join":
             return pltpu.make_async_copy(self.part.at[:, :, :, n.c], self.held, self.local)
         return pltpu.make_async_copy(self.part.at[:, :, n.c], self.held.at[n.c], self.local)
@@ -751,11 +747,8 @@
 
     def begin(self):
         self.keep().start()
-        if self.kind != "later":
+        if self.kind in ("join", "swap"):
             self.copy("sibling").start()
-        else:
-            self.copy("x2").start()
-            self.copy("y2").start()
 
     def first(self):
         n = self.links
@@ -786,31 +779,32 @@
 
     def third(self):
         n = self.links
-        if self.kind == "later":
+        if self.kind == "last":
             self.keep().wait()
-        self.arrived(self.y2, 3)
-        self.arrived(self.x2, 4)
+        else:
+            self.arrived(self.y2, 3)
+            self.arrived(self.x2, 4)
         for step in range(1, n.depth):
             q = lax.rem(n.q + step, n.depth)
-            mine = self.mine(q)
-            mine[...] = plus(plus(mine[...], self.x2[q]), self.y2[q])
+            if self.kind != "last":
+                mine = self.mine(q)
+                mine[...] = plus(plus(mine[...], self.x2[q]), self.y2[q])
             self.copy("z", step).start()
 
     def fourth(self):
         n = self.links
-        total = (
-            self.mine(n.q)[...].astype(WIDE)
-            + self.x2[n.q].astype(WIDE)
-            + self.y2[n.q].astype(WIDE)
-        )
+        total = self.mine(n.q)[...].astype(WIDE)
+        if self.kind != "last":
+            total = total + self.x2[n.q].astype(WIDE) + self.y2[n.q].astype(WIDE)
         for step in range(1, n.depth):
             self.arrived(self.z.at[step - 1], 4 + step)
             total = total + self.z[step - 1].astype(WIDE)
         self.out(total)
 
     def close(self):
-        first = () if self.kind == "later" else ("sibling", "x1", "y1")
-        for kind in first + ("x2", "y2"):
+        hops = ("x1", "y1", "x2", "y2")
+        hops = {"last": (), "held": hops}.get(self.kind, ("sibling",) + hops)
+        for kind in hops:
             self.copy(kind).wait_send()
         for step in range(1, self.links.depth):
             self.copy("z", step).wait_send()
@@ -818,21 +812,22 @@
 
 def scatter_scratch(depth, r, columns, cut, kind="swap", of=LOW):
     small = (8, 128)
-    later = kind == "later"
+    later = kind == "last"
     return [
         pltpu.VMEM((depth, r, columns) if later else (2, depth, 2, r, columns), of),
         pltpu.VMEM((2, depth, 2, r, columns) if kind == "join" else small, of),
         pltpu.VMEM(small if later else (depth, r, cut), of),
         pltpu.VMEM(small if later else (depth, r, columns - cut), of),
-        pltpu.VMEM((depth, r, columns), of),
-        pltpu.VMEM((depth, r, columns), of),
+        pltpu.VMEM(small if later else (depth, r, columns), of),
+        pltpu.VMEM(small if later else (depth, r, columns), of),
         pltpu.VMEM((depth - 1, r, columns), of),
     ]
 
 
 class HandOver:
-    def __init__(self, links, source, target, send, recv, base, local):
+    def __init__(self, links, source, target, send, recv, base, local, bounce=None):
         self.links, self.source, self.target, self.local = links, source, target, local
+        self.bounce = bounce
         self.send = lambda k: send.at[base + k]
         self.recv = lambda k: recv.at[base + k]
         self.half = source.shape[1]
@@ -845,7 +840,7 @@
         near, far = self.source.at[n.x], self.source.at[1 - n.x]
         mine = self.rows(n.c)
         return (
-            pltpu.make_async_copy(near, mine, self.local),
+            pltpu.make_async_copy(near if self.bounce is None else self.bounce, mine, self.local),
             remote(far, mine, self.send(0), self.recv(0), n.across),
             remote(near, mine, self.send(1), self.recv(1), n.sibling),
             remote(far, mine, self.send(2), self.recv(2), n.corner),
@@ -928,10 +923,10 @@
     ]
 
 
-def forward_kernel(depth, cuts, note_in, in_ref, gain1, gain2, gain3, gain4, query, key, value, output,
+def forward_kernel(depth, cuts, note_in, in_ref, cot_in, gain1, gain2, gain3, gain4, query, key, value, output,
                    inner, o_own, base, jump,
-                   note, gain, rows, q_full, m_full, o_full, all_context, q_ref, k_ref, v_ref,
-                   p_ref, r_ref, c_ref, marks, meta, held, weight, gain_in, q_own, m_own, piece, send, recv, local, extra_send,
+                   note, gain, cot, rows, q_full, m_full, o_full, all_context, q_out, k_out, v_out,
+                   p_ref, r_ref, c_out, q_ref, k_ref, v_ref, c_ref, marks, meta, held, weight, gain_in, q_own, m_own, piece, send, recv, local, extra_send,
                    extra_recv, context_send, context_recv):
     step = pl.program_id(0)
     scale = HEAD_DIM ** (-0.5)
@@ -947,6 +942,7 @@
         n, in_ref, held, note_in, note, gain_in, gain, extra_send, extra_recv, local.at[pl.ds(3, 3)]
     )
     rows_keep = lambda: pltpu.make_async_copy(held, rows, local.at[7])
+    pull = Pull(n, cot_in, cot, extra_send, extra_recv, 5)
 
     def context_copy(p):
         there = c_ref.at[p, pl.ds((1 - n.c) * half, half)]
@@ -990,11 +986,23 @@
         for item in loads:
             item.wait()
 
+    flush = lambda: [
+        pltpu.make_async_copy(source, target, local.at[13 + at])
+        for at, (source, target) in enumerate(
+            ((q_ref, q_out), (k_ref, k_out), (v_ref, v_out), (c_ref, c_out))
+        )
+    ]
+
+    def flush_early():
+        for item in flush()[:3]:
+            item.start()
+
     hooks = {
-        2: [functools.partial(gathers[1].second, k) for k in range(1, depth)],
-        4: [functools.partial(gathers[2].second, k) for k in range(1, depth)],
-        6: [functools.partial(gathers[1].third, k) for k in range(depth)],
-        10: [gathers[1].fourth],
+        4: [flush_early],
+        1: [functools.partial(gathers[1].second, k) for k in range(1, depth)],
+        3: [functools.partial(gathers[2].second, k) for k in range(1, depth)],
+        7: [functools.partial(gathers[1].third, k) for k in range(depth)] + [pull.begin],
+        11: [gathers[1].fourth],
     }
     for at, actions in hooks.items():
 
@@ -1041,7 +1049,7 @@
             outs.append(contract(soft, values, 1, 0))
             scales.append(inverse)
         inverse = jnp.where(lane < HEAD_DIM, scales[0], scales[1])
-        r_ref[p, here] = inverse
+        r_ref[0, here] = inverse
         c_ref[p, here] = (jnp.where(lane < HEAD_DIM, outs[0], outs[1]) * inverse).astype(LOW)
 
     for p in range(3):
@@ -1053,18 +1061,22 @@
 
     @pl.when(step == 4 * SPAN - 1)
     def _():
+        flush()[3].start()
         gathers[1].finish()
         gathers[2].halfway()
         gathers[0].close()
         gathers[1].close()
         share.finish()
+        pull.finish()
         rows_keep().wait()
         for p in range(3):
             context_copy(p).wait()
             context_keep(p).wait()
-
-
-def forward_call(depth, cuts, note, gains, rows, weights, base, jump):
+        for item in flush():
+            item.wait()
+
+
+def forward_call(depth, cuts, note, gains, rows, cot, weights, base, jump):
     length, part = rows.shape
     half = length // 2
     r, hidden = weights[-1].shape
@@ -1080,6 +1092,7 @@
         out_shape=[
             jax.ShapeDtypeStruct(note.shape, note.dtype),
             jax.ShapeDtypeStruct((2, 8, part), WIDE),
+            low(2, half, part),
             low(2, length, part),
         ]
         + full
@@ -1092,15 +1105,16 @@
             jax.ShapeDtypeStruct((3, length, 128), WIDE),
             trio,
         ],
-        in_specs=[ANY] * 2 + [once(item.shape) for item in (*gains, *weights, base, jump)],
-        out_specs=[ANY] * 7
-        + [vmem] * 3
+        in_specs=[ANY] * 3 + [once(item.shape) for item in (*gains, *weights, base, jump)],
+        out_specs=[ANY] * 8
+        + [ANY] * 3
         + [
             pl.BlockSpec((1, 2, BLOCK, length), lambda s: (jnp.maximum(s - SPAN, 0), 0, 0, 0)),
-            vmem,
-            vmem,
+            pl.BlockSpec((1, length, 128), lambda s: (jnp.maximum(s - SPAN, 0) // SPAN, 0, 0)),
+            ANY,
         ],
-        scratch_shapes=[
+        scratch_shapes=[pltpu.VMEM((3, length, 128), LOW)] * 4
+        + [
             pltpu.VMEM((length, 128), LOW),
             pltpu.SMEM(note.shape, note.dtype),
             pltpu.VMEM((2, length, part), LOW),
@@ -1111,7 +1125,7 @@
             pltpu.SemaphoreType.DMA((4 * depth,)),
             marks,
             marks,
-            pltpu.SemaphoreType.DMA((13,)),
+            pltpu.SemaphoreType.DMA((17,)),
             pltpu.SemaphoreType.DMA((8,)),
             pltpu.SemaphoreType.DMA((8,)),
             pltpu.SemaphoreType.DMA((3,)),
@@ -1121,7 +1135,7 @@
             collective_id=0, has_side_effects=True, vmem_limit_bytes=60 * MEGA
         ),
         name="attend",
-    )(note, rows, *gains, *weights, base, jump)
+    )(note, rows, cot, *gains, *weights, base, jump)
 
 
 def norm_of(summed):
@@ -1141,9 +1155,9 @@
 HIDDEN = 512
 
 
-def middle_kernel(depth, cuts, context, rows, gains, cot_in, m_full, o_full, lo_out, gfs_ref, sums, grads,
+def middle_kernel(depth, cuts, context, rows, gains, cot_in, cot_got, m_full, o_full, lo_out, gfs_ref, sums, grads,
                   o_held, m_held, m_mat, o_mat, act, gi, fl, gm, ga, gc, n1, n2, scales, cot, lo,
-                  o_part, m_part, o_other, m_other, ox, oy, mx, my, local, send, recv, load):
+                  o_part, m_part, o_other, m_other, ox, oy, ox2, oy2, local, send, recv, load):
     step = pl.program_id(0)
     tile, part = rows.shape[1:]
     half = fl.shape[0]
@@ -1152,9 +1166,15 @@
     pieces = o_mat.shape[2] // HIDDEN
     width = pieces * HIDDEN
     n = Links(depth)
-    here = pl.ds(lax.rem(step, tiles) * tile, tile)
-    pull = Pull(n, cot_in, cot, send, recv, 5, local.at[7])
-    lo_over = HandOver(n, lo, lo_out, send, recv, 8, local.at[8])
+    early = step < 2 * tiles
+    turn_of = jnp.where(early, lax.rem(step, tiles), jnp.clip(step - 2 * tiles - 2, 0, tiles - 1))
+    here = pl.ds(pl.multiple_of(turn_of * tile, tile), tile)
+    cot_raw = lambda: pltpu.make_async_copy(
+        cot_in.at[pl.ds(n.c * half, half)], cot.at[n.x], local.at[7]
+    )
+    cot_near = lambda: pltpu.make_async_copy(cot_got.at[n.x], cot.at[n.x], local.at[7])
+    cot_far = lambda: pltpu.make_async_copy(cot_got.at[1 - n.x], cot.at[1 - n.x], local.at[5])
+    lo_copy = lambda: pltpu.make_async_copy(lo, lo_out, local.at[8])
     finish = Finish(n, o_full, o_mat, cuts[0], send, recv, 15, load)
     m_load = lambda: pltpu.make_async_copy(m_full, m_mat, local.at[0])
 
@@ -1166,8 +1186,8 @@
         own = grads.at[:, pl.ds(n.c * half, half)]
         return remote(gc.at[1 - n.c], own, send.at[4], recv.at[4], n.sibling)
 
-    order = ((0, 1 - n.x), (1, 1 - n.x), (0, n.x), (1, n.x))
-    chunks = ((o_part, o_other, ox, oy, o_held), (m_part, m_other, mx, my, m_held))
+    order = ((0, 1 - n.x), (0, n.x), (1, 1 - n.x), (1, n.x))
+    chunks = ((o_part, o_other, ox, oy, o_held), (m_part, m_other, None, None, m_held))
 
     def part_copy(k):
         chunk, h = order[k]
@@ -1203,15 +1223,39 @@
             target[n.x, q, 1 - n.y, :, low] = plus(target[n.x, q, 1 - n.y, :, low], x1[q])
             target[1 - n.x, q, n.y, :, high] = plus(target[1 - n.x, q, n.y, :, high], y1[q])
 
+    def hop2(across):
+        mark = 13 + across
+        if across:
+            part = o_other.at[1 - n.x, :, n.y]
+            return remote(part, ox2, send.at[mark], recv.at[mark], n.across)
+        part = o_other.at[n.x, :, 1 - n.y]
+        return remote(part, oy2, send.at[mark], recv.at[mark], n.beside)
+
+    def land2():
+        hop2(True).wait_recv()
+        hop2(False).wait_recv()
+        for q in range(depth):
+            ox2[q] = plus(plus(o_other[n.x, q, n.y], ox2[q]), oy2[q])
+
     def held_copy(chunk):
-        return pltpu.make_async_copy(chunks[chunk][1], chunks[chunk][4], local.at[3 + chunk])
+        source, target = ((ox2, o_held), (m_other, m_held))[chunk]
+        return pltpu.make_async_copy(source, target, local.at[3 + chunk])
 
     @pl.when(step == 0)
     def _():
         m_load().start()
         n.meet()
         finish.begin()
-        pull.begin()
+        cot_far().start()
+
+        @pl.when(n.x == n.c)
+        def _():
+            cot_raw().start()
+
+        @pl.when(n.x != n.c)
+        def _():
+            cot_near().start()
+
         m_load().wait()
 
     @pl.when(step < tiles)
@@ -1241,6 +1285,8 @@
     @pl.when(step == tiles)
     def _():
         finish.fourth()
+        cot_far().wait()
+        cot_near().wait()
         finish.finish()
 
     @pl.when((step >= tiles) & (step < 2 * tiles))
@@ -1251,35 +1297,38 @@
         for h in range(2):
             mixed = mixed + contract(act[here, h * width : (h + 1) * width], o_mat[h], 1, 1)
         normed2, scale2 = norm_of(mixed)
-        n2[here] = normed2
-        scales[here, 1:2] = scale2
         result = (normed2 * gain2 + bias2).astype(LOW)
         for h in range(2):
             lo[h, here] = result[:, h * part : (h + 1) * part]
-
-    @pl.when(step == 2 * tiles)
-    def _():
-        pull.finish()
-        lo_over.begin()
-
-    @pl.when((step >= 2 * tiles) & (step < 3 * tiles))
-    def _():
-        whole = jnp.concatenate([gains[0], gains[1]], axis=1)
-        gain1, bias1, gain2, bias2 = (whole[k : k + 1, :] for k in range(4))
-        normed1, scale1 = n1[here], scales[here, 0:1]
-        normed2, scale2 = n2[here], scales[here, 1:2]
         cotangent = jnp.concatenate([cot[0, here], cot[1, here]], axis=1).astype(WIDE)
         second_gain = jnp.sum(cotangent * normed2, axis=0, keepdims=True)
         second_bias = jnp.sum(cotangent, axis=0, keepdims=True)
         grad_second = norm_back(cotangent * gain2, normed2, scale2)
         grad_mixed = grad_second.astype(LOW)
         gm[here] = grad_mixed
+        n2[here] = grad_second
+        found = jnp.concatenate([second_gain, second_bias], axis=0)
+
+        @pl.when(step == tiles)
+        def _():
+            sums[2:4] = found
+
+        @pl.when(step > tiles)
+        def _():
+            sums[2:4] += found
+
+    @pl.when((step >= 2 * tiles + 2) & (step < 3 * tiles + 2))
+    def _():
+        whole = jnp.concatenate([gains[0], gains[1]], axis=1)
+        gain1 = whole[0:1, :]
+        normed1, scale1 = n1[here], scales[here, 0:1]
+        grad_mixed = gm[here]
         for h in range(2):
             for j in range(pieces):
                 there = slice(h * width + j * HIDDEN, h * width + (j + 1) * HIDDEN)
                 raised = contract(grad_mixed, o_mat[h, :, j * HIDDEN : (j + 1) * HIDDEN], 1, 0)
                 gi[here, there] = (raised * gi[here, there].astype(WIDE)).astype(LOW)
-        grad_first = grad_second
+        grad_first = n2[here]
         for h in range(2):
             grad_first = grad_first + contract(
                 gi[here, h * width : (h + 1) * width], m_mat[h, :, part : part + width], 1, 1
@@ -1294,17 +1343,25 @@
             made = contract(grad_attended, m_mat[h, :, 0:part], 1, 0).astype(LOW)
             for p in range(3):
                 gc[h, p, here] = made[:, p * 128 : (p + 1) * 128]
-        found = jnp.concatenate([first_gain, first_bias, second_gain, second_bias], axis=0)
-
-        @pl.when(step == 2 * tiles)
-        def _():
-            sums[...] = found
-
-        @pl.when(step > 2 * tiles)
-        def _():
-            sums[...] += found
-
-    @pl.when(step == 3 * tiles - 1)
+        found = jnp.concatenate([first_gain, first_bias], axis=0)
+
+        @pl.when(step == 2 * tiles + 2)
+        def _():
+            sums[0:2] = found
+
+        @pl.when(step > 2 * tiles + 2)
+        def _():
+            sums[0:2] += found
+
+    @pl.when(step == 2 * tiles + 3)
+    def _():
+        join(1)
+        land(0)
+        hop2(True).start()
+        hop2(False).start()
+        lo_copy().start()
+
+    @pl.when(step == 3 * tiles + 1)
     def _():
         grads_keep().start()
         grads_copy().start()
@@ -1319,7 +1376,7 @@
 
     for k in range(4):
 
-        @pl.when(step == 3 * tiles + k)
+        @pl.when(step == (2 * tiles + k if k < 2 else 3 * tiles + k))
         def _():
             chunk, h = order[k]
             target = chunks[chunk][0]
@@ -1338,26 +1395,27 @@
                     made = contract(ga[:, row : row + part], seen, 0, 0)
                     put(target, h, row, 0, made.astype(LOW))
             part_copy(k).start()
-            if k:
-                join(k - 1)
-            if k in (1, 2):
-                hop(k - 1, True).start()
-                hop(k - 1, False).start()
+            if k == 1:
+                join(0)
+                hop(0, True).start()
+                hop(0, False).start()
             if k == 3:
-                land(0)
+                join(2)
+                join(3)
+                held_copy(1).start()
+                land2()
                 held_copy(0).start()
-                join(3)
-                land(1)
-                held_copy(1).start()
                 grads_keep().wait()
                 grads_copy().wait()
                 for item in range(4):
                     part_copy(item).wait_send()
-                for item in range(2):
-                    hop(item, True).wait_send()
-                    hop(item, False).wait_send()
-                    held_copy(item).wait()
-                lo_over.finish()
+                hop(0, True).wait_send()
+                hop(0, False).wait_send()
+                hop2(True).wait_send()
+                hop2(False).wait_send()
+                held_copy(0).wait()
+                held_copy(1).wait()
+                lo_copy().wait()
                 finish.close()
 
 
@@ -1366,9 +1424,9 @@
     return pl.BlockSpec(shape, lambda *_: zeros, pipeline_mode=pl.Buffered(1))
 
 
-def middle_call(depth, cuts, context, rows, cot, m_full, o_full, gains):
+def middle_call(depth, cuts, context, rows, cot_in, cot, m_full, o_full, gains):
     tile = 256
-    half, part = cot.shape[0] // 2, cot.shape[1]
+    half, part = cot.shape[1:]
     tiles = half // tile
     width = 2 * part
     hidden = 2 * o_full.shape[-1]
@@ -1377,22 +1435,23 @@
     low = lambda *shape: jax.ShapeDtypeStruct(shape, LOW)
     held = [(2, depth, 2, r, item) for item in columns]
     last = lambda i: jnp.minimum(i, tiles - 1)
-    later = lambda i: jnp.clip(i - 2 * tiles, 0, tiles - 1)
+    later = lambda i: jnp.clip(i - 2 * tiles - 2, 0, tiles - 1)
     c = lambda: lax.rem(lax.axis_index("wide"), 2)
     return pl.pallas_call(
         functools.partial(middle_kernel, depth, cuts),
         grid=(3 * tiles + 4,),
         out_shape=[
-            low(2 * half, part),
+            low(2, half, part),
             jax.ShapeDtypeStruct((half, width), WIDE),
             jax.ShapeDtypeStruct((4, width), WIDE),
             low(3, 2 * half, 128),
         ]
-        + [low(*item) for item in held],
+        + [low(depth, r, columns[0]), low(*held[1])],
         in_specs=[
             once((2, 3, half, 128)),
             pl.BlockSpec((2, tile, part), lambda i: (0, c() * tiles + last(i), 0)),
             once(gains.shape),
+            ANY,
             ANY,
             ANY,
             ANY,
@@ -1424,8 +1483,7 @@
         + [pltpu.VMEM(item, LOW) for item in held]
         + [
             pltpu.VMEM((depth, r, item), LOW)
-            for whole, cut in zip(columns, cuts)
-            for item in (cut, whole - cut)
+            for item in (cuts[0], columns[0] - cuts[0], columns[0], columns[0])
         ]
         + [
             pltpu.SemaphoreType.DMA((9,)),
@@ -1437,15 +1495,16 @@
             collective_id=1, has_side_effects=True, vmem_limit_bytes=62 * MEGA
         ),
         name="middle",
-    )(context, rows, gains, cot, m_full, o_full)
+    )(context, rows, gains, cot_in, cot, m_full, o_full)
 
 
 def backward_kernel(depth, cuts, meta, base, jump, soft, grads, context, inverse, q_ref, k_ref, v_ref,
-                    rows, kept, q_full, o_in, m_in, t_in, dx_out, o_out, m_out,
+                    rows_in, kept_in, q_full, lo_in, o_in, m_in, t_in, lo_out, dx_out, o_out, m_out,
                     i_out, q_out, k_out, v_out, t_out, *scratch):
     ones, keys_sum, values_sum, made, weight, q_part, dx_own, dx_give, dx_other = scratch[:9]
+    rows, kept, bounce = scratch[-3:]
     bufs = [scratch[9 + 7 * k : 16 + 7 * k] for k in range(6)]
-    piece, send, recv, local, extra_send, extra_recv = scratch[51:]
+    piece, send, recv, local, extra_send, extra_recv = scratch[51:-3]
     step = pl.program_id(0)
     p = step // SPAN
     i = step % SPAN
@@ -1457,7 +1516,7 @@
     r = o_in.shape[-2]
     half, width = kept.shape
     part = width // 2
-    kinds = ("later", "later", "swap", "swap", "swap", "join")
+    kinds = ("last", "held", "swap", "swap", "swap", "join")
     parts = (o_in, m_in) + tuple(q_part.at[k] for k in range(3)) + (t_in,)
 
     def put_pair(p, total):
@@ -1480,6 +1539,10 @@
     ]
     outer, inner, pair0, pair1, pair2, small = every
     dx_over = HandOver(n, dx_own, dx_out, extra_send, extra_recv, 0, local.at[6])
+    rows_load = lambda: pltpu.make_async_copy(rows_in, rows, local.at[7])
+    kept_load = lambda: pltpu.make_async_copy(kept_in, kept, local.at[8])
+    lo_load = lambda: pltpu.make_async_copy(lo_in.at[n.x], bounce, local.at[9])
+    lo_over = HandOver(n, lo_in, lo_out, extra_send, extra_recv, 4, local.at[10], bounce)
     dx_swap = lambda: remote(dx_give, dx_other, extra_send.at[3], extra_recv.at[3], n.sibling)
 
     @pl.when(step == 0)
@@ -1487,22 +1550,25 @@
         ones[...] = (lanes(length) < 2).astype(WIDE).astype(LOW)
         for item in weight_loads(q_full, n.c, weight, piece):
             item.start()
+        inner.begin()
+        outer.begin()
+        rows_load().start()
+        kept_load().start()
+        lo_load().start()
         n.meet()
         small.begin()
         small.first()
-        outer.begin()
-        inner.begin()
+        inner.first()
+        outer.third()
         for item in weight_loads(q_full, n.c, weight, piece):
             item.wait()
 
-    hooks = {
-        1: [small.second],
-        3: [outer.third, pair0.first],
-        5: [inner.third, small.third],
-        6: [outer.fourth, pair0.second, pair1.first],
-        7: [pair0.third, pair1.second],
-        8: [pair1.third, inner.fourth, small.fourth],
-    }
+
+    def lo_begin():
+        lo_load().wait()
+        lo_over.begin()
+
+    hooks = {1: [small.second], 2: [lambda: rows_load().wait(), lo_begin], 3: [inner.second], 4: [outer.fourth, pair0.first], 6: [small.third, pair1.first], 8: [inner.third, pair0.second, pair0.third, pair1.second]}
     for at, actions in hooks.items():
 
         @pl.when(step == at)
@@ -1510,13 +1576,13 @@
             for action in actions:
                 action()
 
-    grad = grads[p, here].astype(WIDE)
-    turned = grad * inverse[p, here]
-    both = turned * context[p, here].astype(WIDE)
+    grad = grads[0, here].astype(WIDE)
+    turned = grad * inverse[0, here]
+    both = turned * context[0, here].astype(WIDE)
     turned_low = turned.astype(LOW)
-    queries = q_ref[p, here]
-    keys = k_ref[p]
-    values = jnp.concatenate([v_ref[p], ones[...]], axis=1)
+    queries = q_ref[0, here]
+    keys = k_ref[0]
+    values = jnp.concatenate([v_ref[0], ones[...]], axis=1)
     turned_flip = jnp.transpose(turned).astype(LOW)
     queries_flip = jnp.transpose(queries.astype(WIDE)).astype(LOW)
     found = []
@@ -1572,6 +1638,7 @@
 
     @pl.when(step == 3 * SPAN - 1)
     def _():
+        kept_load().wait()
         for own in (False, True):
             there = pl.ds((n.c if own else 1 - n.c) * half, half)
             gained = kept[...] if own else jnp.zeros(kept.shape, WIDE)
@@ -1591,23 +1658,27 @@
         for h in range(2):
             dx_own[h] = plus(dx_own[h], dx_other[h])
         dx_over.begin()
+        pair1.third()
         pair2.third()
+        small.fourth()
+        inner.fourth()
         pair0.fourth()
         pair1.fourth()
         pair2.fourth()
         for item in every:
             item.close()
         dx_swap().wait_send()
+        lo_over.finish()
         dx_over.finish()
 
 
 def backward_call(depth, cuts, meta, base, jump, soft, grads, context, inverse, q, k, v, rows, kept,
-                  q_full, o_held, m_held, t_part):
+                  q_full, lo, o_held, m_held, t_part):
     length = q.shape[1]
     half, width = kept.shape
     part = width // 2
     r = o_held.shape[-2]
-    trio = once((3, length, 128))
+    trio = pl.BlockSpec((1, length, 128), lambda s: (s // SPAN, 0, 0))
     low = lambda *shape: jax.ShapeDtypeStruct(shape, LOW)
     widths = (o_held.shape[-1], m_held.shape[-1])
     shape = lambda *item: jax.ShapeDtypeStruct(item, WIDE)
@@ -1625,13 +1696,13 @@
         pltpu.VMEM((2, half, part), LOW),
     ]
     for at, columns in enumerate(widths + (384,) * 3):
-        scratch += scatter_scratch(depth, r, columns, cuts[at], "later" if at < 2 else "swap")
+        scratch += scatter_scratch(depth, r, columns, cuts[at], ("last", "held", "swap")[min(at, 2)])
     scratch += scatter_scratch(depth, t_part.shape[-2], t_part.shape[-1], cuts[5], "join", WIDE)
     marks = pltpu.SemaphoreType.DMA((6, scatter_marks(depth)))
     return pl.pallas_call(
         functools.partial(backward_kernel, depth, cuts),
         grid=(3 * SPAN,),
-        out_shape=[low(2 * half, part)] + outs,
+        out_shape=[low(2 * half, part)] * 2 + outs,
         in_specs=[
             pl.BlockSpec(memory_space=pltpu.SMEM),
             once(base.shape),
@@ -1643,25 +1714,26 @@
             trio,
             trio,
             trio,
-            once(rows.shape),
-            once(kept.shape),
         ]
-        + [ANY] * 4,
-        out_specs=[ANY] + [once(item.shape) for item in outs],
+        + [ANY] * 7,
+        out_specs=[ANY] * 2 + [once(item.shape) for item in outs],
         scratch_shapes=scratch
         + [
             pltpu.SemaphoreType.DMA((4 * depth,)),
             marks,
             marks,
-            pltpu.SemaphoreType.DMA((8,)),
+            pltpu.SemaphoreType.DMA((11,)),
             pltpu.SemaphoreType.DMA((7,)),
             pltpu.SemaphoreType.DMA((7,)),
+            pltpu.VMEM(rows.shape, LOW),
+            pltpu.VMEM(kept.shape, WIDE),
+            pltpu.VMEM((half, part), LOW),
         ],
         compiler_params=pltpu.CompilerParams(
             collective_id=2, has_side_effects=True, vmem_limit_bytes=63 * MEGA
         ),
         name="attend_back",
-    )(meta, base, jump, soft, grads, context, inverse, q, k, v, rows, kept, q_full, o_held, m_held, t_part)
+    )(meta, base, jump, soft, grads, context, inverse, q, k, v, rows, kept, q_full, lo, o_held, m_held, t_part)
 
 
 def owned(
@@ -1690,20 +1762,22 @@
     meta = jnp.pad(block_segment[None], ((0, 0), (0, 128 - SPAN)))
     hidden = inner_weight.shape[1]
     widths = [3 * part, part + hidden, hidden]
-    cuts = [(item // 256) * 128 for item in widths]
+    cuts = [(item // 384) * 128 for item in widths]
     cuts[0] = 128
     gains = [first_gain, first_bias, second_gain, second_bias]
     weights = [query_weight, key_weight, value_weight, output_weight.T, inner_weight, outer_weight.T]
     base, jump = angle_tables()
-    meta, gains, rows, q_full, m_full, o_full, pairs_context, q, k, v, soft, inverse, context = (
-        forward_call(depth, cuts, meta, gains, inputs, weights, base, jump)
-    )
-    layer_output, kept, sums, grads, o_held, m_held = middle_call(
+    found = forward_call(
+        depth, cuts, meta, gains, inputs, output_cotangent, weights, base, jump
+    )
+    meta, gains, cot, rows, q_full, m_full, o_full, pairs_context, q, k, v, soft, inverse, context = found
+    lo, kept, sums, grads, o_held, m_held = middle_call(
         depth,
         [cuts[2], cuts[1]],
         pairs_context,
         rows,
         output_cotangent,
+        cot,
         m_full.reshape(2, 2 * part, widths[1]),
         o_full,
         gains,
@@ -1712,9 +1786,9 @@
     spots = jnp.moveaxis(sums.reshape(2, 2, 2, wide, few), (2, 3), (0, 1))
     spots = jnp.pad(jnp.moveaxis(spots, 2, 3), ((0, 0), (0, 0), (0, 6), (0, 0), (0, 128 - few)))
     spots = spots.reshape(2, depth, 2, 2, 8, 256)
-    input_gradient, o_sum, m_sum, i_sum, q_sum, k_sum, v_sum, found = backward_call(
+    layer_output, input_gradient, o_sum, m_sum, i_sum, q_sum, k_sum, v_sum, found = backward_call(
         depth,
-        [(item // 256) * 128 for item in (widths[2], widths[1])] + [128] * 4,
+        [(item // 512) * 128 for item in (widths[2], widths[1])] + [128] * 4,
         meta,
         base,
         jump,
@@ -1728,6 +1802,7 @@
         rows,
         kept,
         q_full,
+        lo,
         o_held,
         m_held,
         spots,

time: 259 us -> 240 us (0.927)
  Pallas kernels: 246 us -> 227 us
    pallas_call x1, Pallas kernels: 93.1 us -> 83.7 us  [backward_call(): pl.pallas_call(functools.partial(backward_kernel, depth, cuts), grid=(3 *...]
    pallas_call x1, Pallas kernels: 65.7 us -> 59.1 us  [middle_call(): pl.pallas_call(functools.partial(middle_kernel, depth, cuts), grid=(3 * t...]
    pallas_call x1, Pallas kernels: 87.3 us -> 84.6 us  [forward_call(): pl.pallas_call(functools.partial(forward_kernel, depth, cuts), grid=(SPAN...]
where the time goes in v5:
time: 240 us
  Pallas kernels  227 us (95%)
  local copies, waits for them, and re-layouts  11.5 us (5%)
    pallas_call x1, Pallas kernels, forward_call(): pl.pallas_call(functools.partial(forward_kernel, depth, cuts), grid=(SPAN...  84.6 us
    pallas_call x1, Pallas kernels, backward_call(): pl.pallas_call(functools.partial(backward_kernel, depth, cuts), grid=(3 *...  83.7 us
    pallas_call x1, Pallas kernels, middle_call(): pl.pallas_call(functools.partial(middle_kernel, depth, cuts), grid=(3 * t...  59.1 us
    unnamed x22, local copies, waits for them, and re-layouts  7.5 us

profile of v5, /device:TPU:1, one launch (start us, length us, event | category | flops | bytes accessed | tf_op | source)
XLA Modules:
  0.0 239.6 jit_solution(6848958099136287160)
XLA Ops:
  0.6 1.2 pad.8.note_in
  1.8 84.6 %attend.1 = (s32[1,128]{1,0:T(1,128)}, f32[2,8,384]{2,1,0:T(8,128)}, bf16[2,768,384]{2,1,0:T(8,128)(2,1)}, bf16[2,1536,384]{2,1,0:T(8,128)(2,1)}, bf16[2,4,2,2,4...) custom-call(s32[1,128]{1,0:T(1,128)} %pad.8.note_in, ...), custom_call_target="tpu_custom_call" | custom-call | tf_op jit(solution)/shard_map/attend/pallas_call | solution.py:1089
  86.5 59.1 %middle.1 = (bf16[2,768,384]{2,1,0:T(8,128)(2,1)}, f32[768,768]{1,0:T(8,128)}, f32[4,768]{1,0:T(4,128)}, bf16[3,1536,128]{2,1,0:T(8,128)(2,1)}, bf16[4,48,1536]{...) custom-call(bf16[2,3,768,128]{3,2,1,0:T(8,128)(2,1)} %get-tuple-element.43.context, ...), custom_call_target="tpu_custom_call" | custom-call | tf_op jit(solution)/shard_map/middle/pallas_call | solution.py:1440
  145.5 0.8 reshape.34
  146.3 0.1 copy.29
  146.4 0.7 pad.9
  147.1 83.7 %attend_back.1 = (bf16[1536,384]{1,0:T(8,128)(2,1)}, bf16[1536,384]{1,0:T(8,128)(2,1)}, f32[48,1536]{1,0:T(8,128)}, f32[48,384]{1,0:T(8,128)}, f32[48,1536]{1,0:...) custom-call(s32[1,128]{1,0:T(1,128)} %get-tuple-element.41.meta, ...), custom_call_target="tpu_custom_call" | custom-call | tf_op jit(solution)/shard_map/attend_back/pallas_call | solution.py:1702
  230.8 1.3 slice_bitcast_fusion
  232.1 0.0 copy-start
  232.1 2.5 %copy.38 = bf16[1536,384]{1,0:T(8,128)(2,1)} copy(bf16[1536,384]{1,0:T(8,128)(2,1)} %get-tuple-element.86) | data formatting | bytes 2359296
  234.6 0.0 copy-done
  234.6 0.0 copy-start.6
  234.6 0.0 copy-start.5
  234.6 0.0 copy-start.4
  234.6 0.0 copy-start.3
  234.6 0.0 copy-start.2
  234.6 1.0 copy.39
  235.7 0.0 copy-done.6
  235.7 0.0 copy-start.1
  235.7 0.6 copy.40
  236.3 0.0 copy-done.5
  236.3 0.6 copy.41
  236.9 0.0 copy-done.4
  236.9 0.6 copy.42
  237.6 0.0 copy-done.3
  237.6 0.6 copy.43
  238.2 0.0 copy-done.2
  238.2 0.7 copy.44
  238.9 0.0 copy-done.1
  238.9 0.7 copy.45
Async XLA Ops:
  232.1 2.5 %copy-start = (bf16[1536,384]{1,0:T(8,128)(2,1)S(1)}, bf16[1536,384]{1,0:T(8,128)(2,1)}, u32[]{:S(2)}) copy-start(bf16[1536,384]{1,0:T(8,128)(2,1)} %get-tuple-element.87) | copy-start | bytes 3538948
  234.6 1.0 copy-start.6
  234.6 1.7 copy-start.5
  234.6 2.3 copy-start.4
  234.6 2.9 %copy-start.3 = (f32[48,384]{1,0:T(8,128)S(1)}, f32[48,384]{1,0:T(8,128)}, u32[]{:S(2)}) copy-start(f32[48,384]{1,0:T(8,128)} %get-tuple-element.66) | copy-start | bytes 221188
  234.6 3.6 %copy-start.2 = (f32[48,1536]{1,0:T(8,128)S(1)}, f32[48,1536]{1,0:T(8,128)}, u32[]{:S(2)}) copy-start(f32[48,1536]{1,0:T(8,128)} %get-tuple-element.92) | copy-start | bytes 884740
  235.7 3.3 %copy-start.1 = (f32[48,1536]{1,0:T(8,128)S(1)}, f32[48,1536]{1,0:T(8,128)}, u32[]{:S(2)}) copy-start(f32[48,1536]{1,0:T(8,128)} %get-tuple-element.68) | copy-start | bytes 884740

commit v6 on v5

--- a/solution.py
+++ b/solution.py
@@ -1788,7 +1788,7 @@
     spots = spots.reshape(2, depth, 2, 2, 8, 256)
     layer_output, input_gradient, o_sum, m_sum, i_sum, q_sum, k_sum, v_sum, found = backward_call(
         depth,
-        [(item // 512) * 128 for item in (widths[2], widths[1])] + [128] * 4,
+        [(item // 384) * 128 for item in (widths[2], widths[1])] + [128] * 4,
         meta,
         base,
         jump,

time: 240 us -> 240 us (level)
  no operation moved by 1% of the time
where the time goes in v6:
time: 240 us
  Pallas kernels  227 us (95%)
  local copies, waits for them, and re-layouts  11.5 us (5%)
    pallas_call x1, Pallas kernels, forward_call(): pl.pallas_call(functools.partial(forward_kernel, depth, cuts), grid=(SPAN...  84.6 us
    pallas_call x1, Pallas kernels, backward_call(): pl.pallas_call(functools.partial(backward_kernel, depth, cuts), grid=(3 *...  83.7 us
    pallas_call x1, Pallas kernels, middle_call(): pl.pallas_call(functools.partial(middle_kernel, depth, cuts), grid=(3 * t...  59.1 us
    unnamed x22, local copies, waits for them, and re-layouts  7.5 us

profile of v6, /device:TPU:1, one launch (start us, length us, event | category | flops | bytes accessed | tf_op | source)
XLA Modules:
  0.0 239.6 jit_solution(8612628710444490680)
XLA Ops:
  0.6 1.2 pad.8.note_in
  1.8 84.6 %attend.1 = (s32[1,128]{1,0:T(1,128)}, f32[2,8,384]{2,1,0:T(8,128)}, bf16[2,768,384]{2,1,0:T(8,128)(2,1)}, bf16[2,1536,384]{2,1,0:T(8,128)(2,1)}, bf16[2,4,2,2,4...) custom-call(s32[1,128]{1,0:T(1,128)} %pad.8.note_in, ...), custom_call_target="tpu_custom_call" | custom-call | tf_op jit(solution)/shard_map/attend/pallas_call | solution.py:1089
  86.5 59.1 %middle.1 = (bf16[2,768,384]{2,1,0:T(8,128)(2,1)}, f32[768,768]{1,0:T(8,128)}, f32[4,768]{1,0:T(4,128)}, bf16[3,1536,128]{2,1,0:T(8,128)(2,1)}, bf16[4,48,1536]{...) custom-call(bf16[2,3,768,128]{3,2,1,0:T(8,128)(2,1)} %get-tuple-element.43.context, ...), custom_call_target="tpu_custom_call" | custom-call | tf_op jit(solution)/shard_map/middle/pallas_call | solution.py:1440
  145.5 0.8 reshape.34
  146.3 0.1 copy.29
  146.4 0.7 pad.9
  147.1 83.7 %attend_back.1 = (bf16[1536,384]{1,0:T(8,128)(2,1)}, bf16[1536,384]{1,0:T(8,128)(2,1)}, f32[48,1536]{1,0:T(8,128)}, f32[48,384]{1,0:T(8,128)}, f32[48,1536]{1,0:...) custom-call(s32[1,128]{1,0:T(1,128)} %get-tuple-element.41.meta, ...), custom_call_target="tpu_custom_call" | custom-call | tf_op jit(solution)/shard_map/attend_back/pallas_call | solution.py:1702
  230.8 1.3 slice_bitcast_fusion
  232.1 0.0 copy-start
  232.1 2.5 %copy.38 = bf16[1536,384]{1,0:T(8,128)(2,1)} copy(bf16[1536,384]{1,0:T(8,128)(2,1)} %get-tuple-element.86) | data formatting | bytes 2359296
  234.6 0.0 copy-done
  234.6 0.0 copy-start.6
  234.6 0.0 copy-start.5
  234.6 0.0 copy-start.4
  234.6 0.0 copy-start.3
  234.6 0.0 copy-start.2
  234.6 1.0 copy.39
  235.7 0.0 copy-done.6
  235.7 0.0 copy-start.1
  235.7 0.6 copy.40
  236.3 0.0 copy-done.5
  236.3 0.6 copy.41
  236.9 0.0 copy-done.4
  236.9 0.6 copy.42
  237.6 0.0 copy-done.3
  237.6 0.6 copy.43
  238.2 0.0 copy-done.2
  238.2 0.7 copy.44
  238.9 0.0 copy-done.1
  238.9 0.7 copy.45
Async XLA Ops:
  232.1 2.5 %copy-start = (bf16[1536,384]{1,0:T(8,128)(2,1)S(1)}, bf16[1536,384]{1,0:T(8,128)(2,1)}, u32[]{:S(2)}) copy-start(bf16[1536,384]{1,0:T(8,128)(2,1)} %get-tuple-element.87) | copy-start | bytes 3538948
  234.6 1.0 copy-start.6
  234.6 1.7 copy-start.5
  234.6 2.3 copy-start.4
  234.6 2.9 %copy-start.3 = (f32[48,384]{1,0:T(8,128)S(1)}, f32[48,384]{1,0:T(8,128)}, u32[]{:S(2)}) copy-start(f32[48,384]{1,0:T(8,128)} %get-tuple-element.66) | copy-start | bytes 221188
  234.6 3.6 %copy-start.2 = (f32[48,1536]{1,0:T(8,128)S(1)}, f32[48,1536]{1,0:T(8,128)}, u32[]{:S(2)}) copy-start(f32[48,1536]{1,0:T(8,128)} %get-tuple-element.92) | copy-start | bytes 884740
  235.7 3.3 %copy-start.1 = (f32[48,1536]{1,0:T(8,128)S(1)}, f32[48,1536]{1,0:T(8,128)}, u32[]{:S(2)}) copy-start(f32[48,1536]{1,0:T(8,128)} %get-tuple-element.68) | copy-start | bytes 884740
